TPU v7x, 32 devices: a whole 2x2x4 slice. The times are simulated.
32 devices in a mesh: grp: 2 (over x), ctx: 8 (over z, y), head: 2 (over core).
Axes of the slice: x: 2, y: 2, z: 4, core: 2. Of those that a mesh axis runs over, the one named last changes fastest.
Arguments:
- queries: bfloat16 [3072, 16, 128], P(('grp', 'ctx'), 'head'), parts along dimension 0
- key_vecs: bfloat16 [3072, 16, 128], P(('grp', 'ctx'), 'head'), parts along dimension 0
- value_vecs: bfloat16 [3072, 16, 128], P(('grp', 'ctx'), 'head'), parts along dimension 0, may hold values from -6 to 6
- out_grad: bfloat16 [3072, 16, 128], P(('grp', 'ctx'), 'head'), parts along dimension 0, may hold values from -6 to 6
- doc_ids: int32 [3072], P('grp'), parts along dimension 0, may hold values from 0 to 5, never falling along the last dimension, each value on 1 to 960 neighbouring positions
Outputs:
- attn_out: bfloat16 [3072, 16, 128], P(('grp', 'ctx'), 'head'), parts along dimension 0
- query_grad: bfloat16 [3072, 16, 128], P(('grp', 'ctx'), 'head'), parts along dimension 0
- key_grad: bfloat16 [3072, 16, 128], P(('grp', 'ctx'), 'head'), parts along dimension 0
- value_grad: bfloat16 [3072, 16, 128], P(('grp', 'ctx'), 'head'), parts along dimension 0
There are 2 independent parts, one for each index of `grp`. A program takes and returns all parts, laid end to end along the dimension named above; each array names one. Nothing has to cross between parts.
Inputs may be any that keep to these rules, and one draw needn't show every extreme that they name: doc_ids never fall along the sequence; every document has 1 to 960 tokens and one has exactly 960.
All inputs are finite; a program needn't handle non-finite values.
Results may differ from a plain program's by a relative error of at most 0.035.
Values may be sent and summed in bfloat16 or wider, within the bound.
No kernel may reach another device: no remote copies, remote signals or barrier semaphores. Data moves between devices by JAX's collectives and lax.ppermute only.
A program may use at most 128 MiB of HBM per device.

v0:
```python
import jax
import jax.numpy as jnp
from jax import lax
from jax.sharding import PartitionSpec as P


def block_length(shard_rows, shard_count):
    factor = 1
    while factor * shard_rows < 512 and shard_count % (factor * 2) == 0:
        factor = factor * 2
    return factor * shard_rows


def stored_position(rows, shard_rows, shard_count):
    half_rows = shard_rows // 2
    shard = rows // shard_rows
    within = rows % shard_rows
    return jnp.where(
        within < half_rows,
        shard * half_rows + within,
        (2 * shard_count - 1 - shard) * half_rows + within - half_rows,
    )


def score_block(query_blk, query_pos, query_doc, key_blk, key_pos, key_doc, scaling):
    scores = (
        jnp.einsum("qhd,khd->hqk", query_blk, key_blk, preferred_element_type=jnp.float32) * scaling
    )
    allowed = (key_doc[None, :] == query_doc[:, None]) & (key_pos[None, :] <= query_pos[:, None])
    return (scores, allowed[None])


def probs_of(scores, allowed, lse):
    return jnp.where(allowed, jnp.exp(scores - lse[:, :, None]), 0.0).astype(jnp.bfloat16)


def dscores_of(probs, grad_blk, value_blk, delta):
    dprobs = jnp.einsum("qhd,khd->hqk", grad_blk, value_blk, preferred_element_type=jnp.float32)
    return (probs.astype(jnp.float32) * (dprobs - delta[:, :, None])).astype(jnp.bfloat16)


def on_device(queries, key_vecs, value_vecs, out_grad, doc_ids):
    shard_rows = queries.shape[0]
    head_count = queries.shape[1]
    head_size = queries.shape[2]
    scaling = head_size ** (-0.5)
    shard_count = lax.axis_size("ctx")
    shard_index = lax.axis_index("ctx")
    own_start = shard_index * shard_rows

    def positions(start, length):
        return stored_position(start + jnp.arange(length, dtype=jnp.int32), shard_rows, shard_count)

    own_pos = positions(own_start, shard_rows)
    own_doc = jnp.take(doc_ids, own_pos)
    keys_all, values_all = (
        lax.all_gather(key_vecs, "ctx", axis=0, tiled=True),
        lax.all_gather(value_vecs, "ctx", axis=0, tiled=True),
    )
    block = block_length(shard_rows, shard_count)
    block_count = keys_all.shape[0] // block

    def key_slices(start, length):
        key_blk = lax.dynamic_slice_in_dim(keys_all, start, length, 0)
        value_blk = lax.dynamic_slice_in_dim(values_all, start, length, 0)
        key_pos = positions(start, length)
        key_doc = jnp.take(doc_ids, key_pos)
        return (key_blk, value_blk, key_pos, key_doc)

    def stat_step(index, carry):
        running, total = carry
        key_blk, value_blk, key_pos, key_doc = key_slices(index * block, block)
        scores, allowed = score_block(queries, own_pos, own_doc, key_blk, key_pos, key_doc, scaling)
        newmax = jnp.maximum(running, jnp.max(jnp.where(allowed, scores, -1e30), axis=-1))
        total = total * jnp.exp(running - newmax) + jnp.sum(
            jnp.where(allowed, jnp.exp(scores - newmax[:, :, None]), 0.0), axis=-1
        )
        return (newmax, total)

    start_max = jnp.full((head_count, shard_rows), -1e30, jnp.float32)
    start_sum = jnp.zeros((head_count, shard_rows), jnp.float32)
    running, total = lax.fori_loop(0, block_count, stat_step, (start_max, start_sum))
    lse = running + jnp.log(total)

    def out_step(index, accum):
        key_blk, value_blk, key_pos, key_doc = key_slices(index * block, block)
        scores, allowed = score_block(queries, own_pos, own_doc, key_blk, key_pos, key_doc, scaling)
        probs = probs_of(scores, allowed, lse)
        return accum + jnp.einsum(
            "hqk,khd->qhd", probs, value_blk, preferred_element_type=jnp.float32
        )

    zero_rows = jnp.zeros((shard_rows, head_count, head_size), jnp.float32)
    attn_out = lax.fori_loop(0, block_count, out_step, zero_rows).astype(jnp.bfloat16)
    delta_rows = jnp.sum(out_grad.astype(jnp.float32) * attn_out.astype(jnp.float32), axis=-1)
    delta = delta_rows.T

    def query_step(index, accum):
        key_blk, value_blk, key_pos, key_doc = key_slices(index * block, block)
        scores, allowed = score_block(queries, own_pos, own_doc, key_blk, key_pos, key_doc, scaling)
        probs = probs_of(scores, allowed, lse)
        dscores = dscores_of(probs, out_grad, value_blk, delta)
        return accum + jnp.einsum(
            "hqk,khd->qhd", dscores, key_blk, preferred_element_type=jnp.float32
        )

    query_grad = (scaling * lax.fori_loop(0, block_count, query_step, zero_rows)).astype(
        jnp.bfloat16
    )
    lse_all, delta_all = (
        lax.all_gather(lse.T, "ctx", axis=0, tiled=True),
        lax.all_gather(delta_rows, "ctx", axis=0, tiled=True),
    )
    query_blk = lax.all_gather(queries, "ctx", axis=0, tiled=True)
    grad_blk = lax.all_gather(out_grad, "ctx", axis=0, tiled=True)
    length = query_blk.shape[0]
    query_pos = positions(jnp.int32(0), length)
    query_doc = jnp.take(doc_ids, query_pos)
    lse_blk = lse_all.T
    delta_blk = delta_all.T
    scores, allowed = score_block(
        query_blk, query_pos, query_doc, key_vecs, own_pos, own_doc, scaling
    )
    probs = probs_of(scores, allowed, lse_blk)
    dscores = dscores_of(probs, grad_blk, value_vecs, delta_blk)
    key_accum = scaling * jnp.einsum(
        "hqk,qhd->khd", dscores, query_blk, preferred_element_type=jnp.float32
    )
    value_accum = jnp.einsum("hqk,qhd->khd", probs, grad_blk, preferred_element_type=jnp.float32)
    key_grad = key_accum.astype(jnp.bfloat16)
    value_grad = value_accum.astype(jnp.bfloat16)
    return (attn_out, query_grad, key_grad, value_grad)


def solution(mesh):
    return jax.shard_map(
        on_device,
        mesh=mesh,
        in_specs=(
            P(("grp", "ctx"), "head", None),
            P(("grp", "ctx"), "head", None),
            P(("grp", "ctx"), "head", None),
            P(("grp", "ctx"), "head", None),
            P("grp"),
        ),
        out_specs=(
            P(("grp", "ctx"), "head", None),
            P(("grp", "ctx"), "head", None),
            P(("grp", "ctx"), "head", None),
            P(("grp", "ctx"), "head", None),
        ),
        check_vma=False,
    )
```

profile of v0, /device:TPU:0, one launch (start us, length us, event | category | flops | bytes accessed | tf_op | source)
XLA Modules:
  0.0 294.1 jit_solution(10098897156930762609)
XLA Ops:
  16.3 8.4 %gather_fusion.4 = s32[1536]{0:T(1024)S(1)} fusion(s32[1536]{0:T(1024)S(1)} %copy-done, s32[2048]{0:T(1024)S(1)} %pad_clamp_fusion.3), kind=kCustom, calls=%fused_computation.4 | custom fusion | bytes 18432 | tf_op jit(solution)/shard_map/jit(_take)/gather | solution.py:118
  26.4 47.6 %all-gather.9.cloned.1.call-done = bf16[1536,8,128]{2,0,1:T(8,128)(2,1)} async-done(((bf16[192,8,128]{2,0,1:T(8,128)(2,1)}), bf16[1536,8,128]{2,0,1:T(8,128)(2,1)}) %all-gather.9.cloned.1.call-update) | async-done | bytes 3145744 | tf_op jit(solution)/shard_map/all_gather | solution.py:57
  74.0 38.8 %while.50 = (s32[]{:T(128)}, f32[8,192]{1,0:T(8,128)S(1)}, f32[8,192]{1,0:T(8,128)}, s32[1536]{0:T(1024)S(1)}, s32[192]{0:T(256)}, /*index=5*/bf16[1536,8,128]{2...) while((s32[]{:T(128)}, f32[8,192]{1,0:T(8,128)S(1)}, ...), condition=%wide.region_3.5_spmd.clone, body=%wide.region_0.4_spmd.clone.sunk | while | flops 310742464 | bytes 24594968 | solution.py:82
  75.3 6.3 %gather_fusion = s32[768]{0:T(1024)} fusion(s32[1536]{0:T(1024)S(1)} %get-tuple-element.1162, s32[1024]{0:T(1024)} %pad_clamp_fusion.8), kind=kCustom, calls=%fused_computation.clone.clone.1 | custom fusion | bytes 9216 | tf_op jit(solution)/shard_map/while/body/eval_jaxpr/jit(_take)/gather | solution.py:67
  83.8 4.6 %fusion.142 = (f32[8,192]{1,0:T(8,128)}, f32[8,768,192]{1,2,0:T(8,128)}) fusion(pred[192,768]{1,0:T(8,128)(4,1)} %compare_and_fusion.7, bf16[192,8,128]{2,0,1:T(8,128)(2,1)S(1)} %get-tuple-element.1165, bf16[1536,8,128]{2,0,1:T(8,128)(2,1)S(1)} %copy-done.1, s32[]{:T(128)S(6)} %select_n.841), kind=kOutput, calls=%fused_computation.10.clone.1 | convolution fusion | flops 305527296 | bytes 6838276 | tf_op jit(solution)/shard_map/while/body/eval_jaxpr/qhd,khd->hqk/dot_general | solution.py:27
  94.7 6.3 %gather_fusion = s32[768]{0:T(1024)} fusion(s32[1536]{0:T(1024)S(1)} %get-tuple-element.1162, s32[1024]{0:T(1024)} %pad_clamp_fusion.8), kind=kCustom, calls=%fused_computation.clone.clone.1 | custom fusion | bytes 9216 | tf_op jit(solution)/shard_map/while/body/eval_jaxpr/jit(_take)/gather | solution.py:67
  103.2 4.6 %fusion.142 = (f32[8,192]{1,0:T(8,128)}, f32[8,768,192]{1,2,0:T(8,128)}) fusion(pred[192,768]{1,0:T(8,128)(4,1)} %compare_and_fusion.7, bf16[192,8,128]{2,0,1:T(8,128)(2,1)S(1)} %get-tuple-element.1165, bf16[1536,8,128]{2,0,1:T(8,128)(2,1)S(1)} %copy-done.1, s32[]{:T(128)S(6)} %select_n.841), kind=kOutput, calls=%fused_computation.10.clone.1 | convolution fusion | flops 305527296 | bytes 6838276 | tf_op jit(solution)/shard_map/while/body/eval_jaxpr/qhd,khd->hqk/dot_general | solution.py:27
  114.3 21.0 %all-gather.7.cloned.1.call-done = bf16[1536,8,128]{2,1,0:T(8,128)(2,1)} async-done(((bf16[192,8,128]{2,1,0:T(8,128)(2,1)}), bf16[1536,8,128]{2,1,0:T(8,128)(2,1)}) %all-gather.7.cloned.1.call-update) | async-done | bytes 3145744 | tf_op jit(solution)/shard_map/all_gather | solution.py:58
  135.3 4.0 %copy.35 = bf16[1536,8,128]{2,0,1:T(8,128)(2,1)} copy(bf16[1536,8,128]{2,1,0:T(8,128)(2,1)} %all-gather.7.cloned.1.call-done) | data formatting | bytes 6291456
  139.4 21.8 %while.51 = (s32[]{:T(128)}, f32[192,8,128]{2,0,1:T(8,128)}, bf16[1536,8,128]{2,0,1:T(8,128)(2,1)}, s32[1536]{0:T(1024)S(1)}, s32[192]{0:T(256)}, /*index=5*/bf1...) while((s32[]{:T(128)}, f32[192,8,128]{2,0,1:T(8,128)}, ...), condition=%wide.region_5.7_spmd.clone, body=%wide.region_4.6_spmd.clone.sunk | while | flops 609578944 | bytes 5453768 | solution.py:94
  140.0 4.6 %gather_fusion.1 = s32[768]{0:T(1024)S(1)} fusion(s32[1536]{0:T(1024)S(1)} %get-tuple-element.1200, s32[1024]{0:T(1024)} %pad_clamp_fusion.9), kind=kCustom, calls=%fused_computation.1.clone.clone.1 | custom fusion | bytes 9216 | tf_op jit(solution)/shard_map/while/body/eval_jaxpr/jit(_take)/gather | solution.py:67
  146.1 4.1 %fusion.149 = f32[192,8,128]{2,0,1:T(8,128)} fusion(bf16[1536,8,128]{2,0,1:T(8,128)(2,1)} %get-tuple-element.1199, s32[]{:T(128)S(6)} %select_n.855, bf16[192,8,128]{2,0,1:T(8,128)(2,1)S(1)} %get-tuple-element.1203, f32[8,192]{1,0:T(8,128)} %get-tuple-element.1204, pred[192,768]{1,0:T(8,128)(4,1)} %compare_and_fusion.8, ...), kind=kOutput, calls=%fused_computation.49.clone.1 | convolution fusion | flops 609091584 | bytes 5268992 | tf_op jit(solution)/shard_map/while/body/eval_jaxpr/hqk,khd->qhd/dot_general | solution.py:89
  150.8 4.6 %gather_fusion.1 = s32[768]{0:T(1024)S(1)} fusion(s32[1536]{0:T(1024)S(1)} %get-tuple-element.1200, s32[1024]{0:T(1024)} %pad_clamp_fusion.9), kind=kCustom, calls=%fused_computation.1.clone.clone.1 | custom fusion | bytes 9216 | tf_op jit(solution)/shard_map/while/body/eval_jaxpr/jit(_take)/gather | solution.py:67
  156.9 4.3 %fusion.149 = f32[192,8,128]{2,0,1:T(8,128)} fusion(bf16[1536,8,128]{2,0,1:T(8,128)(2,1)} %get-tuple-element.1199, s32[]{:T(128)S(6)} %select_n.855, bf16[192,8,128]{2,0,1:T(8,128)(2,1)S(1)} %get-tuple-element.1203, f32[8,192]{1,0:T(8,128)} %get-tuple-element.1204, pred[192,768]{1,0:T(8,128)(4,1)} %compare_and_fusion.8, ...), kind=kOutput, calls=%fused_computation.49.clone.1 | convolution fusion | flops 609091584 | bytes 5268992 | tf_op jit(solution)/shard_map/while/body/eval_jaxpr/hqk,khd->qhd/dot_general | solution.py:89
  165.9 31.1 %all-gather = f32[8,192,8]{1,2,0:T(8,128)S(1)} all-gather(f32[1,192,8]{1,2,0:T(8,128)} %bitcast.99), channel_id=1, replica_groups=mesh['grp'=2,'ctx'=8,'head'=2] {'ctx'}, dimensions={0}, use_global_device_ids=true | all-gather | bytes 55296 | tf_op jit(solution)/shard_map/all_gather | solution.py:111
  200.1 30.8 %all-gather.1 = f32[8,192,8]{1,2,0:T(8,128)S(1)} all-gather(f32[1,192,8]{1,2,0:T(8,128)S(1)} %copy.48), channel_id=1, replica_groups=mesh['grp'=2,'ctx'=8,'head'=2] {'ctx'}, dimensions={0}, use_global_device_ids=true | all-gather | bytes 55296 | tf_op jit(solution)/shard_map/all_gather | solution.py:112
  233.1 31.8 %while.52 = (s32[]{:T(128)}, f32[192,8,128]{2,0,1:T(8,128)}, bf16[1536,8,128]{2,0,1:T(8,128)(2,1)S(1)}, s32[1536]{0:T(1024)S(1)}, s32[192]{0:T(256)}, /*index=5*...) while((s32[]{:T(128)}, f32[192,8,128]{2,0,1:T(8,128)}, ...), condition=%wide.region_8.10_spmd.clone, body=%wide.region_7.9_spmd.clone.sunk | while | flops 916287424 | bytes 16865244 | solution.py:107
  236.6 4.6 %gather_fusion.2 = s32[768]{0:T(1024)S(1)} fusion(s32[1536]{0:T(1024)S(1)} %get-tuple-element.1243, s32[1024]{0:T(1024)} %pad_clamp_fusion.10), kind=kCustom, calls=%fused_computation.2.clone.clone.1 | custom fusion | bytes 9216 | tf_op jit(solution)/shard_map/while/body/eval_jaxpr/jit(_take)/gather | solution.py:67
  242.7 6.2 %fusion.157 = f32[192,8,128]{2,0,1:T(8,128)} fusion(bf16[1536,8,128]{2,0,1:T(8,128)(2,1)S(1)} %get-tuple-element.1242, s32[]{:T(128)S(6)} %select_n.869, f32[8,768,192]{1,2,0:T(8,128)} %fusion.156, f32[8,192]{1,0:T(8,128)} %get-tuple-element.1249, f32[8,192]{1,0:T(8,128)} %get-tuple-element.1246, pred[192,768]{1,0:T(8,128)(4,1)} %compare_and_fusion.9, ...), kind=kOutput, calls=%fused_computation.83.clone.1 | convolution fusion | flops 613810176 | bytes 9995776 | tf_op jit(solution)/shard_map/while/body/eval_jaxpr/hqk,khd->qhd/dot_general | solution.py:103
  252.4 4.6 %gather_fusion.2 = s32[768]{0:T(1024)S(1)} fusion(s32[1536]{0:T(1024)S(1)} %get-tuple-element.1243, s32[1024]{0:T(1024)} %pad_clamp_fusion.10), kind=kCustom, calls=%fused_computation.2.clone.clone.1 | custom fusion | bytes 9216 | tf_op jit(solution)/shard_map/while/body/eval_jaxpr/jit(_take)/gather | solution.py:67
  258.6 6.3 %fusion.157 = f32[192,8,128]{2,0,1:T(8,128)} fusion(bf16[1536,8,128]{2,0,1:T(8,128)(2,1)S(1)} %get-tuple-element.1242, s32[]{:T(128)S(6)} %select_n.869, f32[8,768,192]{1,2,0:T(8,128)} %fusion.156, f32[8,192]{1,0:T(8,128)} %get-tuple-element.1249, f32[8,192]{1,0:T(8,128)} %get-tuple-element.1246, pred[192,768]{1,0:T(8,128)(4,1)} %compare_and_fusion.9, ...), kind=kOutput, calls=%fused_computation.83.clone.1 | convolution fusion | flops 613810176 | bytes 9995776 | tf_op jit(solution)/shard_map/while/body/eval_jaxpr/hqk,khd->qhd/dot_general | solution.py:103
  267.3 6.7 %select_convert_fusion = bf16[8,1536,192]{1,2,0:T(8,128)(2,1)} fusion(bf16[1536,8,128]{2,0,1:T(8,128)(2,1)} %all-gather.11.cloned.1.call-done, f32[8,1536]{1,0:T(8,128)} %bitcast.97, pred[1536,192]{0,1:T(8,128)(4,1)} %compare_and_fusion.3, bf16[192,8,128]{2,1,0:T(8,128)(2,1)} %param.14), kind=kOutput, calls=%fused_computation.107 | convolution fusion | flops 613416960 | bytes 8601600 | tf_op jit(solution)/shard_map/qhd,khd->hqk/dot_general | solution.py:27
  274.0 6.9 %fusion.97 = bf16[192,8,128]{2,0,1:T(8,128)(2,1)S(1)} fusion(bf16[1536,8,128]{2,0,1:T(8,128)(2,1)} %all-gather.11.cloned.1.call-done, bf16[8,1536,192]{1,2,0:T(8,128)(2,1)} %select_convert_fusion, bf16[1536,8,128]{2,0,1:T(8,128)(2,1)} %all-gather.13.cloned.1.call-done, f32[8,1536]{1,0:T(8,128)S(1)} %bitcast.98, bf16[192,8,128]{2,1,0:T(8,128)(2,1)S(1)} %copy-done.4), kind=kOutput, calls=%fused_computation.113 | convolution fusion | flops 1217789952 | bytes 11845632 | tf_op jit(solution)/shard_map/hqk,qhd->khd/dot_general | solution.py:126
  281.9 4.7 %fusion.96 = bf16[192,8,128]{2,0,1:T(8,128)(2,1)S(1)} fusion(bf16[8,1536,192]{1,2,0:T(8,128)(2,1)} %select_convert_fusion, bf16[1536,8,128]{2,0,1:T(8,128)(2,1)} %all-gather.13.cloned.1.call-done), kind=kOutput, calls=%fused_computation.112 | convolution fusion | flops 604176384 | bytes 8257536 | tf_op jit(solution)/shard_map/hqk,qhd->khd/dot_general | solution.py:129
  (99 shorter events, 57.9 us)
Async XLA Ops:
  7.2 9.2 %copy-start = (s32[1536]{0:T(1024)S(1)}, s32[1536]{0:T(1024)}, u32[]{:S(2)}) copy-start(s32[1536]{0:T(1024)} %param.17) | copy-start | bytes 18436
  7.2 66.9 %all-gather.9.cloned.1.call-start = ((), (), s32[]{:S(2)}) async-start(), calls=%async_computation.1 | async-start | bytes 3538944 | tf_op jit(solution)/shard_map/all_gather | solution.py:57
  9.0 126.3 %all-gather.7.cloned.1.call-start = ((), (), s32[]{:S(2)}) async-start(), calls=%async_computation | async-start | bytes 3538944 | tf_op jit(solution)/shard_map/all_gather | solution.py:58
  9.8 257.5 %all-gather.11.cloned.1.call-start = ((), (), s32[]{:S(2)}) async-start(), calls=%async_computation.2 | async-start | bytes 3538944 | tf_op jit(solution)/shard_map/all_gather | solution.py:114
  11.7 262.3 %all-gather.13.cloned.1.call-start = ((), (), s32[]{:S(2)}) async-start(), calls=%async_computation.3 | async-start | bytes 3538944 | tf_op jit(solution)/shard_map/all_gather | solution.py:115
  13.8 60.3 %copy-start.3 = (bf16[192,8,128]{2,0,1:T(8,128)(2,1)S(1)}, bf16[192,8,128]{2,0,1:T(8,128)(2,1)}, u32[]{:S(2)}) copy-start(bf16[192,8,128]{2,0,1:T(8,128)(2,1)} %copy.36) | copy-start | bytes 1179652
  74.0 9.8 %copy-start.1 = (bf16[1536,8,128]{2,0,1:T(8,128)(2,1)S(1)}, bf16[1536,8,128]{2,0,1:T(8,128)(2,1)}, u32[]{:S(2)}) copy-start(bf16[1536,8,128]{2,0,1:T(8,128)(2,1)} %get-tuple-element.1164) | copy-start | bytes 9437188 | tf_op jit(solution)/shard_map/while
  88.4 4.4 %copy-start.5 = (f32[8,192]{1,0:T(8,128)S(1)}, f32[8,192]{1,0:T(8,128)}, u32[]{:S(2)}) copy-start(f32[8,192]{1,0:T(8,128)} %get-tuple-element.1149) | copy-start | bytes 18436 | tf_op jit(solution)/shard_map/while
  92.9 0.6 copy-start.6
  93.5 9.8 %copy-start.1 = (bf16[1536,8,128]{2,0,1:T(8,128)(2,1)S(1)}, bf16[1536,8,128]{2,0,1:T(8,128)(2,1)}, u32[]{:S(2)}) copy-start(bf16[1536,8,128]{2,0,1:T(8,128)(2,1)} %get-tuple-element.1164) | copy-start | bytes 9437188 | tf_op jit(solution)/shard_map/while
  107.8 4.4 %copy-start.5 = (f32[8,192]{1,0:T(8,128)S(1)}, f32[8,192]{1,0:T(8,128)}, u32[]{:S(2)}) copy-start(f32[8,192]{1,0:T(8,128)} %get-tuple-element.1149) | copy-start | bytes 18436 | tf_op jit(solution)/shard_map/while
  112.3 0.6 copy-start.6
  112.9 26.5 %copy-start.2 = (bf16[1536,8,128]{2,0,1:T(8,128)(2,1)S(1)}, bf16[1536,8,128]{2,0,1:T(8,128)(2,1)}, u32[]{:S(2)}) copy-start(bf16[1536,8,128]{2,0,1:T(8,128)(2,1)} %get-tuple-element.1262) | copy-start | bytes 9437188
  267.2 6.7 %copy-start.4 = (bf16[192,8,128]{2,1,0:T(8,128)(2,1)S(1)}, bf16[192,8,128]{2,1,0:T(8,128)(2,1)}, u32[]{:S(2)}) copy-start(bf16[192,8,128]{2,1,0:T(8,128)(2,1)} %param.15) | copy-start | bytes 1179652
  267.3 6.7 %copy-start.7 = (f32[1536,8]{0,1:T(8,128)S(1)}, f32[1536,8]{0,1:T(8,128)}, u32[]{:S(2)}) copy-start(f32[1536,8]{0,1:T(8,128)} %reshape.579) | copy-start | bytes 147460
Sparse Core Ops, SparseCore 0:
  10.8 63.2 all-gather.8
  76.2 59.0 all-gather.6
  138.1 60.3 all-gather.10
  200.5 59.2 all-gather.12
where the time goes:
time: 295 us; the launch traced here: 294 us
  waiting for transfers between devices  69.4 us (24%)
  blocking collectives  61.9 us (21%)
  local copies, waits for them, and re-layouts  60.9 us (21%)
  matrix products  54.1 us (18%)
  other arithmetic  33.7 us (11%)
  between operations  13.9 us (5%)
    all_gather x1, waiting for transfers between devices, on_device(): lax.all_gather(key_vecs, 'ctx', axis=0, tiled=True)  47.6 us
    all_gather x1, blocking collectives, on_device(): lax.all_gather(lse.T, 'ctx', axis=0, tiled=True)  31.1 us
    gather x6, local copies, waits for them, and re-layouts, key_slices(): key_doc = jnp.take(doc_ids, key_pos)  30.9 us
    all_gather x1, blocking collectives, on_device(): lax.all_gather(delta_rows, 'ctx', axis=0, tiled=True)  30.8 us
    dot_general x5, matrix products, score_block(): jnp.einsum('qhd,khd->hqk', query_blk, key_blk, preferred_element_type=jnp...  21.7 us
    all_gather x1, waiting for transfers between devices, on_device(): lax.all_gather(value_vecs, 'ctx', axis=0, tiled=True)  21 us
    unnamed x20, local copies, waits for them, and re-layouts  17.1 us
    dot_general x2, matrix products, query_step(): jnp.einsum('hqk,khd->qhd', dscores, key_blk, preferred_element_type=jnp.f...  12.5 us
  transfers between devices with their start and end apart: 4, of which 2 were waited for; matrix products, arithmetic and copies ran while one was open for 45% of the time, Pallas kernels for 0%

commit v1 on v0

v1 whole, which is shorter than its diff:
```python
import functools
import math

import jax
import jax.numpy as jnp
from jax import lax
from jax.experimental import pallas as pl
from jax.experimental.pallas import tpu as pltpu
from jax.sharding import PartitionSpec as P

TILE = 256
HIDDEN = -1e30


def partner_order(count):
    return sorted(range(1, count), key=lambda d: (-(d.bit_length()), -d))


def nt_dot(a, b):
    return lax.dot_general(a, b, (((1,), (1,)), ((), ())), preferred_element_type=jnp.float32)


def dot(a, b):
    return jnp.dot(a, b, preferred_element_type=jnp.float32)


def attention_kernel(count, tile_most, *refs):
    scalars, start_ref = refs[0], refs[1]
    ins = refs[2 : 2 + count]
    outs = refs[2 + count : 2 + 2 * count]
    rows, key_t, value_t, scores, weights, key_sum, value_sum, result = refs[2 + 2 * count :]
    me = scalars[0]
    shard_rows = ins[0].shape[1]
    half = shard_rows // 2
    tokens = rows.shape[1]
    head_size = rows.shape[2]
    tile = TILE
    scaling = head_size ** (-0.5)
    exponent = scaling * math.log2(math.e)

    for d in range(count):
        shard = me ^ d
        low = pl.multiple_of(shard * half, half)
        high = pl.multiple_of((2 * count - 1 - shard) * half, half)
        for t in range(4):
            rows[t, pl.ds(low, half), :] = ins[d][t, :half, :]
            rows[t, pl.ds(high, half), :] = ins[d][t, half:, :]
    for b in range(tokens // tile):
        block = pl.ds(b * tile, tile)
        key_t[:, block] = rows[1, block, :].T
        value_t[:, block] = rows[2, block, :].T
    key_sum[...] = jnp.zeros_like(key_sum)
    value_sum[...] = jnp.zeros_like(value_sum)

    def query_tile(size, j):
        q_at = pl.multiple_of(j * tile, tile)
        k_at = pl.multiple_of((j - (size - 1)) * tile, tile)
        q_blk = rows[0, pl.ds(q_at, tile), :]
        start = start_ref[:, pl.ds(q_at, tile)]
        best = jnp.full((1, tile), HIDDEN, jnp.float32)
        for i in range(size):
            s = nt_dot(rows[1, pl.ds(k_at + i * tile, tile), :], q_blk) * exponent
            k_pos = lax.broadcasted_iota(jnp.int32, (tile, tile), 0) + (k_at + i * tile)
            seen = k_pos >= start
            if i == size - 1:
                q_pos = lax.broadcasted_iota(jnp.int32, (tile, tile), 1) + q_at
                seen = seen & (k_pos <= q_pos)
            s = jnp.where(seen, s, HIDDEN)
            scores[i * tile : (i + 1) * tile, :] = s
            best = jnp.maximum(best, jnp.max(s, axis=0, keepdims=True))
        total = jnp.zeros((1, tile), jnp.float32)
        for i in range(size):
            e = jnp.exp2(scores[i * tile : (i + 1) * tile, :] - best)
            total = total + jnp.sum(e, axis=0, keepdims=True)
            weights[i * tile : (i + 1) * tile, :] = e.astype(jnp.bfloat16)
        inverse = 1.0 / total
        out_t = dot(value_t[:, pl.ds(k_at, size * tile)], weights[: size * tile, :]) * inverse
        out = out_t.astype(jnp.bfloat16)
        result[0, pl.ds(q_at, tile), :] = out_t.T.astype(jnp.bfloat16)
        grad_t = rows[3, pl.ds(q_at, tile), :].astype(jnp.float32).T * inverse
        delta = jnp.sum(grad_t * out.astype(jnp.float32), axis=0, keepdims=True)
        grad_tb = grad_t.astype(jnp.bfloat16)
        grad = grad_t.T.astype(jnp.bfloat16)
        query_t = jnp.zeros((head_size, tile), jnp.float32)
        for i in range(size):
            keys = pl.ds(k_at + i * tile, tile)
            e = weights[i * tile : (i + 1) * tile, :]
            value_sum[keys, :] += dot(e, grad)
            dprobs = dot(rows[2, keys, :], grad_tb)
            ds = (e.astype(jnp.float32) * (dprobs - delta)).astype(jnp.bfloat16)
            key_sum[keys, :] += dot(ds, q_blk)
            query_t = query_t + dot(key_t[:, keys], ds)
        result[1, pl.ds(q_at, tile), :] = (query_t * scaling).T.astype(jnp.bfloat16)

    @pl.loop(0, tokens // tile)
    def _(j):
        size = j - scalars[1 + j] + 1
        for n in range(1, tile_most + 1):

            @pl.when(size == n)
            def _(n=n):
                query_tile(n, j)

    result[2] = (key_sum[...] * scaling).astype(jnp.bfloat16)
    result[3] = value_sum[...].astype(jnp.bfloat16)
    for d in range(count):
        shard = me ^ d
        low = pl.multiple_of(shard * half, half)
        high = pl.multiple_of((2 * count - 1 - shard) * half, half)
        for t in range(4):
            outs[d][t, :half, :] = result[t, pl.ds(low, half), :]
            outs[d][t, half:, :] = result[t, pl.ds(high, half), :]


def attend(blocks, doc_ids, me):
    count = len(blocks)
    tokens = doc_ids.shape[0]
    head_size = blocks[0].shape[2]
    tiles = tokens // TILE
    longest = tokens * 5 // 8
    tile_most = min(tiles, 1 + -(-(longest - 1) // TILE))
    start = jnp.sum((doc_ids[:, None] < doc_ids[None, :]).astype(jnp.int32), axis=0)
    scalars = jnp.concatenate([me[None], start[::TILE] // TILE]).astype(jnp.int32)
    span = tile_most * TILE
    return pl.pallas_call(
        functools.partial(attention_kernel, count, tile_most),
        out_shape=[jax.ShapeDtypeStruct(b.shape, b.dtype) for b in blocks],
        in_specs=[pl.BlockSpec(memory_space=pltpu.SMEM)]
        + [pl.BlockSpec(memory_space=pltpu.VMEM)] * (count + 1),
        out_specs=[pl.BlockSpec(memory_space=pltpu.VMEM)] * count,
        scratch_shapes=[
            pltpu.VMEM((4, tokens, head_size), jnp.bfloat16),
            pltpu.VMEM((head_size, tokens), jnp.bfloat16),
            pltpu.VMEM((head_size, tokens), jnp.bfloat16),
            pltpu.VMEM((span, TILE), jnp.float32),
            pltpu.VMEM((span, TILE), jnp.bfloat16),
            pltpu.VMEM((tokens, head_size), jnp.float32),
            pltpu.VMEM((tokens, head_size), jnp.float32),
            pltpu.VMEM((4, tokens, head_size), jnp.bfloat16),
        ],
        compiler_params=pltpu.CompilerParams(vmem_limit_bytes=40 << 20),
    )(scalars, start[None, :], *blocks)


def on_device(queries, key_vecs, value_vecs, out_grad, doc_ids):
    head_count = queries.shape[1]
    count = lax.axis_size("ctx")
    me = lax.axis_index("ctx")
    copies = count // head_count

    def exchange(blocks):
        got = [blocks[0]] + [None] * (count - 1)
        for d in partner_order(count):
            got[d] = lax.ppermute(blocks[d], "ctx", [(s, s ^ d) for s in range(count)])
        return got

    arrays = (queries, key_vecs, value_vecs, out_grad)
    packed = jnp.stack([jnp.swapaxes(a, 0, 1) for a in arrays], 1)
    mine = [
        lax.dynamic_index_in_dim(packed, (me ^ d) // copies, 0, keepdims=False)
        for d in range(count)
    ]
    returned = exchange(attend(exchange(mine), doc_ids, me))
    whole = jnp.zeros_like(packed)
    for d in range(count):
        whole = lax.dynamic_update_index_in_dim(whole, returned[d], (me ^ d) // copies, 0)
    return tuple(jnp.swapaxes(whole[:, t], 0, 1) for t in range(4))


def solution(mesh):
    spec = P(("grp", "ctx"), "head", None)
    return jax.shard_map(
        on_device,
        mesh=mesh,
        in_specs=(spec, spec, spec, spec, P("grp")),
        out_specs=(spec, spec, spec, spec),
        check_vma=False,
    )
```

time: 295 us -> 157 us (0.53)
  blocking collectives: 61.9 us -> 0 us
  matrix products: 54.1 us -> 0 us
  waiting for transfers between devices: 69.4 us -> 26.7 us
  starting transfers between devices: 0.16 us -> 32.6 us
  other arithmetic: 33.7 us -> 1.27 us
  local copies, waits for them, and re-layouts: 60.9 us -> 84.4 us
  between operations: 13.9 us -> 0.96 us
  Pallas kernels: 0 us -> 9.57 us
    dynamic_update_slice x0 -> x8, local copies, waits for them, and re-layouts: none -> 70.6 us  [on_device(): lax.dynamic_update_index_in_dim(whole, returned[d], (me ^ d) // copies, 0)]
    all_gather x4 -> x0, waiting for transfers between devices: 68.6 us -> none  [the longest x1 47.6 us: on_device(): lax.all_gather(key_vecs, 'ctx', axis=0, tiled=True)]
    all_gather x2 -> x0, blocking collectives: 61.9 us -> none  [the longest x1 31.1 us: on_device(): lax.all_gather(lse.T, 'ctx', axis=0, tiled=True)]
    dot_general x11 -> x0, matrix products: 54.1 us -> none  [the longest x5 21.7 us: score_block(): jnp.einsum('qhd,khd->hqk', query_blk, key_blk, preferred_element_type=jnp...]
    gather x8 -> x0, local copies, waits for them, and re-layouts: 41.3 us -> none  [the longest x6 30.9 us: key_slices(): key_doc = jnp.take(doc_ids, key_pos)]
    ppermute x0 -> x14, starting transfers between devices: none -> 32.6 us  [exchange(): got[d] = lax.ppermute(blocks[d], 'ctx', [(s, s ^ d) for s in range(count)])]
    ppermute x0 -> x14, waiting for transfers between devices: none -> 26.7 us  [exchange(): got[d] = lax.ppermute(blocks[d], 'ctx', [(s, s ^ d) for s in range(count)])]
    unnamed x20, local copies, waits for them, and re-layouts: 17.1 us -> 0.05 us
  transfers between devices with their start and end apart: 4 -> 14, of which waited for: 2 -> 5; matrix products, arithmetic and copies ran while one was open for 45% -> 12% of each run, Pallas kernels for 0% -> 0%
where the time goes in v1:
time: 157 us; the launch traced here: 156 us
  local copies, waits for them, and re-layouts  84.4 us (54%)
  starting transfers between devices  32.6 us (21%)
  waiting for transfers between devices  26.7 us (17%)
  Pallas kernels  9.57 us (6%)
    dynamic_update_slice x8, local copies, waits for them, and re-layouts, on_device(): lax.dynamic_update_index_in_dim(whole, returned[d], (me ^ d) // copies, 0)  70.6 us
    ppermute x14, starting transfers between devices, exchange(): got[d] = lax.ppermute(blocks[d], 'ctx', [(s, s ^ d) for s in range(count)])  32.6 us
    ppermute x14, waiting for transfers between devices, exchange(): got[d] = lax.ppermute(blocks[d], 'ctx', [(s, s ^ d) for s in range(count)])  26.7 us
    broadcast_in_dim x8, local copies, waits for them, and re-layouts, on_device(): lax.dynamic_update_index_in_dim(whole, returned[d], (me ^ d) // copies, 0)  10.7 us
    pallas_call x1, Pallas kernels, attend(): pl.pallas_call(functools.partial(attention_kernel, count, tile_most), out...  9.57 us
  transfers between devices with their start and end apart: 14, of which 5 were waited for; matrix products, arithmetic and copies ran while one was open for 12% of the time, Pallas kernels for 0%

profile of v1, /device:TPU:0, one launch (start us, length us, event | category | flops | bytes accessed | tf_op | source)
XLA Modules:
  0.0 155.5 jit_solution(10507154003305135454)
XLA Ops:
  2.6 3.0 %collective-permute-start = (bf16[4,192,128]{2,1,0:T(8,128)(2,1)S(1)}, bf16[4,192,128]{2,1,0:T(8,128)(2,1)S(1)}, u32[]{:S(2)}, u32[]{:S(2)}) collective-permute-start(bf16[4,192,128]{2,1,0:T(8,128)(2,1)S(1)} %get-tuple-element.30), channel_id=1, source_target_pairs={{0,2},{2,0},{4,6},{6,4},{8,10},{10,8},{12,14},{14,12},{1,3},{3,1},... | collective-permute-start | bytes 589832 | tf_op jit(solution)/shard_map/ppermute | solution.py:154
  5.6 1.6 %collective-permute-start.1 = (bf16[4,192,128]{2,1,0:T(8,128)(2,1)S(1)}, bf16[4,192,128]{2,1,0:T(8,128)(2,1)S(1)}, u32[]{:S(2)}, u32[]{:S(2)}) collective-permute-start(bf16[4,192,128]{2,1,0:T(8,128)(2,1)S(1)} %get-tuple-element.29), channel_id=1, source_target_pairs={{0,4},{2,6},{4,0},{6,2},{8,12},{10,14},{12,8},{14,10},{1,5},{3,7},... | collective-permute-start | bytes 589832 | tf_op jit(solution)/shard_map/ppermute | solution.py:154
  7.2 3.0 %collective-permute-start.3 = (bf16[4,192,128]{2,1,0:T(8,128)(2,1)S(1)}, bf16[4,192,128]{2,1,0:T(8,128)(2,1)S(1)}, u32[]{:S(2)}, u32[]{:S(2)}) collective-permute-start(bf16[4,192,128]{2,1,0:T(8,128)(2,1)S(1)} %get-tuple-element.27), channel_id=1, source_target_pairs={{0,8},{2,10},{4,12},{6,14},{8,0},{10,2},{12,4},{14,6},{1,9},{3,11}... | collective-permute-start | bytes 589832 | tf_op jit(solution)/shard_map/ppermute | solution.py:154
  12.5 3.7 %collective-permute-start.5 = (bf16[4,192,128]{2,1,0:T(8,128)(2,1)S(1)}, bf16[4,192,128]{2,1,0:T(8,128)(2,1)S(1)}, u32[]{:S(2)}, u32[]{:S(2)}) collective-permute-start(bf16[4,192,128]{2,1,0:T(8,128)(2,1)S(1)} %get-tuple-element.25), channel_id=1, source_target_pairs={{0,12},{2,14},{4,8},{6,10},{8,4},{10,6},{12,0},{14,2},{1,13},{3,15... | collective-permute-start | bytes 589832 | tf_op jit(solution)/shard_map/ppermute | solution.py:154
  16.2 4.9 %collective-permute-done.1.refs_4_ = bf16[4,192,128]{2,1,0:T(8,128)(2,1)S(1)} collective-permute-done((bf16[4,192,128]{2,1,0:T(8,128)(2,1)S(1)}, bf16[4,192,128]{2,1,0:T(8,128)(2,1)S(1)}, u32[]{:S(2)}, u32[]{:S(2)}) %collective-permute-start.1) | collective-permute-done | bytes 196640 | tf_op jit(solution)/shard_map/ppermute | solution.py:154
  22.8 15.5 %collective-permute-done.4.refs_7_ = bf16[4,192,128]{2,1,0:T(8,128)(2,1)S(1)} collective-permute-done((bf16[4,192,128]{2,1,0:T(8,128)(2,1)S(1)}, bf16[4,192,128]{2,1,0:T(8,128)(2,1)S(1)}, u32[]{:S(2)}, u32[]{:S(2)}) %collective-permute-start.4) | collective-permute-done | bytes 196640 | tf_op jit(solution)/shard_map/ppermute | solution.py:154
  38.3 9.6 %shard_map.84 = (bf16[4,192,128]{2,1,0:T(8,128)(2,1)S(1)}, bf16[4,192,128]{2,1,0:T(8,128)(2,1)S(1)}, bf16[4,192,128]{2,1,0:T(8,128)(2,1)S(1)}, bf16[4,192,128]{2...) custom-call(s32[7]{0:T(128)S(1)} %pad_add_fusion.refs_0_, ...), custom_call_target="tpu_custom_call" | custom-call | tf_op jit(solution)/shard_map/pallas_call | solution.py:125
  48.0 7.8 %collective-permute-start.8 = (bf16[4,192,128]{2,1,0:T(8,128)(2,1)S(1)}, bf16[4,192,128]{2,1,0:T(8,128)(2,1)S(1)}, u32[]{:S(2)}, u32[]{:S(2)}) collective-permute-start(bf16[4,192,128]{2,1,0:T(8,128)(2,1)S(1)} %get-tuple-element.14), channel_id=1, source_target_pairs={{0,4},{2,6},{4,0},{6,2},{8,12},{10,14},{12,8},{14,10},{1,5},{3,7},... | collective-permute-start | bytes 589832 | tf_op jit(solution)/shard_map/ppermute | solution.py:154
  56.4 4.2 %collective-permute-start.10 = (bf16[4,192,128]{2,1,0:T(8,128)(2,1)S(1)}, bf16[4,192,128]{2,1,0:T(8,128)(2,1)S(1)}, u32[]{:S(2)}, u32[]{:S(2)}) collective-permute-start(bf16[4,192,128]{2,1,0:T(8,128)(2,1)S(1)} %get-tuple-element.16), channel_id=1, source_target_pairs={{0,8},{2,10},{4,12},{6,14},{8,0},{10,2},{12,4},{14,6},{1,9},{3,11}... | collective-permute-start | bytes 589832 | tf_op jit(solution)/shard_map/ppermute | solution.py:154
  60.6 2.4 %collective-permute-start.12 = (bf16[4,192,128]{2,1,0:T(8,128)(2,1)S(1)}, bf16[4,192,128]{2,1,0:T(8,128)(2,1)}, u32[]{:S(2)}, u32[]{:S(2)}) collective-permute-start(bf16[4,192,128]{2,1,0:T(8,128)(2,1)S(1)} %get-tuple-element.18), channel_id=1, source_target_pairs={{0,12},{2,14},{4,8},{6,10},{8,4},{10,6},{12,0},{14,2},{1,13},{3,15... | collective-permute-start | bytes 589832 | tf_op jit(solution)/shard_map/ppermute | solution.py:154
  63.0 3.6 %collective-permute-done.8 = bf16[4,192,128]{2,1,0:T(8,128)(2,1)S(1)} collective-permute-done((bf16[4,192,128]{2,1,0:T(8,128)(2,1)S(1)}, bf16[4,192,128]{2,1,0:T(8,128)(2,1)S(1)}, u32[]{:S(2)}, u32[]{:S(2)}) %collective-permute-start.8) | collective-permute-done | bytes 196640 | tf_op jit(solution)/shard_map/ppermute | solution.py:154
  66.5 4.2 %collective-permute-start.13 = (bf16[4,192,128]{2,1,0:T(8,128)(2,1)S(1)}, bf16[4,192,128]{2,1,0:T(8,128)(2,1)}, u32[]{:S(2)}, u32[]{:S(2)}) collective-permute-start(bf16[4,192,128]{2,1,0:T(8,128)(2,1)S(1)} %get-tuple-element.19), channel_id=1, source_target_pairs={{0,14},{2,12},{4,10},{6,8},{8,6},{10,4},{12,2},{14,0},{1,15},{3,13... | collective-permute-start | bytes 589832 | tf_op jit(solution)/shard_map/ppermute | solution.py:154
  71.2 8.8 %dynamic_update_slice.25 = bf16[8,4,192,128]{3,0,2,1:T(8,128)(2,1)S(1)} dynamic-update-slice(bf16[8,4,192,128]{3,0,2,1:T(8,128)(2,1)S(1)} %broadcast_in_dim.36, bf16[1,4,192,128]{3,0,2,1:T(2,128)(2,1)S(1)} %copy.33, s32[]{:T(128)S(6)} %select_n.58, s32[]{:T(128)} %constant.138.clone.1, s32[]{:T(128)} %constant.138.clone.1, s32[]{:T(128)} %constant.138.clone.1) | dynamic-update-slice | bytes 393220 | tf_op jit(solution)/shard_map/jit(dynamic_update_index_in_dim)/dynamic_update_slice | solution.py:166
  82.4 2.0 %copy.36 = bf16[1,4,192,128]{3,0,2,1:T(2,128)(2,1)} copy(bf16[1,4,192,128]{3,2,1,0:T(8,128)(2,1)} %bitcast.20) | data formatting | bytes 393216 | tf_op jit(solution)/shard_map/jit(dynamic_update_index_in_dim)/broadcast_in_dim | solution.py:166
  85.4 2.0 %collective-permute-done.11 = bf16[4,192,128]{2,1,0:T(8,128)(2,1)S(1)} collective-permute-done((bf16[4,192,128]{2,1,0:T(8,128)(2,1)S(1)}, bf16[4,192,128]{2,1,0:T(8,128)(2,1)S(1)}, u32[]{:S(2)}, u32[]{:S(2)}) %collective-permute-start.11) | collective-permute-done | bytes 196640 | tf_op jit(solution)/shard_map/ppermute | solution.py:154
  88.5 2.0 %copy.39 = bf16[1,4,192,128]{3,0,2,1:T(2,128)(2,1)} copy(bf16[1,4,192,128]{3,2,1,0:T(8,128)(2,1)} %bitcast.23) | data formatting | bytes 393216 | tf_op jit(solution)/shard_map/jit(dynamic_update_index_in_dim)/broadcast_in_dim | solution.py:166
  90.4 2.0 %copy.40 = bf16[1,4,192,128]{3,0,2,1:T(2,128)(2,1)} copy(bf16[1,4,192,128]{3,2,1,0:T(8,128)(2,1)} %bitcast.24) | data formatting | bytes 393216 | tf_op jit(solution)/shard_map/jit(dynamic_update_index_in_dim)/broadcast_in_dim | solution.py:166
  92.5 8.8 %dynamic_update_slice.26 = bf16[8,4,192,128]{3,0,2,1:T(8,128)(2,1)S(1)} dynamic-update-slice(bf16[8,4,192,128]{3,0,2,1:T(8,128)(2,1)S(1)} %dynamic_update_slice.25, bf16[1,4,192,128]{3,0,2,1:T(2,128)(2,1)S(1)} %copy-done, s32[]{:T(128)S(6)} %select_n.59, s32[]{:T(128)} %constant.138.clone.1, s32[]{:T(128)} %constant.138.clone.1, s32[]{:T(128)} %constant.138.clone.1) | dynamic-update-slice | bytes 393220 | tf_op jit(solution)/shard_map/jit(dynamic_update_index_in_dim)/dynamic_update_slice | solution.py:166
  101.3 8.8 %dynamic_update_slice.27 = bf16[8,4,192,128]{3,0,2,1:T(8,128)(2,1)S(1)} dynamic-update-slice(bf16[8,4,192,128]{3,0,2,1:T(8,128)(2,1)S(1)} %dynamic_update_slice.26, bf16[1,4,192,128]{3,0,2,1:T(2,128)(2,1)S(1)} %copy.35, s32[]{:T(128)S(6)} %select_n.60, s32[]{:T(128)} %constant.138.clone.1, s32[]{:T(128)} %constant.138.clone.1, s32[]{:T(128)} %constant.138.clone.1) | dynamic-update-slice | bytes 393220 | tf_op jit(solution)/shard_map/jit(dynamic_update_index_in_dim)/dynamic_update_slice | solution.py:166
  110.1 8.8 %dynamic_update_slice.28 = bf16[8,4,192,128]{3,0,2,1:T(8,128)(2,1)S(1)} dynamic-update-slice(bf16[8,4,192,128]{3,0,2,1:T(8,128)(2,1)S(1)} %dynamic_update_slice.27, bf16[1,4,192,128]{3,0,2,1:T(2,128)(2,1)S(1)} %copy-done.1, s32[]{:T(128)S(6)} %select_n.61, s32[]{:T(128)} %constant.138.clone.1, s32[]{:T(128)} %constant.138.clone.1, s32[]{:T(128)} %constant.138.clone.1) | dynamic-update-slice | bytes 393220 | tf_op jit(solution)/shard_map/jit(dynamic_update_index_in_dim)/dynamic_update_slice | solution.py:166
  118.9 9.0 %dynamic_update_slice.29 = bf16[8,4,192,128]{3,0,2,1:T(8,128)(2,1)S(1)} dynamic-update-slice(bf16[8,4,192,128]{3,0,2,1:T(8,128)(2,1)S(1)} %dynamic_update_slice.28, bf16[1,4,192,128]{3,0,2,1:T(2,128)(2,1)S(1)} %copy-done.2, s32[]{:T(128)S(6)} %select_n.62, s32[]{:T(128)} %constant.138.clone.1, s32[]{:T(128)} %constant.138.clone.1, s32[]{:T(128)} %constant.138.clone.1) | dynamic-update-slice | bytes 393220 | tf_op jit(solution)/shard_map/jit(dynamic_update_index_in_dim)/dynamic_update_slice | solution.py:166
  127.9 8.8 %dynamic_update_slice.30 = bf16[8,4,192,128]{3,0,2,1:T(8,128)(2,1)S(1)} dynamic-update-slice(bf16[8,4,192,128]{3,0,2,1:T(8,128)(2,1)S(1)} %dynamic_update_slice.29, bf16[1,4,192,128]{3,0,2,1:T(2,128)(2,1)S(1)} %copy-done.3, s32[]{:T(128)S(6)} %select_n.63, s32[]{:T(128)} %constant.138.clone.1, s32[]{:T(128)} %constant.138.clone.1, s32[]{:T(128)} %constant.138.clone.1) | dynamic-update-slice | bytes 393220 | tf_op jit(solution)/shard_map/jit(dynamic_update_index_in_dim)/dynamic_update_slice | solution.py:166
  136.8 8.8 %dynamic_update_slice.31 = bf16[8,4,192,128]{3,0,2,1:T(8,128)(2,1)S(1)} dynamic-update-slice(bf16[8,4,192,128]{3,0,2,1:T(8,128)(2,1)S(1)} %dynamic_update_slice.30, bf16[1,4,192,128]{3,0,2,1:T(2,128)(2,1)S(1)} %copy-done.4, s32[]{:T(128)S(6)} %select_n.64, s32[]{:T(128)} %constant.138.clone.1, s32[]{:T(128)} %constant.138.clone.1, s32[]{:T(128)} %constant.138.clone.1) | dynamic-update-slice | bytes 393220 | tf_op jit(solution)/shard_map/jit(dynamic_update_index_in_dim)/dynamic_update_slice | solution.py:166
  145.6 8.8 %dynamic_update_slice.32 = bf16[8,4,192,128]{3,0,2,1:T(8,128)(2,1)S(1)} dynamic-update-slice(bf16[8,4,192,128]{3,0,2,1:T(8,128)(2,1)S(1)} %dynamic_update_slice.31, bf16[1,4,192,128]{3,0,2,1:T(2,128)(2,1)S(1)} %copy-done.5, s32[]{:T(128)S(6)} %select_n.65, s32[]{:T(128)} %constant.138.clone.1, s32[]{:T(128)} %constant.138.clone.1, s32[]{:T(128)} %constant.138.clone.1) | dynamic-update-slice | bytes 393220 | tf_op jit(solution)/shard_map/jit(dynamic_update_index_in_dim)/dynamic_update_slice | solution.py:166
  (52 shorter events, 12.8 us)
Async XLA Ops:
  0.6 1.4 copy-start.7
  0.6 1.4 copy-start.6
  2.4 9.1 %copy-start.9 = (s32[1536]{0:T(1024)S(1)}, s32[1536]{0:T(1024)}, u32[]{:S(2)}) copy-start(s32[1536]{0:T(1024)} %param.9) | copy-start | bytes 18436
  2.6 10.0 %collective-permute-start = (bf16[4,192,128]{2,1,0:T(8,128)(2,1)S(1)}, bf16[4,192,128]{2,1,0:T(8,128)(2,1)S(1)}, u32[]{:S(2)}, u32[]{:S(2)}) collective-permute-start(bf16[4,192,128]{2,1,0:T(8,128)(2,1)S(1)} %get-tuple-element.30), channel_id=1, source_target_pairs={{0,2},{2,0},{4,6},{6,4},{8,10},{10,8},{12,14},{14,12},{1,3},{3,1},... | collective-permute-start | bytes 589832 | tf_op jit(solution)/shard_map/ppermute | solution.py:154
  5.6 15.5 %collective-permute-start.1 = (bf16[4,192,128]{2,1,0:T(8,128)(2,1)S(1)}, bf16[4,192,128]{2,1,0:T(8,128)(2,1)S(1)}, u32[]{:S(2)}, u32[]{:S(2)}) collective-permute-start(bf16[4,192,128]{2,1,0:T(8,128)(2,1)S(1)} %get-tuple-element.29), channel_id=1, source_target_pairs={{0,4},{2,6},{4,0},{6,2},{8,12},{10,14},{12,8},{14,10},{1,5},{3,7},... | collective-permute-start | bytes 589832 | tf_op jit(solution)/shard_map/ppermute | solution.py:154
  7.2 15.6 %collective-permute-start.2 = (bf16[4,192,128]{2,1,0:T(8,128)(2,1)S(1)}, bf16[4,192,128]{2,1,0:T(8,128)(2,1)S(1)}, u32[]{:S(2)}, u32[]{:S(2)}) collective-permute-start(bf16[4,192,128]{2,1,0:T(8,128)(2,1)S(1)} %get-tuple-element.28), channel_id=1, source_target_pairs={{0,6},{2,4},{4,2},{6,0},{8,14},{10,12},{12,10},{14,8},{1,7},{3,5},... | collective-permute-start | bytes 589832 | tf_op jit(solution)/shard_map/ppermute | solution.py:154
  7.2 15.6 %collective-permute-start.3 = (bf16[4,192,128]{2,1,0:T(8,128)(2,1)S(1)}, bf16[4,192,128]{2,1,0:T(8,128)(2,1)S(1)}, u32[]{:S(2)}, u32[]{:S(2)}) collective-permute-start(bf16[4,192,128]{2,1,0:T(8,128)(2,1)S(1)} %get-tuple-element.27), channel_id=1, source_target_pairs={{0,8},{2,10},{4,12},{6,14},{8,0},{10,2},{12,4},{14,6},{1,9},{3,11}... | collective-permute-start | bytes 589832 | tf_op jit(solution)/shard_map/ppermute | solution.py:154
  10.2 28.2 %collective-permute-start.4 = (bf16[4,192,128]{2,1,0:T(8,128)(2,1)S(1)}, bf16[4,192,128]{2,1,0:T(8,128)(2,1)S(1)}, u32[]{:S(2)}, u32[]{:S(2)}) collective-permute-start(bf16[4,192,128]{2,1,0:T(8,128)(2,1)S(1)} %get-tuple-element.26), channel_id=1, source_target_pairs={{0,10},{2,8},{4,14},{6,12},{8,2},{10,0},{12,6},{14,4},{1,11},{3,9}... | collective-permute-start | bytes 589832 | tf_op jit(solution)/shard_map/ppermute | solution.py:154
  12.5 25.8 %collective-permute-start.5 = (bf16[4,192,128]{2,1,0:T(8,128)(2,1)S(1)}, bf16[4,192,128]{2,1,0:T(8,128)(2,1)S(1)}, u32[]{:S(2)}, u32[]{:S(2)}) collective-permute-start(bf16[4,192,128]{2,1,0:T(8,128)(2,1)S(1)} %get-tuple-element.25), channel_id=1, source_target_pairs={{0,12},{2,14},{4,8},{6,10},{8,4},{10,6},{12,0},{14,2},{1,13},{3,15... | collective-permute-start | bytes 589832 | tf_op jit(solution)/shard_map/ppermute | solution.py:154
  21.1 17.3 %collective-permute-start.6 = (bf16[4,192,128]{2,1,0:T(8,128)(2,1)S(1)}, bf16[4,192,128]{2,1,0:T(8,128)(2,1)S(1)}, u32[]{:S(2)}, u32[]{:S(2)}) collective-permute-start(bf16[4,192,128]{2,1,0:T(8,128)(2,1)S(1)} %get-tuple-element.24), channel_id=1, source_target_pairs={{0,14},{2,12},{4,10},{6,8},{8,6},{10,4},{12,2},{14,0},{1,15},{3,13... | collective-permute-start | bytes 589832 | tf_op jit(solution)/shard_map/ppermute | solution.py:154
  47.9 12.7 %collective-permute-start.7 = (bf16[4,192,128]{2,1,0:T(8,128)(2,1)S(1)}, bf16[4,192,128]{2,1,0:T(8,128)(2,1)S(1)}, u32[]{:S(2)}, u32[]{:S(2)}) collective-permute-start(bf16[4,192,128]{2,1,0:T(8,128)(2,1)S(1)} %get-tuple-element.13), channel_id=1, source_target_pairs={{0,2},{2,0},{4,6},{6,4},{8,10},{10,8},{12,14},{14,12},{1,3},{3,1},... | collective-permute-start | bytes 589832 | tf_op jit(solution)/shard_map/ppermute | solution.py:154
  48.0 18.5 %collective-permute-start.8 = (bf16[4,192,128]{2,1,0:T(8,128)(2,1)S(1)}, bf16[4,192,128]{2,1,0:T(8,128)(2,1)S(1)}, u32[]{:S(2)}, u32[]{:S(2)}) collective-permute-start(bf16[4,192,128]{2,1,0:T(8,128)(2,1)S(1)} %get-tuple-element.14), channel_id=1, source_target_pairs={{0,4},{2,6},{4,0},{6,2},{8,12},{10,14},{12,8},{14,10},{1,5},{3,7},... | collective-permute-start | bytes 589832 | tf_op jit(solution)/shard_map/ppermute | solution.py:154
  55.7 26.6 %collective-permute-start.9 = (bf16[4,192,128]{2,1,0:T(8,128)(2,1)S(1)}, bf16[4,192,128]{2,1,0:T(8,128)(2,1)}, u32[]{:S(2)}, u32[]{:S(2)}) collective-permute-start(bf16[4,192,128]{2,1,0:T(8,128)(2,1)S(1)} %get-tuple-element.15), channel_id=1, source_target_pairs={{0,6},{2,4},{4,2},{6,0},{8,14},{10,12},{12,10},{14,8},{1,7},{3,5},... | collective-permute-start | bytes 589832 | tf_op jit(solution)/shard_map/ppermute | solution.py:154
  56.4 28.0 %collective-permute-start.10 = (bf16[4,192,128]{2,1,0:T(8,128)(2,1)S(1)}, bf16[4,192,128]{2,1,0:T(8,128)(2,1)S(1)}, u32[]{:S(2)}, u32[]{:S(2)}) collective-permute-start(bf16[4,192,128]{2,1,0:T(8,128)(2,1)S(1)} %get-tuple-element.16), channel_id=1, source_target_pairs={{0,8},{2,10},{4,12},{6,14},{8,0},{10,2},{12,4},{14,6},{1,9},{3,11}... | collective-permute-start | bytes 589832 | tf_op jit(solution)/shard_map/ppermute | solution.py:154
  60.6 26.8 %collective-permute-start.11 = (bf16[4,192,128]{2,1,0:T(8,128)(2,1)S(1)}, bf16[4,192,128]{2,1,0:T(8,128)(2,1)S(1)}, u32[]{:S(2)}, u32[]{:S(2)}) collective-permute-start(bf16[4,192,128]{2,1,0:T(8,128)(2,1)S(1)} %get-tuple-element.17), channel_id=1, source_target_pairs={{0,10},{2,8},{4,14},{6,12},{8,2},{10,0},{12,6},{14,4},{1,11},{3,9}... | collective-permute-start | bytes 589832 | tf_op jit(solution)/shard_map/ppermute | solution.py:154
  60.6 27.9 %collective-permute-start.12 = (bf16[4,192,128]{2,1,0:T(8,128)(2,1)S(1)}, bf16[4,192,128]{2,1,0:T(8,128)(2,1)}, u32[]{:S(2)}, u32[]{:S(2)}) collective-permute-start(bf16[4,192,128]{2,1,0:T(8,128)(2,1)S(1)} %get-tuple-element.18), channel_id=1, source_target_pairs={{0,12},{2,14},{4,8},{6,10},{8,4},{10,6},{12,0},{14,2},{1,13},{3,15... | collective-permute-start | bytes 589832 | tf_op jit(solution)/shard_map/ppermute | solution.py:154
  66.5 4.5 %copy-start.8 = (bf16[4,192,128]{2,1,0:T(8,128)(2,1)}, bf16[4,192,128]{2,1,0:T(8,128)(2,1)S(1)}, u32[]{:S(2)}) copy-start(bf16[4,192,128]{2,1,0:T(8,128)(2,1)S(1)} %collective-permute-done.8) | copy-start | bytes 589828
  66.5 23.9 %collective-permute-start.13 = (bf16[4,192,128]{2,1,0:T(8,128)(2,1)S(1)}, bf16[4,192,128]{2,1,0:T(8,128)(2,1)}, u32[]{:S(2)}, u32[]{:S(2)}) collective-permute-start(bf16[4,192,128]{2,1,0:T(8,128)(2,1)S(1)} %get-tuple-element.19), channel_id=1, source_target_pairs={{0,14},{2,12},{4,10},{6,8},{8,6},{10,4},{12,2},{14,0},{1,15},{3,13... | collective-permute-start | bytes 589832 | tf_op jit(solution)/shard_map/ppermute | solution.py:154
  82.3 10.1 %copy-start = (bf16[1,4,192,128]{3,0,2,1:T(2,128)(2,1)S(1)}, bf16[1,4,192,128]{3,0,2,1:T(2,128)(2,1)}, u32[]{:S(2)}) copy-start(bf16[1,4,192,128]{3,0,2,1:T(2,128)(2,1)} %copy.34) | copy-start | bytes 589828
  87.4 22.7 %copy-start.1 = (bf16[1,4,192,128]{3,0,2,1:T(2,128)(2,1)S(1)}, bf16[1,4,192,128]{3,0,2,1:T(2,128)(2,1)}, u32[]{:S(2)}) copy-start(bf16[1,4,192,128]{3,0,2,1:T(2,128)(2,1)} %copy.36) | copy-start | bytes 589828
  90.4 28.5 %copy-start.2 = (bf16[1,4,192,128]{3,0,2,1:T(2,128)(2,1)S(1)}, bf16[1,4,192,128]{3,0,2,1:T(2,128)(2,1)}, u32[]{:S(2)}) copy-start(bf16[1,4,192,128]{3,0,2,1:T(2,128)(2,1)} %copy.37) | copy-start | bytes 589828
  101.2 26.7 %copy-start.3 = (bf16[1,4,192,128]{3,0,2,1:T(2,128)(2,1)S(1)}, bf16[1,4,192,128]{3,0,2,1:T(2,128)(2,1)}, u32[]{:S(2)}) copy-start(bf16[1,4,192,128]{3,0,2,1:T(2,128)(2,1)} %copy.38) | copy-start | bytes 589828
  110.1 26.7 %copy-start.4 = (bf16[1,4,192,128]{3,0,2,1:T(2,128)(2,1)S(1)}, bf16[1,4,192,128]{3,0,2,1:T(2,128)(2,1)}, u32[]{:S(2)}) copy-start(bf16[1,4,192,128]{3,0,2,1:T(2,128)(2,1)} %copy.39) | copy-start | bytes 589828
  118.9 26.7 %copy-start.5 = (bf16[1,4,192,128]{3,0,2,1:T(2,128)(2,1)S(1)}, bf16[1,4,192,128]{3,0,2,1:T(2,128)(2,1)}, u32[]{:S(2)}) copy-start(bf16[1,4,192,128]{3,0,2,1:T(2,128)(2,1)} %copy.40) | copy-start | bytes 589828

commit v2 on v1

--- a/solution.py
+++ b/solution.py
@@ -142,6 +142,43 @@
     )(scalars, start[None, :], *blocks)
 
 
+def unpack_kernel(count, copies, *refs):
+    scalars = refs[0]
+    ins = refs[1 : 1 + count]
+    outs = refs[1 + count : 5 + count]
+    heads, turned, done = refs[5 + count :]
+    me = scalars[0]
+    sends = []
+    for t in range(4):
+        for d in range(count):
+            heads[t, (me ^ d) // copies] = ins[d][t]
+        turned[t] = jnp.swapaxes(heads[t], 0, 1)
+        send = pltpu.make_async_copy(turned.at[t], outs[t], done.at[t])
+        send.start()
+        sends.append(send)
+    for send in sends:
+        send.wait()
+
+
+def unpack(blocks, me, head_count):
+    count = len(blocks)
+    kinds, shard_rows, head_size = blocks[0].shape
+    shape = (shard_rows, head_count, head_size)
+    return pl.pallas_call(
+        functools.partial(unpack_kernel, count, count // head_count),
+        out_shape=[jax.ShapeDtypeStruct(shape, blocks[0].dtype)] * kinds,
+        in_specs=[pl.BlockSpec(memory_space=pltpu.SMEM)]
+        + [pl.BlockSpec(memory_space=pltpu.VMEM)] * count,
+        out_specs=[pl.BlockSpec(memory_space=pl.ANY)] * kinds,
+        scratch_shapes=[
+            pltpu.VMEM((kinds, head_count, shard_rows, head_size), blocks[0].dtype),
+            pltpu.VMEM((kinds,) + shape, blocks[0].dtype),
+            pltpu.SemaphoreType.DMA((kinds,)),
+        ],
+        compiler_params=pltpu.CompilerParams(vmem_limit_bytes=40 << 20),
+    )(me[None].astype(jnp.int32), *blocks)
+
+
 def on_device(queries, key_vecs, value_vecs, out_grad, doc_ids):
     head_count = queries.shape[1]
     count = lax.axis_size("ctx")
@@ -161,10 +198,7 @@
         for d in range(count)
     ]
     returned = exchange(attend(exchange(mine), doc_ids, me))
-    whole = jnp.zeros_like(packed)
-    for d in range(count):
-        whole = lax.dynamic_update_index_in_dim(whole, returned[d], (me ^ d) // copies, 0)
-    return tuple(jnp.swapaxes(whole[:, t], 0, 1) for t in range(4))
+    return tuple(unpack(returned, me, head_count))
 
 
 def solution(mesh):

time: 157 us -> 91.4 us (0.58)
  local copies, waits for them, and re-layouts: 84.4 us -> 1.72 us
  waiting for transfers between devices: 26.7 us -> 48.5 us
  starting transfers between devices: 32.6 us -> 27.9 us
    dynamic_update_slice x8 -> x0, local copies, waits for them, and re-layouts: 70.6 us -> none  [on_device(): lax.dynamic_update_index_in_dim(whole, returned[d], (me ^ d) // copies, 0)]
    ppermute x14, waiting for transfers between devices: 26.7 us -> 48.5 us  [exchange(): got[d] = lax.ppermute(blocks[d], 'ctx', [(s, s ^ d) for s in range(count)])]
    broadcast_in_dim x9 -> x0, local copies, waits for them, and re-layouts: 10.9 us -> none  [the longest x8 10.7 us: on_device(): lax.dynamic_update_index_in_dim(whole, returned[d], (me ^ d) // copies, 0)]
    ppermute x14, starting transfers between devices: 32.6 us -> 27.9 us  [exchange(): got[d] = lax.ppermute(blocks[d], 'ctx', [(s, s ^ d) for s in range(count)])]
  transfers between devices with their start and end apart: 14 -> 14, of which waited for: 5 -> 7; matrix products, arithmetic and copies ran while one was open for 12% -> 1% of each run, Pallas kernels for 0% -> 0%
where the time goes in v2:
time: 91.4 us; the launch traced here: 91 us
  waiting for transfers between devices  48.5 us (53%)
  starting transfers between devices  27.9 us (31%)
  Pallas kernels  10.8 us (12%)
  local copies, waits for them, and re-layouts  1.72 us (2%)
  other arithmetic  1.27 us (1%)
    ppermute x14, waiting for transfers between devices, exchange(): got[d] = lax.ppermute(blocks[d], 'ctx', [(s, s ^ d) for s in range(count)])  48.5 us
    ppermute x14, starting transfers between devices, exchange(): got[d] = lax.ppermute(blocks[d], 'ctx', [(s, s ^ d) for s in range(count)])  27.9 us
    pallas_call x1, Pallas kernels, attend(): pl.pallas_call(functools.partial(attention_kernel, count, tile_most), out...  9.35 us
  transfers between devices with their start and end apart: 14, of which 7 were waited for; matrix products, arithmetic and copies ran while one was open for 1% of the time, Pallas kernels for 0%

profile of v2, /device:TPU:0, one launch (start us, length us, event | category | flops | bytes accessed | tf_op | source)
XLA Modules:
  0.0 91.0 jit_solution(10848306553564721126)
XLA Ops:
  0.7 1.3 %copy_bitcast_fusion = (bf16[8,1,192,128]{3,2,1,0:T(8,128)(2,1)S(1)}, bf16[8,1,192,128]{3,2,1,0:T(8,128)(2,1)S(1)}) fusion(bf16[192,8,128]{2,1,0:T(8,128)(2,1)} %param.8, bf16[192,8,128]{2,1,0:T(8,128)(2,1)} %param.7), kind=kLoop, calls=%fused_computation.2 | loop fusion | bytes 1572864 | tf_op jit(solution)/shard_map/stack | solution.py:195
  2.0 0.1 copy_bitcast_fusion.2
  2.2 0.2 pad_maximum_fusion
  2.4 0.2 dynamic-slice_bitcast_fusion
  2.6 3.0 %collective-permute-start = (bf16[4,192,128]{2,1,0:T(8,128)(2,1)S(1)}, bf16[4,192,128]{2,1,0:T(8,128)(2,1)S(1)}, u32[]{:S(2)}, u32[]{:S(2)}) collective-permute-start(bf16[4,192,128]{2,1,0:T(8,128)(2,1)S(1)} %get-tuple-element.26), channel_id=1, source_target_pairs={{0,2},{2,0},{4,6},{6,4},{8,10},{10,8},{12,14},{14,12},{1,3},{3,1},... | collective-permute-start | bytes 589832 | tf_op jit(solution)/shard_map/ppermute | solution.py:191
  5.6 1.6 %collective-permute-start.1 = (bf16[4,192,128]{2,1,0:T(8,128)(2,1)S(1)}, bf16[4,192,128]{2,1,0:T(8,128)(2,1)S(1)}, u32[]{:S(2)}, u32[]{:S(2)}) collective-permute-start(bf16[4,192,128]{2,1,0:T(8,128)(2,1)S(1)} %get-tuple-element.25), channel_id=1, source_target_pairs={{0,4},{2,6},{4,0},{6,2},{8,12},{10,14},{12,8},{14,10},{1,5},{3,7},... | collective-permute-start | bytes 589832 | tf_op jit(solution)/shard_map/ppermute | solution.py:191
  7.2 3.0 %collective-permute-start.3 = (bf16[4,192,128]{2,1,0:T(8,128)(2,1)S(1)}, bf16[4,192,128]{2,1,0:T(8,128)(2,1)S(1)}, u32[]{:S(2)}, u32[]{:S(2)}) collective-permute-start(bf16[4,192,128]{2,1,0:T(8,128)(2,1)S(1)} %get-tuple-element.23), channel_id=1, source_target_pairs={{0,8},{2,10},{4,12},{6,14},{8,0},{10,2},{12,4},{14,6},{1,9},{3,11}... | collective-permute-start | bytes 589832 | tf_op jit(solution)/shard_map/ppermute | solution.py:191
  10.2 1.3 %collective-permute-start.4 = (bf16[4,192,128]{2,1,0:T(8,128)(2,1)S(1)}, bf16[4,192,128]{2,1,0:T(8,128)(2,1)S(1)}, u32[]{:S(2)}, u32[]{:S(2)}) collective-permute-start(bf16[4,192,128]{2,1,0:T(8,128)(2,1)S(1)} %get-tuple-element.22), channel_id=1, source_target_pairs={{0,10},{2,8},{4,14},{6,12},{8,2},{10,0},{12,6},{14,4},{1,11},{3,9}... | collective-permute-start | bytes 589832 | tf_op jit(solution)/shard_map/ppermute | solution.py:191
  11.5 1.0 %convert_reduce_fusion = s32[1536]{0:T(1024)S(1)} fusion(s32[1536]{0:T(1024)S(1)} %copy-done.2), kind=kLoop, calls=%fused_computation | loop fusion | flops 7076352 | bytes 12288 | tf_op jit(solution)/shard_map/reduce_sum | solution.py:122
  12.5 3.7 %collective-permute-start.5 = (bf16[4,192,128]{2,1,0:T(8,128)(2,1)S(1)}, bf16[4,192,128]{2,1,0:T(8,128)(2,1)S(1)}, u32[]{:S(2)}, u32[]{:S(2)}) collective-permute-start(bf16[4,192,128]{2,1,0:T(8,128)(2,1)S(1)} %get-tuple-element.21), channel_id=1, source_target_pairs={{0,12},{2,14},{4,8},{6,10},{8,4},{10,6},{12,0},{14,2},{1,13},{3,15... | collective-permute-start | bytes 589832 | tf_op jit(solution)/shard_map/ppermute | solution.py:191
  16.2 4.9 %collective-permute-done.1.refs_4_ = bf16[4,192,128]{2,1,0:T(8,128)(2,1)S(1)} collective-permute-done((bf16[4,192,128]{2,1,0:T(8,128)(2,1)S(1)}, bf16[4,192,128]{2,1,0:T(8,128)(2,1)S(1)}, u32[]{:S(2)}, u32[]{:S(2)}) %collective-permute-start.1) | collective-permute-done | bytes 196640 | tf_op jit(solution)/shard_map/ppermute | solution.py:191
  21.1 0.8 collective-permute-start.6
  22.0 0.8 collective-permute-done.2.refs_5_
  22.8 15.5 %collective-permute-done.4.refs_7_ = bf16[4,192,128]{2,1,0:T(8,128)(2,1)S(1)} collective-permute-done((bf16[4,192,128]{2,1,0:T(8,128)(2,1)S(1)}, bf16[4,192,128]{2,1,0:T(8,128)(2,1)S(1)}, u32[]{:S(2)}, u32[]{:S(2)}) %collective-permute-start.4) | collective-permute-done | bytes 196640 | tf_op jit(solution)/shard_map/ppermute | solution.py:191
  38.3 9.3 %shard_map.84 = (bf16[4,192,128]{2,1,0:T(8,128)(2,1)S(1)}, bf16[4,192,128]{2,1,0:T(8,128)(2,1)S(1)}, bf16[4,192,128]{2,1,0:T(8,128)(2,1)S(1)}, bf16[4,192,128]{2...) custom-call(s32[7]{0:T(128)S(1)} %pad_add_fusion.refs_0_, ...), custom_call_target="tpu_custom_call" | custom-call | tf_op jit(solution)/shard_map/pallas_call | solution.py:125
  47.7 9.2 %collective-permute-start.10 = (bf16[4,192,128]{2,1,0:T(8,128)(2,1)S(1)}, bf16[4,192,128]{2,1,0:T(8,128)(2,1)S(1)}, u32[]{:S(2)}, u32[]{:S(2)}) collective-permute-start(bf16[4,192,128]{2,1,0:T(8,128)(2,1)S(1)} %get-tuple-element.16), channel_id=1, source_target_pairs={{0,8},{2,10},{4,12},{6,14},{8,0},{10,2},{12,4},{14,6},{1,9},{3,11}... | collective-permute-start | bytes 589832 | tf_op jit(solution)/shard_map/ppermute | solution.py:191
  56.9 0.5 collective-permute-start.12
  57.4 4.3 %collective-permute-start.13 = (bf16[4,192,128]{2,1,0:T(8,128)(2,1)S(1)}, bf16[4,192,128]{2,1,0:T(8,128)(2,1)S(1)}, u32[]{:S(2)}, u32[]{:S(2)}) collective-permute-start(bf16[4,192,128]{2,1,0:T(8,128)(2,1)S(1)} %get-tuple-element.19), channel_id=1, source_target_pairs={{0,14},{2,12},{4,10},{6,8},{8,6},{10,4},{12,2},{14,0},{1,15},{3,13... | collective-permute-start | bytes 589832 | tf_op jit(solution)/shard_map/ppermute | solution.py:191
  61.7 0.5 collective-permute-start.7
  62.2 14.8 %collective-permute-done.10.refs_5_ = bf16[4,192,128]{2,1,0:T(8,128)(2,1)S(1)} collective-permute-done((bf16[4,192,128]{2,1,0:T(8,128)(2,1)S(1)}, bf16[4,192,128]{2,1,0:T(8,128)(2,1)S(1)}, u32[]{:S(2)}, u32[]{:S(2)}) %collective-permute-start.10) | collective-permute-done | bytes 196640 | tf_op jit(solution)/shard_map/ppermute | solution.py:191
  77.0 4.8 %collective-permute-done.11.refs_6_ = bf16[4,192,128]{2,1,0:T(8,128)(2,1)S(1)} collective-permute-done((bf16[4,192,128]{2,1,0:T(8,128)(2,1)S(1)}, bf16[4,192,128]{2,1,0:T(8,128)(2,1)S(1)}, u32[]{:S(2)}, u32[]{:S(2)}) %collective-permute-start.11) | collective-permute-done | bytes 196640 | tf_op jit(solution)/shard_map/ppermute | solution.py:191
  81.8 3.6 %collective-permute-done.8.refs_3_ = bf16[4,192,128]{2,1,0:T(8,128)(2,1)S(1)} collective-permute-done((bf16[4,192,128]{2,1,0:T(8,128)(2,1)S(1)}, bf16[4,192,128]{2,1,0:T(8,128)(2,1)S(1)}, u32[]{:S(2)}, u32[]{:S(2)}) %collective-permute-start.8) | collective-permute-done | bytes 196640 | tf_op jit(solution)/shard_map/ppermute | solution.py:191
  85.4 4.1 %collective-permute-done.9.refs_4_ = bf16[4,192,128]{2,1,0:T(8,128)(2,1)S(1)} collective-permute-done((bf16[4,192,128]{2,1,0:T(8,128)(2,1)S(1)}, bf16[4,192,128]{2,1,0:T(8,128)(2,1)S(1)}, u32[]{:S(2)}, u32[]{:S(2)}) %collective-permute-start.9) | collective-permute-done | bytes 196640 | tf_op jit(solution)/shard_map/ppermute | solution.py:191
  89.5 1.4 %shard_map.85 = (bf16[192,8,128]{2,1,0:T(8,128)(2,1)}, bf16[192,8,128]{2,1,0:T(8,128)(2,1)}, bf16[192,8,128]{2,1,0:T(8,128)(2,1)}, bf16[192,8,128]{2,1,0:T(8,128)(2,1)}) custom-call(s32[1]{0:T(128)} %bitcast.refs_0_, bf16[4,192,128]{2,1,0:T(8,128)(2,1)S(1)} %get-tuple-element.12.refs_1_, bf16[4,192,128]{2,1,0:T(8,128)(2,1)S(1)} %collective-permute-done.7.refs_2_, ...), custom_call_target="tpu_custom_call" | custom-call | tf_op jit(solution)/shard_map/pallas_call | solution.py:167
  (21 shorter events, 0.2 us)
Async XLA Ops:
  0.6 1.4 %copy-start.1 = (bf16[192,8,128]{2,1,0:T(8,128)(2,1)S(1)}, bf16[192,8,128]{2,1,0:T(8,128)(2,1)}, u32[]{:S(2)}) copy-start(bf16[192,8,128]{2,1,0:T(8,128)(2,1)} %param.5) | copy-start | bytes 1179652
  0.6 1.4 %copy-start = (bf16[192,8,128]{2,1,0:T(8,128)(2,1)S(1)}, bf16[192,8,128]{2,1,0:T(8,128)(2,1)}, u32[]{:S(2)}) copy-start(bf16[192,8,128]{2,1,0:T(8,128)(2,1)} %param.6) | copy-start | bytes 1179652
  2.4 9.1 %copy-start.2 = (s32[1536]{0:T(1024)S(1)}, s32[1536]{0:T(1024)}, u32[]{:S(2)}) copy-start(s32[1536]{0:T(1024)} %param.9) | copy-start | bytes 18436
  2.6 10.0 %collective-permute-start = (bf16[4,192,128]{2,1,0:T(8,128)(2,1)S(1)}, bf16[4,192,128]{2,1,0:T(8,128)(2,1)S(1)}, u32[]{:S(2)}, u32[]{:S(2)}) collective-permute-start(bf16[4,192,128]{2,1,0:T(8,128)(2,1)S(1)} %get-tuple-element.26), channel_id=1, source_target_pairs={{0,2},{2,0},{4,6},{6,4},{8,10},{10,8},{12,14},{14,12},{1,3},{3,1},... | collective-permute-start | bytes 589832 | tf_op jit(solution)/shard_map/ppermute | solution.py:191
  5.6 15.5 %collective-permute-start.1 = (bf16[4,192,128]{2,1,0:T(8,128)(2,1)S(1)}, bf16[4,192,128]{2,1,0:T(8,128)(2,1)S(1)}, u32[]{:S(2)}, u32[]{:S(2)}) collective-permute-start(bf16[4,192,128]{2,1,0:T(8,128)(2,1)S(1)} %get-tuple-element.25), channel_id=1, source_target_pairs={{0,4},{2,6},{4,0},{6,2},{8,12},{10,14},{12,8},{14,10},{1,5},{3,7},... | collective-permute-start | bytes 589832 | tf_op jit(solution)/shard_map/ppermute | solution.py:191
  7.2 15.6 %collective-permute-start.2 = (bf16[4,192,128]{2,1,0:T(8,128)(2,1)S(1)}, bf16[4,192,128]{2,1,0:T(8,128)(2,1)S(1)}, u32[]{:S(2)}, u32[]{:S(2)}) collective-permute-start(bf16[4,192,128]{2,1,0:T(8,128)(2,1)S(1)} %get-tuple-element.24), channel_id=1, source_target_pairs={{0,6},{2,4},{4,2},{6,0},{8,14},{10,12},{12,10},{14,8},{1,7},{3,5},... | collective-permute-start | bytes 589832 | tf_op jit(solution)/shard_map/ppermute | solution.py:191
  7.2 15.6 %collective-permute-start.3 = (bf16[4,192,128]{2,1,0:T(8,128)(2,1)S(1)}, bf16[4,192,128]{2,1,0:T(8,128)(2,1)S(1)}, u32[]{:S(2)}, u32[]{:S(2)}) collective-permute-start(bf16[4,192,128]{2,1,0:T(8,128)(2,1)S(1)} %get-tuple-element.23), channel_id=1, source_target_pairs={{0,8},{2,10},{4,12},{6,14},{8,0},{10,2},{12,4},{14,6},{1,9},{3,11}... | collective-permute-start | bytes 589832 | tf_op jit(solution)/shard_map/ppermute | solution.py:191
  10.2 28.2 %collective-permute-start.4 = (bf16[4,192,128]{2,1,0:T(8,128)(2,1)S(1)}, bf16[4,192,128]{2,1,0:T(8,128)(2,1)S(1)}, u32[]{:S(2)}, u32[]{:S(2)}) collective-permute-start(bf16[4,192,128]{2,1,0:T(8,128)(2,1)S(1)} %get-tuple-element.22), channel_id=1, source_target_pairs={{0,10},{2,8},{4,14},{6,12},{8,2},{10,0},{12,6},{14,4},{1,11},{3,9}... | collective-permute-start | bytes 589832 | tf_op jit(solution)/shard_map/ppermute | solution.py:191
  12.5 25.8 %collective-permute-start.5 = (bf16[4,192,128]{2,1,0:T(8,128)(2,1)S(1)}, bf16[4,192,128]{2,1,0:T(8,128)(2,1)S(1)}, u32[]{:S(2)}, u32[]{:S(2)}) collective-permute-start(bf16[4,192,128]{2,1,0:T(8,128)(2,1)S(1)} %get-tuple-element.21), channel_id=1, source_target_pairs={{0,12},{2,14},{4,8},{6,10},{8,4},{10,6},{12,0},{14,2},{1,13},{3,15... | collective-permute-start | bytes 589832 | tf_op jit(solution)/shard_map/ppermute | solution.py:191
  21.1 17.3 %collective-permute-start.6 = (bf16[4,192,128]{2,1,0:T(8,128)(2,1)S(1)}, bf16[4,192,128]{2,1,0:T(8,128)(2,1)S(1)}, u32[]{:S(2)}, u32[]{:S(2)}) collective-permute-start(bf16[4,192,128]{2,1,0:T(8,128)(2,1)S(1)} %get-tuple-element.20), channel_id=1, source_target_pairs={{0,14},{2,12},{4,10},{6,8},{8,6},{10,4},{12,2},{14,0},{1,15},{3,13... | collective-permute-start | bytes 589832 | tf_op jit(solution)/shard_map/ppermute | solution.py:191
  47.7 29.3 %collective-permute-start.10 = (bf16[4,192,128]{2,1,0:T(8,128)(2,1)S(1)}, bf16[4,192,128]{2,1,0:T(8,128)(2,1)S(1)}, u32[]{:S(2)}, u32[]{:S(2)}) collective-permute-start(bf16[4,192,128]{2,1,0:T(8,128)(2,1)S(1)} %get-tuple-element.16), channel_id=1, source_target_pairs={{0,8},{2,10},{4,12},{6,14},{8,0},{10,2},{12,4},{14,6},{1,9},{3,11}... | collective-permute-start | bytes 589832 | tf_op jit(solution)/shard_map/ppermute | solution.py:191
  56.9 24.9 %collective-permute-start.11 = (bf16[4,192,128]{2,1,0:T(8,128)(2,1)S(1)}, bf16[4,192,128]{2,1,0:T(8,128)(2,1)S(1)}, u32[]{:S(2)}, u32[]{:S(2)}) collective-permute-start(bf16[4,192,128]{2,1,0:T(8,128)(2,1)S(1)} %get-tuple-element.17), channel_id=1, source_target_pairs={{0,10},{2,8},{4,14},{6,12},{8,2},{10,0},{12,6},{14,4},{1,11},{3,9}... | collective-permute-start | bytes 589832 | tf_op jit(solution)/shard_map/ppermute | solution.py:191
  56.9 24.8 %collective-permute-start.12 = (bf16[4,192,128]{2,1,0:T(8,128)(2,1)S(1)}, bf16[4,192,128]{2,1,0:T(8,128)(2,1)S(1)}, u32[]{:S(2)}, u32[]{:S(2)}) collective-permute-start(bf16[4,192,128]{2,1,0:T(8,128)(2,1)S(1)} %get-tuple-element.18), channel_id=1, source_target_pairs={{0,12},{2,14},{4,8},{6,10},{8,4},{10,6},{12,0},{14,2},{1,13},{3,15... | collective-permute-start | bytes 589832 | tf_op jit(solution)/shard_map/ppermute | solution.py:191
  57.4 24.3 %collective-permute-start.13 = (bf16[4,192,128]{2,1,0:T(8,128)(2,1)S(1)}, bf16[4,192,128]{2,1,0:T(8,128)(2,1)S(1)}, u32[]{:S(2)}, u32[]{:S(2)}) collective-permute-start(bf16[4,192,128]{2,1,0:T(8,128)(2,1)S(1)} %get-tuple-element.19), channel_id=1, source_target_pairs={{0,14},{2,12},{4,10},{6,8},{8,6},{10,4},{12,2},{14,0},{1,15},{3,13... | collective-permute-start | bytes 589832 | tf_op jit(solution)/shard_map/ppermute | solution.py:191
  61.7 20.1 %collective-permute-start.7 = (bf16[4,192,128]{2,1,0:T(8,128)(2,1)S(1)}, bf16[4,192,128]{2,1,0:T(8,128)(2,1)S(1)}, u32[]{:S(2)}, u32[]{:S(2)}) collective-permute-start(bf16[4,192,128]{2,1,0:T(8,128)(2,1)S(1)} %get-tuple-element.13), channel_id=1, source_target_pairs={{0,2},{2,0},{4,6},{6,4},{8,10},{10,8},{12,14},{14,12},{1,3},{3,1},... | collective-permute-start | bytes 589832 | tf_op jit(solution)/shard_map/ppermute | solution.py:191
  77.0 8.4 %collective-permute-start.8 = (bf16[4,192,128]{2,1,0:T(8,128)(2,1)S(1)}, bf16[4,192,128]{2,1,0:T(8,128)(2,1)S(1)}, u32[]{:S(2)}, u32[]{:S(2)}) collective-permute-start(bf16[4,192,128]{2,1,0:T(8,128)(2,1)S(1)} %get-tuple-element.14), channel_id=1, source_target_pairs={{0,4},{2,6},{4,0},{6,2},{8,12},{10,14},{12,8},{14,10},{1,5},{3,7},... | collective-permute-start | bytes 589832 | tf_op jit(solution)/shard_map/ppermute | solution.py:191
  81.7 7.8 %collective-permute-start.9 = (bf16[4,192,128]{2,1,0:T(8,128)(2,1)S(1)}, bf16[4,192,128]{2,1,0:T(8,128)(2,1)S(1)}, u32[]{:S(2)}, u32[]{:S(2)}) collective-permute-start(bf16[4,192,128]{2,1,0:T(8,128)(2,1)S(1)} %get-tuple-element.15), channel_id=1, source_target_pairs={{0,6},{2,4},{4,2},{6,0},{8,14},{10,12},{12,10},{14,8},{1,7},{3,5},... | collective-permute-start | bytes 589832 | tf_op jit(solution)/shard_map/ppermute | solution.py:191

commit v3 on v2

--- a/solution.py
+++ b/solution.py
@@ -12,8 +12,9 @@
 HIDDEN = -1e30
 
 
-def partner_order(count):
-    return sorted(range(1, count), key=lambda d: (-(d.bit_length()), -d))
+def partner_orders(count):
+    far, near = list(range(count - 1, count // 2 - 1, -1)), list(range(count // 2 - 1, 0, -1))
+    return (0, *far[:1], *near, *far[1:]), (0, *far[1:], *far[:1], *near)
 
 
 def nt_dot(a, b):
@@ -24,7 +25,8 @@
     return jnp.dot(a, b, preferred_element_type=jnp.float32)
 
 
-def attention_kernel(count, tile_most, *refs):
+def attention_kernel(order, tile_most, *refs):
+    count = len(order)
     scalars, start_ref = refs[0], refs[1]
     ins = refs[2 : 2 + count]
     outs = refs[2 + count : 2 + 2 * count]
@@ -38,13 +40,13 @@
     scaling = head_size ** (-0.5)
     exponent = scaling * math.log2(math.e)
 
-    for d in range(count):
+    for n, d in enumerate(order):
         shard = me ^ d
         low = pl.multiple_of(shard * half, half)
         high = pl.multiple_of((2 * count - 1 - shard) * half, half)
         for t in range(4):
-            rows[t, pl.ds(low, half), :] = ins[d][t, :half, :]
-            rows[t, pl.ds(high, half), :] = ins[d][t, half:, :]
+            rows[t, pl.ds(low, half), :] = ins[n][t, :half, :]
+            rows[t, pl.ds(high, half), :] = ins[n][t, half:, :]
     for b in range(tokens // tile):
         block = pl.ds(b * tile, tile)
         key_t[:, block] = rows[1, block, :].T
@@ -103,16 +105,16 @@
 
     result[2] = (key_sum[...] * scaling).astype(jnp.bfloat16)
     result[3] = value_sum[...].astype(jnp.bfloat16)
-    for d in range(count):
+    for n, d in enumerate(order):
         shard = me ^ d
         low = pl.multiple_of(shard * half, half)
         high = pl.multiple_of((2 * count - 1 - shard) * half, half)
         for t in range(4):
-            outs[d][t, :half, :] = result[t, pl.ds(low, half), :]
-            outs[d][t, half:, :] = result[t, pl.ds(high, half), :]
-
-
-def attend(blocks, doc_ids, me):
+            outs[n][t, :half, :] = result[t, pl.ds(low, half), :]
+            outs[n][t, half:, :] = result[t, pl.ds(high, half), :]
+
+
+def attend(blocks, order, doc_ids, me):
     count = len(blocks)
     tokens = doc_ids.shape[0]
     head_size = blocks[0].shape[2]
@@ -123,7 +125,7 @@
     scalars = jnp.concatenate([me[None], start[::TILE] // TILE]).astype(jnp.int32)
     span = tile_most * TILE
     return pl.pallas_call(
-        functools.partial(attention_kernel, count, tile_most),
+        functools.partial(attention_kernel, order, tile_most),
         out_shape=[jax.ShapeDtypeStruct(b.shape, b.dtype) for b in blocks],
         in_specs=[pl.BlockSpec(memory_space=pltpu.SMEM)]
         + [pl.BlockSpec(memory_space=pltpu.VMEM)] * (count + 1),
@@ -142,7 +144,44 @@
     )(scalars, start[None, :], *blocks)
 
 
-def unpack_kernel(count, copies, *refs):
+def pack_kernel(order, copies, *refs):
+    count = len(order)
+    scalars = refs[0]
+    ins = refs[1:5]
+    outs = refs[5 : 5 + count]
+    held, heads, done = refs[5 + count :]
+    me = scalars[0]
+    loads = [pltpu.make_async_copy(ins[t], held.at[t], done.at[t]) for t in range(4)]
+    for load in loads:
+        load.start()
+    for t in range(4):
+        loads[t].wait()
+        heads[t] = jnp.swapaxes(held[t], 0, 1)
+        for n, d in enumerate(order):
+            outs[n][t] = heads[t, (me ^ d) // copies]
+
+
+def pack(arrays, order, me):
+    count = len(order)
+    shard_rows, head_count, head_size = arrays[0].shape
+    kinds = len(arrays)
+    return pl.pallas_call(
+        functools.partial(pack_kernel, order, count // head_count),
+        out_shape=[jax.ShapeDtypeStruct((kinds, shard_rows, head_size), arrays[0].dtype)] * count,
+        in_specs=[pl.BlockSpec(memory_space=pltpu.SMEM)]
+        + [pl.BlockSpec(memory_space=pltpu.HBM)] * kinds,
+        out_specs=[pl.BlockSpec(memory_space=pltpu.VMEM)] * count,
+        scratch_shapes=[
+            pltpu.VMEM((kinds,) + arrays[0].shape, arrays[0].dtype),
+            pltpu.VMEM((kinds, head_count, shard_rows, head_size), arrays[0].dtype),
+            pltpu.SemaphoreType.DMA((kinds,)),
+        ],
+        compiler_params=pltpu.CompilerParams(vmem_limit_bytes=40 << 20),
+    )(me[None].astype(jnp.int32), *[pltpu.with_memory_space_constraint(a, pltpu.HBM) for a in arrays])
+
+
+def unpack_kernel(order, copies, *refs):
+    count = len(order)
     scalars = refs[0]
     ins = refs[1 : 1 + count]
     outs = refs[1 + count : 5 + count]
@@ -150,8 +189,8 @@
     me = scalars[0]
     sends = []
     for t in range(4):
-        for d in range(count):
-            heads[t, (me ^ d) // copies] = ins[d][t]
+        for n, d in enumerate(order):
+            heads[t, (me ^ d) // copies] = ins[n][t]
         turned[t] = jnp.swapaxes(heads[t], 0, 1)
         send = pltpu.make_async_copy(turned.at[t], outs[t], done.at[t])
         send.start()
@@ -160,16 +199,16 @@
         send.wait()
 
 
-def unpack(blocks, me, head_count):
+def unpack(blocks, order, me, head_count):
     count = len(blocks)
     kinds, shard_rows, head_size = blocks[0].shape
     shape = (shard_rows, head_count, head_size)
     return pl.pallas_call(
-        functools.partial(unpack_kernel, count, count // head_count),
+        functools.partial(unpack_kernel, order, count // head_count),
         out_shape=[jax.ShapeDtypeStruct(shape, blocks[0].dtype)] * kinds,
         in_specs=[pl.BlockSpec(memory_space=pltpu.SMEM)]
         + [pl.BlockSpec(memory_space=pltpu.VMEM)] * count,
-        out_specs=[pl.BlockSpec(memory_space=pl.ANY)] * kinds,
+        out_specs=[pl.BlockSpec(memory_space=pltpu.HBM)] * kinds,
         scratch_shapes=[
             pltpu.VMEM((kinds, head_count, shard_rows, head_size), blocks[0].dtype),
             pltpu.VMEM((kinds,) + shape, blocks[0].dtype),
@@ -183,22 +222,20 @@
     head_count = queries.shape[1]
     count = lax.axis_size("ctx")
     me = lax.axis_index("ctx")
-    copies = count // head_count
-
-    def exchange(blocks):
-        got = [blocks[0]] + [None] * (count - 1)
-        for d in partner_order(count):
+    order, back = partner_orders(count)
+
+    def exchange(blocks, order):
+        got = {0: blocks[0]}
+        for d in order[1:]:
             got[d] = lax.ppermute(blocks[d], "ctx", [(s, s ^ d) for s in range(count)])
         return got
 
     arrays = (queries, key_vecs, value_vecs, out_grad)
-    packed = jnp.stack([jnp.swapaxes(a, 0, 1) for a in arrays], 1)
-    mine = [
-        lax.dynamic_index_in_dim(packed, (me ^ d) // copies, 0, keepdims=False)
-        for d in range(count)
-    ]
-    returned = exchange(attend(exchange(mine), doc_ids, me))
-    return tuple(unpack(returned, me, head_count))
+    mine = dict(zip(order, pack(arrays, order, me)))
+    got = exchange(mine, order)
+    results = attend([got[d] for d in order], order, doc_ids, me)
+    returned = exchange(dict(zip(order, results)), back)
+    return tuple(unpack([returned[d] for d in back], back, me, head_count))
 
 
 def solution(mesh):

time: 91.4 us -> 85.9 us (0.940)
  waiting for transfers between devices: 48.5 us -> 32.6 us
  starting transfers between devices: 27.9 us -> 38.8 us
  Pallas kernels: 10.8 us -> 12.5 us
  local copies, waits for them, and re-layouts: 1.72 us -> 0.1 us
    ppermute x14, waiting for transfers between devices: 48.5 us -> 32.6 us  [exchange(): got[d] = lax.ppermute(blocks[d], 'ctx', [(s, s ^ d) for s in range(count)])]
    ppermute x14, starting transfers between devices: 27.9 us -> 38.8 us  [exchange(): got[d] = lax.ppermute(blocks[d], 'ctx', [(s, s ^ d) for s in range(count)])]
    pallas_call x2 -> x3, Pallas kernels: 10.8 us -> 12.5 us  [the longest x1 9.38 us: attend(): pl.pallas_call(functools.partial(attention_kernel, order, tile_most), out...]
    another operation x2 -> x0, local copies, waits for them, and re-layouts: 1.46 us -> none  [on_device(): packed = jnp.stack([jnp.swapaxes(a, 0, 1) for a in arrays], 1)]
  transfers between devices with their start and end apart: 14 -> 14, of which waited for: 7 -> 10; matrix products, arithmetic and copies ran while one was open for 1% -> 1% of each run, Pallas kernels for 0% -> 0%
where the time goes in v3:
time: 85.9 us; the launch traced here: 85.8 us
  starting transfers between devices  38.8 us (45%)
  waiting for transfers between devices  32.6 us (38%)
  Pallas kernels  12.5 us (15%)
  other arithmetic  1.07 us (1%)
    ppermute x14, starting transfers between devices, exchange(): got[d] = lax.ppermute(blocks[d], 'ctx', [(s, s ^ d) for s in range(count)])  38.8 us
    ppermute x14, waiting for transfers between devices, exchange(): got[d] = lax.ppermute(blocks[d], 'ctx', [(s, s ^ d) for s in range(count)])  32.6 us
    pallas_call x1, Pallas kernels, attend(): pl.pallas_call(functools.partial(attention_kernel, order, tile_most), out...  9.38 us
  transfers between devices with their start and end apart: 14, of which 10 were waited for; matrix products, arithmetic and copies ran while one was open for 1% of the time, Pallas kernels for 0%

profile of v3, /device:TPU:0, one launch (start us, length us, event | category | flops | bytes accessed | tf_op | source)
XLA Modules:
  0.0 85.8 jit_solution(17363622726775282144)
XLA Ops:
  0.6 1.7 %shard_map.84 = (bf16[4,192,128]{2,1,0:T(8,128)(2,1)S(1)}, bf16[4,192,128]{2,1,0:T(8,128)(2,1)S(1)}, bf16[4,192,128]{2,1,0:T(8,128)(2,1)S(1)}, bf16[4,192,128]{2...) custom-call(s32[1]{0:T(128)} %bitcast.refs_0_, ...), custom_call_target="tpu_custom_call" | custom-call | tf_op jit(solution)/shard_map/pallas_call | solution.py:168
  2.3 6.1 %collective-permute-start = (bf16[4,192,128]{2,1,0:T(8,128)(2,1)S(1)}, bf16[4,192,128]{2,1,0:T(8,128)(2,1)S(1)}, u32[]{:S(2)}, u32[]{:S(2)}) collective-permute-start(bf16[4,192,128]{2,1,0:T(8,128)(2,1)S(1)} %get-tuple-element.21), channel_id=1, source_target_pairs={{0,14},{2,12},{4,10},{6,8},{8,6},{10,4},{12,2},{14,0},{1,15},{3,13... | collective-permute-start | bytes 589832 | tf_op jit(solution)/shard_map/ppermute | solution.py:230
  8.4 2.0 %collective-permute-start.2 = (bf16[4,192,128]{2,1,0:T(8,128)(2,1)S(1)}, bf16[4,192,128]{2,1,0:T(8,128)(2,1)S(1)}, u32[]{:S(2)}, u32[]{:S(2)}) collective-permute-start(bf16[4,192,128]{2,1,0:T(8,128)(2,1)S(1)} %get-tuple-element.23), channel_id=1, source_target_pairs={{0,4},{2,6},{4,0},{6,2},{8,12},{10,14},{12,8},{14,10},{1,5},{3,7},... | collective-permute-start | bytes 589832 | tf_op jit(solution)/shard_map/ppermute | solution.py:230
  10.4 1.5 %collective-permute-start.3 = (bf16[4,192,128]{2,1,0:T(8,128)(2,1)S(1)}, bf16[4,192,128]{2,1,0:T(8,128)(2,1)S(1)}, u32[]{:S(2)}, u32[]{:S(2)}) collective-permute-start(bf16[4,192,128]{2,1,0:T(8,128)(2,1)S(1)} %get-tuple-element.24), channel_id=1, source_target_pairs={{0,2},{2,0},{4,6},{6,4},{8,10},{10,8},{12,14},{14,12},{1,3},{3,1},... | collective-permute-start | bytes 589832 | tf_op jit(solution)/shard_map/ppermute | solution.py:230
  11.9 0.2 collective-permute-start.4
  12.1 1.0 %convert_reduce_fusion = s32[1536]{0:T(1024)S(1)} fusion(s32[1536]{0:T(1024)S(1)} %copy-done), kind=kLoop, calls=%fused_computation | loop fusion | flops 7076352 | bytes 12288 | tf_op jit(solution)/shard_map/reduce_sum | solution.py:124
  13.2 1.0 %collective-permute-done.refs_3_ = bf16[4,192,128]{2,1,0:T(8,128)(2,1)S(1)} collective-permute-done((bf16[4,192,128]{2,1,0:T(8,128)(2,1)S(1)}, bf16[4,192,128]{2,1,0:T(8,128)(2,1)S(1)}, u32[]{:S(2)}, u32[]{:S(2)}) %collective-permute-start) | collective-permute-done | bytes 196640 | tf_op jit(solution)/shard_map/ppermute | solution.py:230
  14.2 6.8 %collective-permute-start.5 = (bf16[4,192,128]{2,1,0:T(8,128)(2,1)S(1)}, bf16[4,192,128]{2,1,0:T(8,128)(2,1)S(1)}, u32[]{:S(2)}, u32[]{:S(2)}) collective-permute-start(bf16[4,192,128]{2,1,0:T(8,128)(2,1)S(1)} %get-tuple-element.26), channel_id=1, source_target_pairs={{0,10},{2,8},{4,14},{6,12},{8,2},{10,0},{12,6},{14,4},{1,11},{3,9}... | collective-permute-start | bytes 589832 | tf_op jit(solution)/shard_map/ppermute | solution.py:230
  21.2 5.6 %collective-permute-done.2.refs_5_ = bf16[4,192,128]{2,1,0:T(8,128)(2,1)S(1)} collective-permute-done((bf16[4,192,128]{2,1,0:T(8,128)(2,1)S(1)}, bf16[4,192,128]{2,1,0:T(8,128)(2,1)S(1)}, u32[]{:S(2)}, u32[]{:S(2)}) %collective-permute-start.2) | collective-permute-done | bytes 196640 | tf_op jit(solution)/shard_map/ppermute | solution.py:230
  26.8 1.0 %collective-permute-done.4.refs_7_ = bf16[4,192,128]{2,1,0:T(8,128)(2,1)S(1)} collective-permute-done((bf16[4,192,128]{2,1,0:T(8,128)(2,1)S(1)}, bf16[4,192,128]{2,1,0:T(8,128)(2,1)S(1)}, u32[]{:S(2)}, u32[]{:S(2)}) %collective-permute-start.4) | collective-permute-done | bytes 196640 | tf_op jit(solution)/shard_map/ppermute | solution.py:230
  27.8 11.3 %collective-permute-done.5.refs_8_ = bf16[4,192,128]{2,1,0:T(8,128)(2,1)S(1)} collective-permute-done((bf16[4,192,128]{2,1,0:T(8,128)(2,1)S(1)}, bf16[4,192,128]{2,1,0:T(8,128)(2,1)S(1)}, u32[]{:S(2)}, u32[]{:S(2)}) %collective-permute-start.5) | collective-permute-done | bytes 196640 | tf_op jit(solution)/shard_map/ppermute | solution.py:230
  39.1 3.1 %collective-permute-done.6.refs_9_ = bf16[4,192,128]{2,1,0:T(8,128)(2,1)S(1)} collective-permute-done((bf16[4,192,128]{2,1,0:T(8,128)(2,1)S(1)}, bf16[4,192,128]{2,1,0:T(8,128)(2,1)S(1)}, u32[]{:S(2)}, u32[]{:S(2)}) %collective-permute-start.6) | collective-permute-done | bytes 196640 | tf_op jit(solution)/shard_map/ppermute | solution.py:230
  42.2 9.4 %shard_map.85 = (bf16[4,192,128]{2,1,0:T(8,128)(2,1)S(1)}, bf16[4,192,128]{2,1,0:T(8,128)(2,1)S(1)}, bf16[4,192,128]{2,1,0:T(8,128)(2,1)S(1)}, bf16[4,192,128]{2...) custom-call(s32[7]{0:T(128)S(1)} %pad_add_fusion.refs_0_, ...), custom_call_target="tpu_custom_call" | custom-call | tf_op jit(solution)/shard_map/pallas_call | solution.py:127
  51.6 2.3 %collective-permute-start.7 = (bf16[4,192,128]{2,1,0:T(8,128)(2,1)S(1)}, bf16[4,192,128]{2,1,0:T(8,128)(2,1)S(1)}, u32[]{:S(2)}, u32[]{:S(2)}) collective-permute-start(bf16[4,192,128]{2,1,0:T(8,128)(2,1)S(1)} %get-tuple-element.29), channel_id=1, source_target_pairs={{0,12},{2,14},{4,8},{6,10},{8,4},{10,6},{12,0},{14,2},{1,13},{3,15... | collective-permute-start | bytes 589832 | tf_op jit(solution)/shard_map/ppermute | solution.py:230
  53.9 2.9 %collective-permute-start.9 = (bf16[4,192,128]{2,1,0:T(8,128)(2,1)S(1)}, bf16[4,192,128]{2,1,0:T(8,128)(2,1)S(1)}, u32[]{:S(2)}, u32[]{:S(2)}) collective-permute-start(bf16[4,192,128]{2,1,0:T(8,128)(2,1)S(1)} %get-tuple-element.31), channel_id=1, source_target_pairs={{0,8},{2,10},{4,12},{6,14},{8,0},{10,2},{12,4},{14,6},{1,9},{3,11}... | collective-permute-start | bytes 589832 | tf_op jit(solution)/shard_map/ppermute | solution.py:230
  56.8 2.5 %collective-permute-start.10 = (bf16[4,192,128]{2,1,0:T(8,128)(2,1)S(1)}, bf16[4,192,128]{2,1,0:T(8,128)(2,1)S(1)}, u32[]{:S(2)}, u32[]{:S(2)}) collective-permute-start(bf16[4,192,128]{2,1,0:T(8,128)(2,1)S(1)} %get-tuple-element.32), channel_id=1, source_target_pairs={{0,14},{2,12},{4,10},{6,8},{8,6},{10,4},{12,2},{14,0},{1,15},{3,13... | collective-permute-start | bytes 589832 | tf_op jit(solution)/shard_map/ppermute | solution.py:230
  59.3 2.0 %collective-permute-done.7.refs_2_ = bf16[4,192,128]{2,1,0:T(8,128)(2,1)S(1)} collective-permute-done((bf16[4,192,128]{2,1,0:T(8,128)(2,1)S(1)}, bf16[4,192,128]{2,1,0:T(8,128)(2,1)S(1)}, u32[]{:S(2)}, u32[]{:S(2)}) %collective-permute-start.7) | collective-permute-done | bytes 196640 | tf_op jit(solution)/shard_map/ppermute | solution.py:230
  61.4 13.3 %collective-permute-start.12 = (bf16[4,192,128]{2,1,0:T(8,128)(2,1)S(1)}, bf16[4,192,128]{2,1,0:T(8,128)(2,1)S(1)}, u32[]{:S(2)}, u32[]{:S(2)}) collective-permute-start(bf16[4,192,128]{2,1,0:T(8,128)(2,1)S(1)} %get-tuple-element.34), channel_id=1, source_target_pairs={{0,4},{2,6},{4,0},{6,2},{8,12},{10,14},{12,8},{14,10},{1,5},{3,7},... | collective-permute-start | bytes 589832 | tf_op jit(solution)/shard_map/ppermute | solution.py:230
  74.6 4.0 %collective-permute-done.8.refs_3_ = bf16[4,192,128]{2,1,0:T(8,128)(2,1)S(1)} collective-permute-done((bf16[4,192,128]{2,1,0:T(8,128)(2,1)S(1)}, bf16[4,192,128]{2,1,0:T(8,128)(2,1)S(1)}, u32[]{:S(2)}, u32[]{:S(2)}) %collective-permute-start.8) | collective-permute-done | bytes 196640 | tf_op jit(solution)/shard_map/ppermute | solution.py:230
  78.6 1.2 %collective-permute-start.13 = (bf16[4,192,128]{2,1,0:T(8,128)(2,1)S(1)}, bf16[4,192,128]{2,1,0:T(8,128)(2,1)S(1)}, u32[]{:S(2)}, u32[]{:S(2)}) collective-permute-start(bf16[4,192,128]{2,1,0:T(8,128)(2,1)S(1)} %get-tuple-element.35), channel_id=1, source_target_pairs={{0,2},{2,0},{4,6},{6,4},{8,10},{10,8},{12,14},{14,12},{1,3},{3,1},... | collective-permute-start | bytes 589832 | tf_op jit(solution)/shard_map/ppermute | solution.py:230
  79.8 2.7 %collective-permute-done.9.refs_4_ = bf16[4,192,128]{2,1,0:T(8,128)(2,1)S(1)} collective-permute-done((bf16[4,192,128]{2,1,0:T(8,128)(2,1)S(1)}, bf16[4,192,128]{2,1,0:T(8,128)(2,1)S(1)}, u32[]{:S(2)}, u32[]{:S(2)}) %collective-permute-start.9) | collective-permute-done | bytes 196640 | tf_op jit(solution)/shard_map/ppermute | solution.py:230
  82.5 1.2 %collective-permute-done.12.refs_7_ = bf16[4,192,128]{2,1,0:T(8,128)(2,1)S(1)} collective-permute-done((bf16[4,192,128]{2,1,0:T(8,128)(2,1)S(1)}, bf16[4,192,128]{2,1,0:T(8,128)(2,1)S(1)}, u32[]{:S(2)}, u32[]{:S(2)}) %collective-permute-start.12) | collective-permute-done | bytes 196640 | tf_op jit(solution)/shard_map/ppermute | solution.py:230
  83.7 0.6 collective-permute-done.13.refs_8_
  84.3 1.4 %shard_map.86 = (bf16[192,8,128]{2,1,0:T(8,128)(2,1)}, bf16[192,8,128]{2,1,0:T(8,128)(2,1)}, bf16[192,8,128]{2,1,0:T(8,128)(2,1)}, bf16[192,8,128]{2,1,0:T(8,128)(2,1)}) custom-call(s32[1]{0:T(128)} %bitcast.refs_0_, bf16[4,192,128]{2,1,0:T(8,128)(2,1)S(1)} %get-tuple-element.28.refs_1_, bf16[4,192,128]{2,1,0:T(8,128)(2,1)S(1)} %collective-permute-done.7.refs_2_, ...), custom_call_target="tpu_custom_call" | custom-call | tf_op jit(solution)/shard_map/pallas_call | solution.py:206
  (14 shorter events, 0.2 us)
Async XLA Ops:
  0.6 11.5 %copy-start = (s32[1536]{0:T(1024)S(1)}, s32[1536]{0:T(1024)}, u32[]{:S(2)}) copy-start(s32[1536]{0:T(1024)} %param.9) | copy-start | bytes 18436
  2.3 11.9 %collective-permute-start = (bf16[4,192,128]{2,1,0:T(8,128)(2,1)S(1)}, bf16[4,192,128]{2,1,0:T(8,128)(2,1)S(1)}, u32[]{:S(2)}, u32[]{:S(2)}) collective-permute-start(bf16[4,192,128]{2,1,0:T(8,128)(2,1)S(1)} %get-tuple-element.21), channel_id=1, source_target_pairs={{0,14},{2,12},{4,10},{6,8},{8,6},{10,4},{12,2},{14,0},{1,15},{3,13... | collective-permute-start | bytes 589832 | tf_op jit(solution)/shard_map/ppermute | solution.py:230
  8.4 12.7 %collective-permute-start.1 = (bf16[4,192,128]{2,1,0:T(8,128)(2,1)S(1)}, bf16[4,192,128]{2,1,0:T(8,128)(2,1)S(1)}, u32[]{:S(2)}, u32[]{:S(2)}) collective-permute-start(bf16[4,192,128]{2,1,0:T(8,128)(2,1)S(1)} %get-tuple-element.22), channel_id=1, source_target_pairs={{0,6},{2,4},{4,2},{6,0},{8,14},{10,12},{12,10},{14,8},{1,7},{3,5},... | collective-permute-start | bytes 589832 | tf_op jit(solution)/shard_map/ppermute | solution.py:230
  8.4 18.4 %collective-permute-start.2 = (bf16[4,192,128]{2,1,0:T(8,128)(2,1)S(1)}, bf16[4,192,128]{2,1,0:T(8,128)(2,1)S(1)}, u32[]{:S(2)}, u32[]{:S(2)}) collective-permute-start(bf16[4,192,128]{2,1,0:T(8,128)(2,1)S(1)} %get-tuple-element.23), channel_id=1, source_target_pairs={{0,4},{2,6},{4,0},{6,2},{8,12},{10,14},{12,8},{14,10},{1,5},{3,7},... | collective-permute-start | bytes 589832 | tf_op jit(solution)/shard_map/ppermute | solution.py:230
  10.4 16.4 %collective-permute-start.3 = (bf16[4,192,128]{2,1,0:T(8,128)(2,1)S(1)}, bf16[4,192,128]{2,1,0:T(8,128)(2,1)S(1)}, u32[]{:S(2)}, u32[]{:S(2)}) collective-permute-start(bf16[4,192,128]{2,1,0:T(8,128)(2,1)S(1)} %get-tuple-element.24), channel_id=1, source_target_pairs={{0,2},{2,0},{4,6},{6,4},{8,10},{10,8},{12,14},{14,12},{1,3},{3,1},... | collective-permute-start | bytes 589832 | tf_op jit(solution)/shard_map/ppermute | solution.py:230
  11.9 15.9 %collective-permute-start.4 = (bf16[4,192,128]{2,1,0:T(8,128)(2,1)S(1)}, bf16[4,192,128]{2,1,0:T(8,128)(2,1)S(1)}, u32[]{:S(2)}, u32[]{:S(2)}) collective-permute-start(bf16[4,192,128]{2,1,0:T(8,128)(2,1)S(1)} %get-tuple-element.25), channel_id=1, source_target_pairs={{0,12},{2,14},{4,8},{6,10},{8,4},{10,6},{12,0},{14,2},{1,13},{3,15... | collective-permute-start | bytes 589832 | tf_op jit(solution)/shard_map/ppermute | solution.py:230
  14.2 24.9 %collective-permute-start.5 = (bf16[4,192,128]{2,1,0:T(8,128)(2,1)S(1)}, bf16[4,192,128]{2,1,0:T(8,128)(2,1)S(1)}, u32[]{:S(2)}, u32[]{:S(2)}) collective-permute-start(bf16[4,192,128]{2,1,0:T(8,128)(2,1)S(1)} %get-tuple-element.26), channel_id=1, source_target_pairs={{0,10},{2,8},{4,14},{6,12},{8,2},{10,0},{12,6},{14,4},{1,11},{3,9}... | collective-permute-start | bytes 589832 | tf_op jit(solution)/shard_map/ppermute | solution.py:230
  21.1 21.1 %collective-permute-start.6 = (bf16[4,192,128]{2,1,0:T(8,128)(2,1)S(1)}, bf16[4,192,128]{2,1,0:T(8,128)(2,1)S(1)}, u32[]{:S(2)}, u32[]{:S(2)}) collective-permute-start(bf16[4,192,128]{2,1,0:T(8,128)(2,1)S(1)} %get-tuple-element.27), channel_id=1, source_target_pairs={{0,8},{2,10},{4,12},{6,14},{8,0},{10,2},{12,4},{14,6},{1,9},{3,11}... | collective-permute-start | bytes 589832 | tf_op jit(solution)/shard_map/ppermute | solution.py:230
  51.6 9.8 %collective-permute-start.7 = (bf16[4,192,128]{2,1,0:T(8,128)(2,1)S(1)}, bf16[4,192,128]{2,1,0:T(8,128)(2,1)S(1)}, u32[]{:S(2)}, u32[]{:S(2)}) collective-permute-start(bf16[4,192,128]{2,1,0:T(8,128)(2,1)S(1)} %get-tuple-element.29), channel_id=1, source_target_pairs={{0,12},{2,14},{4,8},{6,10},{8,4},{10,6},{12,0},{14,2},{1,13},{3,15... | collective-permute-start | bytes 589832 | tf_op jit(solution)/shard_map/ppermute | solution.py:230
  53.9 24.7 %collective-permute-start.8 = (bf16[4,192,128]{2,1,0:T(8,128)(2,1)S(1)}, bf16[4,192,128]{2,1,0:T(8,128)(2,1)S(1)}, u32[]{:S(2)}, u32[]{:S(2)}) collective-permute-start(bf16[4,192,128]{2,1,0:T(8,128)(2,1)S(1)} %get-tuple-element.30), channel_id=1, source_target_pairs={{0,10},{2,8},{4,14},{6,12},{8,2},{10,0},{12,6},{14,4},{1,11},{3,9}... | collective-permute-start | bytes 589832 | tf_op jit(solution)/shard_map/ppermute | solution.py:230
  53.9 28.6 %collective-permute-start.9 = (bf16[4,192,128]{2,1,0:T(8,128)(2,1)S(1)}, bf16[4,192,128]{2,1,0:T(8,128)(2,1)S(1)}, u32[]{:S(2)}, u32[]{:S(2)}) collective-permute-start(bf16[4,192,128]{2,1,0:T(8,128)(2,1)S(1)} %get-tuple-element.31), channel_id=1, source_target_pairs={{0,8},{2,10},{4,12},{6,14},{8,0},{10,2},{12,4},{14,6},{1,9},{3,11}... | collective-permute-start | bytes 589832 | tf_op jit(solution)/shard_map/ppermute | solution.py:230
  56.8 25.7 %collective-permute-start.10 = (bf16[4,192,128]{2,1,0:T(8,128)(2,1)S(1)}, bf16[4,192,128]{2,1,0:T(8,128)(2,1)S(1)}, u32[]{:S(2)}, u32[]{:S(2)}) collective-permute-start(bf16[4,192,128]{2,1,0:T(8,128)(2,1)S(1)} %get-tuple-element.32), channel_id=1, source_target_pairs={{0,14},{2,12},{4,10},{6,8},{8,6},{10,4},{12,2},{14,0},{1,15},{3,13... | collective-permute-start | bytes 589832 | tf_op jit(solution)/shard_map/ppermute | solution.py:230
  59.3 23.2 %collective-permute-start.11 = (bf16[4,192,128]{2,1,0:T(8,128)(2,1)S(1)}, bf16[4,192,128]{2,1,0:T(8,128)(2,1)S(1)}, u32[]{:S(2)}, u32[]{:S(2)}) collective-permute-start(bf16[4,192,128]{2,1,0:T(8,128)(2,1)S(1)} %get-tuple-element.33), channel_id=1, source_target_pairs={{0,6},{2,4},{4,2},{6,0},{8,14},{10,12},{12,10},{14,8},{1,7},{3,5},... | collective-permute-start | bytes 589832 | tf_op jit(solution)/shard_map/ppermute | solution.py:230
  61.4 22.3 %collective-permute-start.12 = (bf16[4,192,128]{2,1,0:T(8,128)(2,1)S(1)}, bf16[4,192,128]{2,1,0:T(8,128)(2,1)S(1)}, u32[]{:S(2)}, u32[]{:S(2)}) collective-permute-start(bf16[4,192,128]{2,1,0:T(8,128)(2,1)S(1)} %get-tuple-element.34), channel_id=1, source_target_pairs={{0,4},{2,6},{4,0},{6,2},{8,12},{10,14},{12,8},{14,10},{1,5},{3,7},... | collective-permute-start | bytes 589832 | tf_op jit(solution)/shard_map/ppermute | solution.py:230
  78.6 5.7 %collective-permute-start.13 = (bf16[4,192,128]{2,1,0:T(8,128)(2,1)S(1)}, bf16[4,192,128]{2,1,0:T(8,128)(2,1)S(1)}, u32[]{:S(2)}, u32[]{:S(2)}) collective-permute-start(bf16[4,192,128]{2,1,0:T(8,128)(2,1)S(1)} %get-tuple-element.35), channel_id=1, source_target_pairs={{0,2},{2,0},{4,6},{6,4},{8,10},{10,8},{12,14},{14,12},{1,3},{3,1},... | collective-permute-start | bytes 589832 | tf_op jit(solution)/shard_map/ppermute | solution.py:230

commit v4 on v3

--- a/solution.py
+++ b/solution.py
@@ -14,7 +14,9 @@
 
 def partner_orders(count):
     far, near = list(range(count - 1, count // 2 - 1, -1)), list(range(count // 2 - 1, 0, -1))
-    return (0, *far[:1], *near, *far[1:]), (0, *far[1:], *far[:1], *near)
+    turns = [d for pair in zip(far, near) for d in pair] + far[-1:]
+    back = near + far
+    return (0, *turns), (0, *back[count // 2 :], *back[: count // 2])
 
 
 def nt_dot(a, b):
@@ -30,7 +32,7 @@
     scalars, start_ref = refs[0], refs[1]
     ins = refs[2 : 2 + count]
     outs = refs[2 + count : 2 + 2 * count]
-    rows, key_t, value_t, scores, weights, key_sum, value_sum, result = refs[2 + 2 * count :]
+    rows, key_t, value_t, scores, weights, dweights, key_sum, value_sum, result = refs[2 + 2 * count :]
     me = scalars[0]
     shard_rows = ins[0].shape[1]
     half = shard_rows // 2
@@ -54,57 +56,79 @@
     key_sum[...] = jnp.zeros_like(key_sum)
     value_sum[...] = jnp.zeros_like(value_sum)
 
+    wide = 2 * tile
+
     def query_tile(size, j):
-        q_at = pl.multiple_of(j * tile, tile)
-        k_at = pl.multiple_of((j - (size - 1)) * tile, tile)
-        q_blk = rows[0, pl.ds(q_at, tile), :]
-        start = start_ref[:, pl.ds(q_at, tile)]
-        best = jnp.full((1, tile), HIDDEN, jnp.float32)
-        for i in range(size):
-            s = nt_dot(rows[1, pl.ds(k_at + i * tile, tile), :], q_blk) * exponent
-            k_pos = lax.broadcasted_iota(jnp.int32, (tile, tile), 0) + (k_at + i * tile)
-            seen = k_pos >= start
-            if i == size - 1:
-                q_pos = lax.broadcasted_iota(jnp.int32, (tile, tile), 1) + q_at
+        q_at = j * wide
+        k_at = q_at + wide - size * tile
+        q_blk = rows[0, pl.ds(q_at, wide), :]
+        start = start_ref[:, pl.ds(q_at, wide)]
+        query_tb = q_blk.T
+
+        def cols(i):
+            return slice(tile, wide) if i == size - 1 else slice(0, wide)
+
+        best = jnp.full((1, wide), HIDDEN, jnp.float32)
+        for i in range(size):
+            c = cols(i)
+            n = c.stop - c.start
+            s = dot(rows[1, pl.ds(k_at + i * tile, tile), :], query_tb[:, c]) * exponent
+            k_pos = lax.broadcasted_iota(jnp.int32, (tile, n), 0) + (k_at + i * tile)
+            seen = k_pos >= start[:, c]
+            if i >= size - 2:
+                q_pos = lax.broadcasted_iota(jnp.int32, (tile, n), 1) + (q_at + c.start)
                 seen = seen & (k_pos <= q_pos)
             s = jnp.where(seen, s, HIDDEN)
-            scores[i * tile : (i + 1) * tile, :] = s
-            best = jnp.maximum(best, jnp.max(s, axis=0, keepdims=True))
-        total = jnp.zeros((1, tile), jnp.float32)
-        for i in range(size):
-            e = jnp.exp2(scores[i * tile : (i + 1) * tile, :] - best)
-            total = total + jnp.sum(e, axis=0, keepdims=True)
-            weights[i * tile : (i + 1) * tile, :] = e.astype(jnp.bfloat16)
+            scores[i * tile : (i + 1) * tile, c] = s
+            top = jnp.max(s, axis=0, keepdims=True)
+            if i == size - 1:
+                best = jnp.concatenate([best[:, :tile], jnp.maximum(best[:, tile:], top)], 1)
+            else:
+                best = jnp.maximum(best, top)
+        total = jnp.zeros((1, wide), jnp.float32)
+        for i in range(size):
+            c = cols(i)
+            e = jnp.exp2(scores[i * tile : (i + 1) * tile, c] - best[:, c])
+            part = jnp.sum(e, axis=0, keepdims=True)
+            if i == size - 1:
+                total = jnp.concatenate([total[:, :tile], total[:, tile:] + part], 1)
+            else:
+                total = total + part
+            weights[i * tile : (i + 1) * tile, c] = e.astype(jnp.bfloat16)
         inverse = 1.0 / total
-        out_t = dot(value_t[:, pl.ds(k_at, size * tile)], weights[: size * tile, :]) * inverse
+        body = size - 1
+        out_t = dot(value_t[:, pl.ds(k_at, body * tile)], weights[: body * tile, :])
+        last = dot(value_t[:, pl.ds(k_at + body * tile, tile)], weights[body * tile : size * tile, tile:])
+        out_t = jnp.concatenate([out_t[:, :tile], out_t[:, tile:] + last], 1) * inverse
         out = out_t.astype(jnp.bfloat16)
-        result[0, pl.ds(q_at, tile), :] = out_t.T.astype(jnp.bfloat16)
-        grad_t = rows[3, pl.ds(q_at, tile), :].astype(jnp.float32).T * inverse
+        result[0, pl.ds(q_at, wide), :] = out_t.T.astype(jnp.bfloat16)
+        grad_t = rows[3, pl.ds(q_at, wide), :].astype(jnp.float32).T * inverse
         delta = jnp.sum(grad_t * out.astype(jnp.float32), axis=0, keepdims=True)
         grad_tb = grad_t.astype(jnp.bfloat16)
-        grad = grad_t.T.astype(jnp.bfloat16)
-        query_t = jnp.zeros((head_size, tile), jnp.float32)
-        for i in range(size):
+        for i in range(size):
+            c = cols(i)
             keys = pl.ds(k_at + i * tile, tile)
-            e = weights[i * tile : (i + 1) * tile, :]
-            value_sum[keys, :] += dot(e, grad)
-            dprobs = dot(rows[2, keys, :], grad_tb)
-            ds = (e.astype(jnp.float32) * (dprobs - delta)).astype(jnp.bfloat16)
-            key_sum[keys, :] += dot(ds, q_blk)
-            query_t = query_t + dot(key_t[:, keys], ds)
-        result[1, pl.ds(q_at, tile), :] = (query_t * scaling).T.astype(jnp.bfloat16)
-
-    @pl.loop(0, tokens // tile)
-    def _(j):
-        size = j - scalars[1 + j] + 1
-        for n in range(1, tile_most + 1):
-
-            @pl.when(size == n)
-            def _(n=n):
-                query_tile(n, j)
-
-    result[2] = (key_sum[...] * scaling).astype(jnp.bfloat16)
-    result[3] = value_sum[...].astype(jnp.bfloat16)
+            e = weights[i * tile : (i + 1) * tile, c]
+            value_sum[:, keys] += nt_dot(grad_tb[:, c], e)
+            dprobs = dot(rows[2, keys, :], grad_tb[:, c])
+            ds = (e.astype(jnp.float32) * (dprobs - delta[:, c])).astype(jnp.bfloat16)
+            dweights[i * tile : (i + 1) * tile, c] = ds
+        for i in range(size):
+            c = cols(i)
+            keys = pl.ds(k_at + i * tile, tile)
+            key_sum[:, keys] += nt_dot(query_tb[:, c], dweights[i * tile : (i + 1) * tile, c])
+        query_t = dot(key_t[:, pl.ds(k_at, body * tile)], dweights[: body * tile, :])
+        last = dot(key_t[:, pl.ds(k_at + body * tile, tile)], dweights[body * tile : size * tile, tile:])
+        query_t = jnp.concatenate([query_t[:, :tile], query_t[:, tile:] + last], 1)
+        result[1, pl.ds(q_at, wide), :] = (query_t * scaling).T.astype(jnp.bfloat16)
+
+    for j in range(tokens // wide):
+        query_tile(min(2 * j + 2, tile_most), j)
+
+    for b in range(tokens // tile):
+        block = pl.ds(b * tile, tile)
+        result[2, block, :] = (key_sum[:, block] * scaling).T.astype(jnp.bfloat16)
+        result[3, block, :] = value_sum[:, block].T.astype(jnp.bfloat16)
     for n, d in enumerate(order):
         shard = me ^ d
         low = pl.multiple_of(shard * half, half)
@@ -120,9 +144,9 @@
     head_size = blocks[0].shape[2]
     tiles = tokens // TILE
     longest = tokens * 5 // 8
-    tile_most = min(tiles, 1 + -(-(longest - 1) // TILE))
+    tile_most = min(tiles, 2 + -(-(longest - 1) // TILE))
     start = jnp.sum((doc_ids[:, None] < doc_ids[None, :]).astype(jnp.int32), axis=0)
-    scalars = jnp.concatenate([me[None], start[::TILE] // TILE]).astype(jnp.int32)
+    scalars = me[None].astype(jnp.int32)
     span = tile_most * TILE
     return pl.pallas_call(
         functools.partial(attention_kernel, order, tile_most),
@@ -134,10 +158,11 @@
             pltpu.VMEM((4, tokens, head_size), jnp.bfloat16),
             pltpu.VMEM((head_size, tokens), jnp.bfloat16),
             pltpu.VMEM((head_size, tokens), jnp.bfloat16),
-            pltpu.VMEM((span, TILE), jnp.float32),
-            pltpu.VMEM((span, TILE), jnp.bfloat16),
-            pltpu.VMEM((tokens, head_size), jnp.float32),
-            pltpu.VMEM((tokens, head_size), jnp.float32),
+            pltpu.VMEM((span, 2 * TILE), jnp.float32),
+            pltpu.VMEM((span, 2 * TILE), jnp.bfloat16),
+            pltpu.VMEM((span, 2 * TILE), jnp.bfloat16),
+            pltpu.VMEM((head_size, tokens), jnp.float32),
+            pltpu.VMEM((head_size, tokens), jnp.float32),
             pltpu.VMEM((4, tokens, head_size), jnp.bfloat16),
         ],
         compiler_params=pltpu.CompilerParams(vmem_limit_bytes=40 << 20),

time: 85.9 us -> 80.9 us (0.942)
  starting transfers between devices: 38.8 us -> 26 us
  waiting for transfers between devices: 32.6 us -> 43.8 us
  Pallas kernels: 12.5 us -> 8.54 us
    ppermute x14, starting transfers between devices: 38.8 us -> 26 us  [exchange(): got[d] = lax.ppermute(blocks[d], 'ctx', [(s, s ^ d) for s in range(count)])]
    ppermute x14, waiting for transfers between devices: 32.6 us -> 43.8 us  [exchange(): got[d] = lax.ppermute(blocks[d], 'ctx', [(s, s ^ d) for s in range(count)])]
    pallas_call x1, Pallas kernels: 9.38 us -> 5.42 us  [attend(): pl.pallas_call(functools.partial(attention_kernel, order, tile_most), out...]
where the time goes in v4:
time: 80.9 us; the launch traced here: 80.1 us
  waiting for transfers between devices  43.8 us (54%)
  starting transfers between devices  26 us (32%)
  Pallas kernels  8.54 us (11%)
  other arithmetic  0.99 us (1%)
    ppermute x14, waiting for transfers between devices, exchange(): got[d] = lax.ppermute(blocks[d], 'ctx', [(s, s ^ d) for s in range(count)])  43.8 us
    ppermute x14, starting transfers between devices, exchange(): got[d] = lax.ppermute(blocks[d], 'ctx', [(s, s ^ d) for s in range(count)])  26 us
    pallas_call x1, Pallas kernels, attend(): pl.pallas_call(functools.partial(attention_kernel, order, tile_most), out...  5.42 us
    pallas_call x1, Pallas kernels, pack(): pl.pallas_call(functools.partial(pack_kernel, order, count // head_count)...  1.68 us
  transfers between devices with their start and end apart: 14, of which 10 were waited for; matrix products, arithmetic and copies ran while one was open for 1% of the time, Pallas kernels for 0%

profile of v4, /device:TPU:0, one launch (start us, length us, event | category | flops | bytes accessed | tf_op | source)
XLA Modules:
  0.0 80.1 jit_solution(7797756014598561015)
XLA Ops:
  0.6 1.7 %shard_map.84 = (bf16[4,192,128]{2,1,0:T(8,128)(2,1)S(1)}, bf16[4,192,128]{2,1,0:T(8,128)(2,1)S(1)}, bf16[4,192,128]{2,1,0:T(8,128)(2,1)S(1)}, bf16[4,192,128]{2...) custom-call(s32[1]{0:T(128)} %bitcast.refs_0_, ...), custom_call_target="tpu_custom_call" | custom-call | tf_op jit(solution)/shard_map/pallas_call | solution.py:193
  2.3 6.1 %collective-permute-start = (bf16[4,192,128]{2,1,0:T(8,128)(2,1)S(1)}, bf16[4,192,128]{2,1,0:T(8,128)(2,1)S(1)}, u32[]{:S(2)}, u32[]{:S(2)}) collective-permute-start(bf16[4,192,128]{2,1,0:T(8,128)(2,1)S(1)} %get-tuple-element.21), channel_id=1, source_target_pairs={{0,14},{2,12},{4,10},{6,8},{8,6},{10,4},{12,2},{14,0},{1,15},{3,13... | collective-permute-start | bytes 589832 | tf_op jit(solution)/shard_map/ppermute | solution.py:255
  8.4 0.8 %collective-permute-start.2 = (bf16[4,192,128]{2,1,0:T(8,128)(2,1)S(1)}, bf16[4,192,128]{2,1,0:T(8,128)(2,1)S(1)}, u32[]{:S(2)}, u32[]{:S(2)}) collective-permute-start(bf16[4,192,128]{2,1,0:T(8,128)(2,1)S(1)} %get-tuple-element.23), channel_id=1, source_target_pairs={{0,12},{2,14},{4,8},{6,10},{8,4},{10,6},{12,0},{14,2},{1,13},{3,15... | collective-permute-start | bytes 589832 | tf_op jit(solution)/shard_map/ppermute | solution.py:255
  9.2 1.1 %collective-permute-start.3 = (bf16[4,192,128]{2,1,0:T(8,128)(2,1)S(1)}, bf16[4,192,128]{2,1,0:T(8,128)(2,1)S(1)}, u32[]{:S(2)}, u32[]{:S(2)}) collective-permute-start(bf16[4,192,128]{2,1,0:T(8,128)(2,1)S(1)} %get-tuple-element.24), channel_id=1, source_target_pairs={{0,4},{2,6},{4,0},{6,2},{8,12},{10,14},{12,8},{14,10},{1,5},{3,7},... | collective-permute-start | bytes 589832 | tf_op jit(solution)/shard_map/ppermute | solution.py:255
  10.4 2.9 %collective-permute-start.4 = (bf16[4,192,128]{2,1,0:T(8,128)(2,1)S(1)}, bf16[4,192,128]{2,1,0:T(8,128)(2,1)S(1)}, u32[]{:S(2)}, u32[]{:S(2)}) collective-permute-start(bf16[4,192,128]{2,1,0:T(8,128)(2,1)S(1)} %get-tuple-element.25), channel_id=1, source_target_pairs={{0,10},{2,8},{4,14},{6,12},{8,2},{10,0},{12,6},{14,4},{1,11},{3,9}... | collective-permute-start | bytes 589832 | tf_op jit(solution)/shard_map/ppermute | solution.py:255
  13.2 0.9 %collective-permute-done.refs_3_ = bf16[4,192,128]{2,1,0:T(8,128)(2,1)S(1)} collective-permute-done((bf16[4,192,128]{2,1,0:T(8,128)(2,1)S(1)}, bf16[4,192,128]{2,1,0:T(8,128)(2,1)S(1)}, u32[]{:S(2)}, u32[]{:S(2)}) %collective-permute-start) | collective-permute-done | bytes 196640 | tf_op jit(solution)/shard_map/ppermute | solution.py:255
  14.2 1.7 %collective-permute-start.5 = (bf16[4,192,128]{2,1,0:T(8,128)(2,1)S(1)}, bf16[4,192,128]{2,1,0:T(8,128)(2,1)S(1)}, u32[]{:S(2)}, u32[]{:S(2)}) collective-permute-start(bf16[4,192,128]{2,1,0:T(8,128)(2,1)S(1)} %get-tuple-element.26), channel_id=1, source_target_pairs={{0,2},{2,0},{4,6},{6,4},{8,10},{10,8},{12,14},{14,12},{1,3},{3,1},... | collective-permute-start | bytes 589832 | tf_op jit(solution)/shard_map/ppermute | solution.py:255
  15.8 3.3 %collective-permute-done.1.refs_4_ = bf16[4,192,128]{2,1,0:T(8,128)(2,1)S(1)} collective-permute-done((bf16[4,192,128]{2,1,0:T(8,128)(2,1)S(1)}, bf16[4,192,128]{2,1,0:T(8,128)(2,1)S(1)}, u32[]{:S(2)}, u32[]{:S(2)}) %collective-permute-start.1) | collective-permute-done | bytes 196640 | tf_op jit(solution)/shard_map/ppermute | solution.py:255
  19.2 2.4 %collective-permute-start.6 = (bf16[4,192,128]{2,1,0:T(8,128)(2,1)S(1)}, bf16[4,192,128]{2,1,0:T(8,128)(2,1)S(1)}, u32[]{:S(2)}, u32[]{:S(2)}) collective-permute-start(bf16[4,192,128]{2,1,0:T(8,128)(2,1)S(1)} %get-tuple-element.27), channel_id=1, source_target_pairs={{0,8},{2,10},{4,12},{6,14},{8,0},{10,2},{12,4},{14,6},{1,9},{3,11}... | collective-permute-start | bytes 589832 | tf_op jit(solution)/shard_map/ppermute | solution.py:255
  21.6 1.0 %convert_reduce_fusion = s32[1536]{0:T(1024)S(1)} fusion(s32[1536]{0:T(1024)S(1)} %copy-done), kind=kLoop, calls=%fused_computation | loop fusion | flops 7076352 | bytes 12288 | tf_op jit(solution)/shard_map/reduce_sum | solution.py:148
  22.6 0.8 %collective-permute-done.2.refs_5_ = bf16[4,192,128]{2,1,0:T(8,128)(2,1)S(1)} collective-permute-done((bf16[4,192,128]{2,1,0:T(8,128)(2,1)S(1)}, bf16[4,192,128]{2,1,0:T(8,128)(2,1)S(1)}, u32[]{:S(2)}, u32[]{:S(2)}) %collective-permute-start.2) | collective-permute-done | bytes 196640 | tf_op jit(solution)/shard_map/ppermute | solution.py:255
  23.4 4.2 %collective-permute-done.3.refs_6_ = bf16[4,192,128]{2,1,0:T(8,128)(2,1)S(1)} collective-permute-done((bf16[4,192,128]{2,1,0:T(8,128)(2,1)S(1)}, bf16[4,192,128]{2,1,0:T(8,128)(2,1)S(1)}, u32[]{:S(2)}, u32[]{:S(2)}) %collective-permute-start.3) | collective-permute-done | bytes 196640 | tf_op jit(solution)/shard_map/ppermute | solution.py:255
  27.7 11.2 %collective-permute-done.4.refs_7_ = bf16[4,192,128]{2,1,0:T(8,128)(2,1)S(1)} collective-permute-done((bf16[4,192,128]{2,1,0:T(8,128)(2,1)S(1)}, bf16[4,192,128]{2,1,0:T(8,128)(2,1)S(1)}, u32[]{:S(2)}, u32[]{:S(2)}) %collective-permute-start.4) | collective-permute-done | bytes 196640 | tf_op jit(solution)/shard_map/ppermute | solution.py:255
  38.9 3.2 %collective-permute-done.6.refs_9_ = bf16[4,192,128]{2,1,0:T(8,128)(2,1)S(1)} collective-permute-done((bf16[4,192,128]{2,1,0:T(8,128)(2,1)S(1)}, bf16[4,192,128]{2,1,0:T(8,128)(2,1)S(1)}, u32[]{:S(2)}, u32[]{:S(2)}) %collective-permute-start.6) | collective-permute-done | bytes 196640 | tf_op jit(solution)/shard_map/ppermute | solution.py:255
  42.1 5.4 %shard_map.85 = (bf16[4,192,128]{2,1,0:T(8,128)(2,1)S(1)}, bf16[4,192,128]{2,1,0:T(8,128)(2,1)S(1)}, bf16[4,192,128]{2,1,0:T(8,128)(2,1)S(1)}, bf16[4,192,128]{2...) custom-call(s32[1]{0:T(128)} %bitcast.refs_0_, ...), custom_call_target="tpu_custom_call" | custom-call | tf_op jit(solution)/shard_map/pallas_call | solution.py:151
  47.5 2.4 %collective-permute-start.7 = (bf16[4,192,128]{2,1,0:T(8,128)(2,1)S(1)}, bf16[4,192,128]{2,1,0:T(8,128)(2,1)S(1)}, u32[]{:S(2)}, u32[]{:S(2)}) collective-permute-start(bf16[4,192,128]{2,1,0:T(8,128)(2,1)S(1)} %get-tuple-element.29), channel_id=1, source_target_pairs={{0,12},{2,14},{4,8},{6,10},{8,4},{10,6},{12,0},{14,2},{1,13},{3,15... | collective-permute-start | bytes 589832 | tf_op jit(solution)/shard_map/ppermute | solution.py:255
  49.9 2.9 %collective-permute-start.9 = (bf16[4,192,128]{2,1,0:T(8,128)(2,1)S(1)}, bf16[4,192,128]{2,1,0:T(8,128)(2,1)S(1)}, u32[]{:S(2)}, u32[]{:S(2)}) collective-permute-start(bf16[4,192,128]{2,1,0:T(8,128)(2,1)S(1)} %get-tuple-element.31), channel_id=1, source_target_pairs={{0,8},{2,10},{4,12},{6,14},{8,0},{10,2},{12,4},{14,6},{1,9},{3,11}... | collective-permute-start | bytes 589832 | tf_op jit(solution)/shard_map/ppermute | solution.py:255
  52.9 2.9 %collective-permute-start.11 = (bf16[4,192,128]{2,1,0:T(8,128)(2,1)S(1)}, bf16[4,192,128]{2,1,0:T(8,128)(2,1)S(1)}, u32[]{:S(2)}, u32[]{:S(2)}) collective-permute-start(bf16[4,192,128]{2,1,0:T(8,128)(2,1)S(1)} %get-tuple-element.33), channel_id=1, source_target_pairs={{0,4},{2,6},{4,0},{6,2},{8,12},{10,14},{12,8},{14,10},{1,5},{3,7},... | collective-permute-start | bytes 589832 | tf_op jit(solution)/shard_map/ppermute | solution.py:255
  55.8 1.5 %collective-permute-done.7.refs_2_ = bf16[4,192,128]{2,1,0:T(8,128)(2,1)S(1)} collective-permute-done((bf16[4,192,128]{2,1,0:T(8,128)(2,1)S(1)}, bf16[4,192,128]{2,1,0:T(8,128)(2,1)S(1)}, u32[]{:S(2)}, u32[]{:S(2)}) %collective-permute-start.7) | collective-permute-done | bytes 196640 | tf_op jit(solution)/shard_map/ppermute | solution.py:255
  57.8 12.4 %collective-permute-done.8.refs_3_ = bf16[4,192,128]{2,1,0:T(8,128)(2,1)S(1)} collective-permute-done((bf16[4,192,128]{2,1,0:T(8,128)(2,1)S(1)}, bf16[4,192,128]{2,1,0:T(8,128)(2,1)S(1)}, u32[]{:S(2)}, u32[]{:S(2)}) %collective-permute-start.8) | collective-permute-done | bytes 196640 | tf_op jit(solution)/shard_map/ppermute | solution.py:255
  70.2 2.3 %collective-permute-start.13 = (bf16[4,192,128]{2,1,0:T(8,128)(2,1)S(1)}, bf16[4,192,128]{2,1,0:T(8,128)(2,1)S(1)}, u32[]{:S(2)}, u32[]{:S(2)}) collective-permute-start(bf16[4,192,128]{2,1,0:T(8,128)(2,1)S(1)} %get-tuple-element.35), channel_id=1, source_target_pairs={{0,14},{2,12},{4,10},{6,8},{8,6},{10,4},{12,2},{14,0},{1,15},{3,13... | collective-permute-start | bytes 589832 | tf_op jit(solution)/shard_map/ppermute | solution.py:255
  72.4 4.0 %collective-permute-done.9.refs_4_ = bf16[4,192,128]{2,1,0:T(8,128)(2,1)S(1)} collective-permute-done((bf16[4,192,128]{2,1,0:T(8,128)(2,1)S(1)}, bf16[4,192,128]{2,1,0:T(8,128)(2,1)S(1)}, u32[]{:S(2)}, u32[]{:S(2)}) %collective-permute-start.9) | collective-permute-done | bytes 196640 | tf_op jit(solution)/shard_map/ppermute | solution.py:255
  76.5 2.2 %collective-permute-done.13.refs_8_ = bf16[4,192,128]{2,1,0:T(8,128)(2,1)S(1)} collective-permute-done((bf16[4,192,128]{2,1,0:T(8,128)(2,1)S(1)}, bf16[4,192,128]{2,1,0:T(8,128)(2,1)S(1)}, u32[]{:S(2)}, u32[]{:S(2)}) %collective-permute-start.13) | collective-permute-done | bytes 196640 | tf_op jit(solution)/shard_map/ppermute | solution.py:255
  78.6 1.4 %shard_map.86 = (bf16[192,8,128]{2,1,0:T(8,128)(2,1)}, bf16[192,8,128]{2,1,0:T(8,128)(2,1)}, bf16[192,8,128]{2,1,0:T(8,128)(2,1)}, bf16[192,8,128]{2,1,0:T(8,128)(2,1)}) custom-call(s32[1]{0:T(128)} %bitcast.refs_0_, bf16[4,192,128]{2,1,0:T(8,128)(2,1)S(1)} %get-tuple-element.28.refs_1_, bf16[4,192,128]{2,1,0:T(8,128)(2,1)S(1)} %collective-permute-done.7.refs_2_, ...), custom_call_target="tpu_custom_call" | custom-call | tf_op jit(solution)/shard_map/pallas_call | solution.py:231
  (11 shorter events, 0.6 us)
Async XLA Ops:
  0.6 21.0 %copy-start = (s32[1536]{0:T(1024)S(1)}, s32[1536]{0:T(1024)}, u32[]{:S(2)}) copy-start(s32[1536]{0:T(1024)} %param.9) | copy-start | bytes 18436
  2.3 11.9 %collective-permute-start = (bf16[4,192,128]{2,1,0:T(8,128)(2,1)S(1)}, bf16[4,192,128]{2,1,0:T(8,128)(2,1)S(1)}, u32[]{:S(2)}, u32[]{:S(2)}) collective-permute-start(bf16[4,192,128]{2,1,0:T(8,128)(2,1)S(1)} %get-tuple-element.21), channel_id=1, source_target_pairs={{0,14},{2,12},{4,10},{6,8},{8,6},{10,4},{12,2},{14,0},{1,15},{3,13... | collective-permute-start | bytes 589832 | tf_op jit(solution)/shard_map/ppermute | solution.py:255
  8.4 10.8 %collective-permute-start.1 = (bf16[4,192,128]{2,1,0:T(8,128)(2,1)S(1)}, bf16[4,192,128]{2,1,0:T(8,128)(2,1)S(1)}, u32[]{:S(2)}, u32[]{:S(2)}) collective-permute-start(bf16[4,192,128]{2,1,0:T(8,128)(2,1)S(1)} %get-tuple-element.22), channel_id=1, source_target_pairs={{0,6},{2,4},{4,2},{6,0},{8,14},{10,12},{12,10},{14,8},{1,7},{3,5},... | collective-permute-start | bytes 589832 | tf_op jit(solution)/shard_map/ppermute | solution.py:255
  8.4 15.0 %collective-permute-start.2 = (bf16[4,192,128]{2,1,0:T(8,128)(2,1)S(1)}, bf16[4,192,128]{2,1,0:T(8,128)(2,1)S(1)}, u32[]{:S(2)}, u32[]{:S(2)}) collective-permute-start(bf16[4,192,128]{2,1,0:T(8,128)(2,1)S(1)} %get-tuple-element.23), channel_id=1, source_target_pairs={{0,12},{2,14},{4,8},{6,10},{8,4},{10,6},{12,0},{14,2},{1,13},{3,15... | collective-permute-start | bytes 589832 | tf_op jit(solution)/shard_map/ppermute | solution.py:255
  9.2 18.4 %collective-permute-start.3 = (bf16[4,192,128]{2,1,0:T(8,128)(2,1)S(1)}, bf16[4,192,128]{2,1,0:T(8,128)(2,1)S(1)}, u32[]{:S(2)}, u32[]{:S(2)}) collective-permute-start(bf16[4,192,128]{2,1,0:T(8,128)(2,1)S(1)} %get-tuple-element.24), channel_id=1, source_target_pairs={{0,4},{2,6},{4,0},{6,2},{8,12},{10,14},{12,8},{14,10},{1,5},{3,7},... | collective-permute-start | bytes 589832 | tf_op jit(solution)/shard_map/ppermute | solution.py:255
  10.4 28.5 %collective-permute-start.4 = (bf16[4,192,128]{2,1,0:T(8,128)(2,1)S(1)}, bf16[4,192,128]{2,1,0:T(8,128)(2,1)S(1)}, u32[]{:S(2)}, u32[]{:S(2)}) collective-permute-start(bf16[4,192,128]{2,1,0:T(8,128)(2,1)S(1)} %get-tuple-element.25), channel_id=1, source_target_pairs={{0,10},{2,8},{4,14},{6,12},{8,2},{10,0},{12,6},{14,4},{1,11},{3,9}... | collective-permute-start | bytes 589832 | tf_op jit(solution)/shard_map/ppermute | solution.py:255
  14.2 24.7 %collective-permute-start.5 = (bf16[4,192,128]{2,1,0:T(8,128)(2,1)S(1)}, bf16[4,192,128]{2,1,0:T(8,128)(2,1)S(1)}, u32[]{:S(2)}, u32[]{:S(2)}) collective-permute-start(bf16[4,192,128]{2,1,0:T(8,128)(2,1)S(1)} %get-tuple-element.26), channel_id=1, source_target_pairs={{0,2},{2,0},{4,6},{6,4},{8,10},{10,8},{12,14},{14,12},{1,3},{3,1},... | collective-permute-start | bytes 589832 | tf_op jit(solution)/shard_map/ppermute | solution.py:255
  19.2 22.9 %collective-permute-start.6 = (bf16[4,192,128]{2,1,0:T(8,128)(2,1)S(1)}, bf16[4,192,128]{2,1,0:T(8,128)(2,1)S(1)}, u32[]{:S(2)}, u32[]{:S(2)}) collective-permute-start(bf16[4,192,128]{2,1,0:T(8,128)(2,1)S(1)} %get-tuple-element.27), channel_id=1, source_target_pairs={{0,8},{2,10},{4,12},{6,14},{8,0},{10,2},{12,4},{14,6},{1,9},{3,11}... | collective-permute-start | bytes 589832 | tf_op jit(solution)/shard_map/ppermute | solution.py:255
  47.5 9.8 %collective-permute-start.7 = (bf16[4,192,128]{2,1,0:T(8,128)(2,1)S(1)}, bf16[4,192,128]{2,1,0:T(8,128)(2,1)S(1)}, u32[]{:S(2)}, u32[]{:S(2)}) collective-permute-start(bf16[4,192,128]{2,1,0:T(8,128)(2,1)S(1)} %get-tuple-element.29), channel_id=1, source_target_pairs={{0,12},{2,14},{4,8},{6,10},{8,4},{10,6},{12,0},{14,2},{1,13},{3,15... | collective-permute-start | bytes 589832 | tf_op jit(solution)/shard_map/ppermute | solution.py:255
  49.9 20.3 %collective-permute-start.8 = (bf16[4,192,128]{2,1,0:T(8,128)(2,1)S(1)}, bf16[4,192,128]{2,1,0:T(8,128)(2,1)S(1)}, u32[]{:S(2)}, u32[]{:S(2)}) collective-permute-start(bf16[4,192,128]{2,1,0:T(8,128)(2,1)S(1)} %get-tuple-element.30), channel_id=1, source_target_pairs={{0,10},{2,8},{4,14},{6,12},{8,2},{10,0},{12,6},{14,4},{1,11},{3,9}... | collective-permute-start | bytes 589832 | tf_op jit(solution)/shard_map/ppermute | solution.py:255
  49.9 26.5 %collective-permute-start.9 = (bf16[4,192,128]{2,1,0:T(8,128)(2,1)S(1)}, bf16[4,192,128]{2,1,0:T(8,128)(2,1)S(1)}, u32[]{:S(2)}, u32[]{:S(2)}) collective-permute-start(bf16[4,192,128]{2,1,0:T(8,128)(2,1)S(1)} %get-tuple-element.31), channel_id=1, source_target_pairs={{0,8},{2,10},{4,12},{6,14},{8,0},{10,2},{12,4},{14,6},{1,9},{3,11}... | collective-permute-start | bytes 589832 | tf_op jit(solution)/shard_map/ppermute | solution.py:255
  52.8 23.7 %collective-permute-start.10 = (bf16[4,192,128]{2,1,0:T(8,128)(2,1)S(1)}, bf16[4,192,128]{2,1,0:T(8,128)(2,1)S(1)}, u32[]{:S(2)}, u32[]{:S(2)}) collective-permute-start(bf16[4,192,128]{2,1,0:T(8,128)(2,1)S(1)} %get-tuple-element.32), channel_id=1, source_target_pairs={{0,6},{2,4},{4,2},{6,0},{8,14},{10,12},{12,10},{14,8},{1,7},{3,5},... | collective-permute-start | bytes 589832 | tf_op jit(solution)/shard_map/ppermute | solution.py:255
  52.9 23.6 %collective-permute-start.11 = (bf16[4,192,128]{2,1,0:T(8,128)(2,1)S(1)}, bf16[4,192,128]{2,1,0:T(8,128)(2,1)S(1)}, u32[]{:S(2)}, u32[]{:S(2)}) collective-permute-start(bf16[4,192,128]{2,1,0:T(8,128)(2,1)S(1)} %get-tuple-element.33), channel_id=1, source_target_pairs={{0,4},{2,6},{4,0},{6,2},{8,12},{10,14},{12,8},{14,10},{1,5},{3,7},... | collective-permute-start | bytes 589832 | tf_op jit(solution)/shard_map/ppermute | solution.py:255
  57.3 19.2 %collective-permute-start.12 = (bf16[4,192,128]{2,1,0:T(8,128)(2,1)S(1)}, bf16[4,192,128]{2,1,0:T(8,128)(2,1)S(1)}, u32[]{:S(2)}, u32[]{:S(2)}) collective-permute-start(bf16[4,192,128]{2,1,0:T(8,128)(2,1)S(1)} %get-tuple-element.34), channel_id=1, source_target_pairs={{0,2},{2,0},{4,6},{6,4},{8,10},{10,8},{12,14},{14,12},{1,3},{3,1},... | collective-permute-start | bytes 589832 | tf_op jit(solution)/shard_map/ppermute | solution.py:255
  70.2 8.5 %collective-permute-start.13 = (bf16[4,192,128]{2,1,0:T(8,128)(2,1)S(1)}, bf16[4,192,128]{2,1,0:T(8,128)(2,1)S(1)}, u32[]{:S(2)}, u32[]{:S(2)}) collective-permute-start(bf16[4,192,128]{2,1,0:T(8,128)(2,1)S(1)} %get-tuple-element.35), channel_id=1, source_target_pairs={{0,14},{2,12},{4,10},{6,8},{8,6},{10,4},{12,2},{14,0},{1,15},{3,13... | collective-permute-start | bytes 589832 | tf_op jit(solution)/shard_map/ppermute | solution.py:255

commit v5 on v4

--- a/solution.py
+++ b/solution.py
@@ -14,7 +14,8 @@
 
 def partner_orders(count):
     far, near = list(range(count - 1, count // 2 - 1, -1)), list(range(count // 2 - 1, 0, -1))
-    turns = [d for pair in zip(far, near) for d in pair] + far[-1:]
+    first = far[count // 4 :] + far[: count // 4]
+    turns = [d for pair in zip(first, near) for d in pair] + first[-1:]
     back = near + far
     return (0, *turns), (0, *back[count // 2 :], *back[: count // 2])
 

time: 80.9 us -> 79.6 us (0.984)
  waiting for transfers between devices: 43.8 us -> 34.9 us
  starting transfers between devices: 26 us -> 33.1 us
    ppermute x14, waiting for transfers between devices: 43.8 us -> 34.9 us  [exchange(): got[d] = lax.ppermute(blocks[d], 'ctx', [(s, s ^ d) for s in range(count)])]
    ppermute x14, starting transfers between devices: 26 us -> 33.1 us  [exchange(): got[d] = lax.ppermute(blocks[d], 'ctx', [(s, s ^ d) for s in range(count)])]
  transfers between devices with their start and end apart: 14 -> 14, of which waited for: 10 -> 8; matrix products, arithmetic and copies ran while one was open for 1% -> 1% of each run, Pallas kernels for 0% -> 0%
where the time goes in v5:
time: 79.6 us; the launch traced here: 78.2 us
  waiting for transfers between devices  34.9 us (44%)
  starting transfers between devices  33.1 us (42%)
  Pallas kernels  8.54 us (11%)
  other arithmetic  0.99 us (1%)
    ppermute x14, waiting for transfers between devices, exchange(): got[d] = lax.ppermute(blocks[d], 'ctx', [(s, s ^ d) for s in range(count)])  34.9 us
    ppermute x14, starting transfers between devices, exchange(): got[d] = lax.ppermute(blocks[d], 'ctx', [(s, s ^ d) for s in range(count)])  33.1 us
    pallas_call x1, Pallas kernels, attend(): pl.pallas_call(functools.partial(attention_kernel, order, tile_most), out...  5.42 us
    pallas_call x1, Pallas kernels, pack(): pl.pallas_call(functools.partial(pack_kernel, order, count // head_count)...  1.68 us
  transfers between devices with their start and end apart: 14, of which 8 were waited for; matrix products, arithmetic and copies ran while one was open for 1% of the time, Pallas kernels for 0%

profile of v5, /device:TPU:0, one launch (start us, length us, event | category | flops | bytes accessed | tf_op | source)
XLA Modules:
  0.0 78.2 jit_solution(12137995794668026182)
XLA Ops:
  0.6 1.7 %shard_map.84 = (bf16[4,192,128]{2,1,0:T(8,128)(2,1)S(1)}, bf16[4,192,128]{2,1,0:T(8,128)(2,1)S(1)}, bf16[4,192,128]{2,1,0:T(8,128)(2,1)S(1)}, bf16[4,192,128]{2...) custom-call(s32[1]{0:T(128)} %bitcast.refs_0_, ...), custom_call_target="tpu_custom_call" | custom-call | tf_op jit(solution)/shard_map/pallas_call | solution.py:194
  2.3 5.1 %collective-permute-start = (bf16[4,192,128]{2,1,0:T(8,128)(2,1)S(1)}, bf16[4,192,128]{2,1,0:T(8,128)(2,1)S(1)}, u32[]{:S(2)}, u32[]{:S(2)}) collective-permute-start(bf16[4,192,128]{2,1,0:T(8,128)(2,1)S(1)} %get-tuple-element.21), channel_id=1, source_target_pairs={{0,10},{2,8},{4,14},{6,12},{8,2},{10,0},{12,6},{14,4},{1,11},{3,9}... | collective-permute-start | bytes 589832 | tf_op jit(solution)/shard_map/ppermute | solution.py:256
  7.4 1.5 %collective-permute-start.1 = (bf16[4,192,128]{2,1,0:T(8,128)(2,1)S(1)}, bf16[4,192,128]{2,1,0:T(8,128)(2,1)S(1)}, u32[]{:S(2)}, u32[]{:S(2)}) collective-permute-start(bf16[4,192,128]{2,1,0:T(8,128)(2,1)S(1)} %get-tuple-element.22), channel_id=1, source_target_pairs={{0,6},{2,4},{4,2},{6,0},{8,14},{10,12},{12,10},{14,8},{1,7},{3,5},... | collective-permute-start | bytes 589832 | tf_op jit(solution)/shard_map/ppermute | solution.py:256
  8.9 0.3 collective-permute-start.2
  9.2 0.3 collective-permute-start.3
  9.5 4.8 %collective-permute-start.4 = (bf16[4,192,128]{2,1,0:T(8,128)(2,1)S(1)}, bf16[4,192,128]{2,1,0:T(8,128)(2,1)S(1)}, u32[]{:S(2)}, u32[]{:S(2)}) collective-permute-start(bf16[4,192,128]{2,1,0:T(8,128)(2,1)S(1)} %get-tuple-element.25), channel_id=1, source_target_pairs={{0,14},{2,12},{4,10},{6,8},{8,6},{10,4},{12,2},{14,0},{1,15},{3,13... | collective-permute-start | bytes 589832 | tf_op jit(solution)/shard_map/ppermute | solution.py:256
  14.3 3.2 %collective-permute-done.refs_3_ = bf16[4,192,128]{2,1,0:T(8,128)(2,1)S(1)} collective-permute-done((bf16[4,192,128]{2,1,0:T(8,128)(2,1)S(1)}, bf16[4,192,128]{2,1,0:T(8,128)(2,1)S(1)}, u32[]{:S(2)}, u32[]{:S(2)}) %collective-permute-start) | collective-permute-done | bytes 196640 | tf_op jit(solution)/shard_map/ppermute | solution.py:256
  17.4 1.9 %collective-permute-start.5 = (bf16[4,192,128]{2,1,0:T(8,128)(2,1)S(1)}, bf16[4,192,128]{2,1,0:T(8,128)(2,1)S(1)}, u32[]{:S(2)}, u32[]{:S(2)}) collective-permute-start(bf16[4,192,128]{2,1,0:T(8,128)(2,1)S(1)} %get-tuple-element.26), channel_id=1, source_target_pairs={{0,2},{2,0},{4,6},{6,4},{8,10},{10,8},{12,14},{14,12},{1,3},{3,1},... | collective-permute-start | bytes 589832 | tf_op jit(solution)/shard_map/ppermute | solution.py:256
  19.4 2.0 %collective-permute-done.1.refs_4_ = bf16[4,192,128]{2,1,0:T(8,128)(2,1)S(1)} collective-permute-done((bf16[4,192,128]{2,1,0:T(8,128)(2,1)S(1)}, bf16[4,192,128]{2,1,0:T(8,128)(2,1)S(1)}, u32[]{:S(2)}, u32[]{:S(2)}) %collective-permute-start.1) | collective-permute-done | bytes 196640 | tf_op jit(solution)/shard_map/ppermute | solution.py:256
  21.3 1.5 %collective-permute-start.6 = (bf16[4,192,128]{2,1,0:T(8,128)(2,1)S(1)}, bf16[4,192,128]{2,1,0:T(8,128)(2,1)S(1)}, u32[]{:S(2)}, u32[]{:S(2)}) collective-permute-start(bf16[4,192,128]{2,1,0:T(8,128)(2,1)S(1)} %get-tuple-element.27), channel_id=1, source_target_pairs={{0,12},{2,14},{4,8},{6,10},{8,4},{10,6},{12,0},{14,2},{1,13},{3,15... | collective-permute-start | bytes 589832 | tf_op jit(solution)/shard_map/ppermute | solution.py:256
  22.8 1.0 %convert_reduce_fusion = s32[1536]{0:T(1024)S(1)} fusion(s32[1536]{0:T(1024)S(1)} %copy-done), kind=kLoop, calls=%fused_computation | loop fusion | flops 7076352 | bytes 12288 | tf_op jit(solution)/shard_map/reduce_sum | solution.py:149
  23.8 2.5 %collective-permute-done.2.refs_5_ = bf16[4,192,128]{2,1,0:T(8,128)(2,1)S(1)} collective-permute-done((bf16[4,192,128]{2,1,0:T(8,128)(2,1)S(1)}, bf16[4,192,128]{2,1,0:T(8,128)(2,1)S(1)}, u32[]{:S(2)}, u32[]{:S(2)}) %collective-permute-start.2) | collective-permute-done | bytes 196640 | tf_op jit(solution)/shard_map/ppermute | solution.py:256
  26.3 6.1 %collective-permute-done.4.refs_7_ = bf16[4,192,128]{2,1,0:T(8,128)(2,1)S(1)} collective-permute-done((bf16[4,192,128]{2,1,0:T(8,128)(2,1)S(1)}, bf16[4,192,128]{2,1,0:T(8,128)(2,1)S(1)}, u32[]{:S(2)}, u32[]{:S(2)}) %collective-permute-start.4) | collective-permute-done | bytes 196640 | tf_op jit(solution)/shard_map/ppermute | solution.py:256
  32.4 3.2 %collective-permute-done.6.refs_9_ = bf16[4,192,128]{2,1,0:T(8,128)(2,1)S(1)} collective-permute-done((bf16[4,192,128]{2,1,0:T(8,128)(2,1)S(1)}, bf16[4,192,128]{2,1,0:T(8,128)(2,1)S(1)}, u32[]{:S(2)}, u32[]{:S(2)}) %collective-permute-start.6) | collective-permute-done | bytes 196640 | tf_op jit(solution)/shard_map/ppermute | solution.py:256
  35.6 5.4 %shard_map.85 = (bf16[4,192,128]{2,1,0:T(8,128)(2,1)S(1)}, bf16[4,192,128]{2,1,0:T(8,128)(2,1)S(1)}, bf16[4,192,128]{2,1,0:T(8,128)(2,1)S(1)}, bf16[4,192,128]{2...) custom-call(s32[1]{0:T(128)} %bitcast.refs_0_, ...), custom_call_target="tpu_custom_call" | custom-call | tf_op jit(solution)/shard_map/pallas_call | solution.py:152
  41.1 1.5 %collective-permute-start.7 = (bf16[4,192,128]{2,1,0:T(8,128)(2,1)S(1)}, bf16[4,192,128]{2,1,0:T(8,128)(2,1)S(1)}, u32[]{:S(2)}, u32[]{:S(2)}) collective-permute-start(bf16[4,192,128]{2,1,0:T(8,128)(2,1)S(1)} %get-tuple-element.29), channel_id=1, source_target_pairs={{0,12},{2,14},{4,8},{6,10},{8,4},{10,6},{12,0},{14,2},{1,13},{3,15... | collective-permute-start | bytes 589832 | tf_op jit(solution)/shard_map/ppermute | solution.py:256
  42.6 7.5 %collective-permute-start.8 = (bf16[4,192,128]{2,1,0:T(8,128)(2,1)S(1)}, bf16[4,192,128]{2,1,0:T(8,128)(2,1)S(1)}, u32[]{:S(2)}, u32[]{:S(2)}) collective-permute-start(bf16[4,192,128]{2,1,0:T(8,128)(2,1)S(1)} %get-tuple-element.30), channel_id=1, source_target_pairs={{0,10},{2,8},{4,14},{6,12},{8,2},{10,0},{12,6},{14,4},{1,11},{3,9}... | collective-permute-start | bytes 589832 | tf_op jit(solution)/shard_map/ppermute | solution.py:256
  50.1 4.2 %collective-permute-start.10 = (bf16[4,192,128]{2,1,0:T(8,128)(2,1)S(1)}, bf16[4,192,128]{2,1,0:T(8,128)(2,1)S(1)}, u32[]{:S(2)}, u32[]{:S(2)}) collective-permute-start(bf16[4,192,128]{2,1,0:T(8,128)(2,1)S(1)} %get-tuple-element.32), channel_id=1, source_target_pairs={{0,6},{2,4},{4,2},{6,0},{8,14},{10,12},{12,10},{14,8},{1,7},{3,5},... | collective-permute-start | bytes 589832 | tf_op jit(solution)/shard_map/ppermute | solution.py:256
  54.4 0.6 collective-permute-start.12
  54.9 13.4 %collective-permute-done.8.refs_3_ = bf16[4,192,128]{2,1,0:T(8,128)(2,1)S(1)} collective-permute-done((bf16[4,192,128]{2,1,0:T(8,128)(2,1)S(1)}, bf16[4,192,128]{2,1,0:T(8,128)(2,1)S(1)}, u32[]{:S(2)}, u32[]{:S(2)}) %collective-permute-start.8) | collective-permute-done | bytes 196640 | tf_op jit(solution)/shard_map/ppermute | solution.py:256
  68.3 3.9 %collective-permute-start.13 = (bf16[4,192,128]{2,1,0:T(8,128)(2,1)S(1)}, bf16[4,192,128]{2,1,0:T(8,128)(2,1)S(1)}, u32[]{:S(2)}, u32[]{:S(2)}) collective-permute-start(bf16[4,192,128]{2,1,0:T(8,128)(2,1)S(1)} %get-tuple-element.35), channel_id=1, source_target_pairs={{0,14},{2,12},{4,10},{6,8},{8,6},{10,4},{12,2},{14,0},{1,15},{3,13... | collective-permute-start | bytes 589832 | tf_op jit(solution)/shard_map/ppermute | solution.py:256
  72.2 0.4 collective-permute-done.9.refs_4_
  72.6 4.2 %collective-permute-done.13.refs_8_ = bf16[4,192,128]{2,1,0:T(8,128)(2,1)S(1)} collective-permute-done((bf16[4,192,128]{2,1,0:T(8,128)(2,1)S(1)}, bf16[4,192,128]{2,1,0:T(8,128)(2,1)S(1)}, u32[]{:S(2)}, u32[]{:S(2)}) %collective-permute-start.13) | collective-permute-done | bytes 196640 | tf_op jit(solution)/shard_map/ppermute | solution.py:256
  76.7 1.4 %shard_map.86 = (bf16[192,8,128]{2,1,0:T(8,128)(2,1)}, bf16[192,8,128]{2,1,0:T(8,128)(2,1)}, bf16[192,8,128]{2,1,0:T(8,128)(2,1)}, bf16[192,8,128]{2,1,0:T(8,128)(2,1)}) custom-call(s32[1]{0:T(128)} %bitcast.refs_0_, bf16[4,192,128]{2,1,0:T(8,128)(2,1)S(1)} %get-tuple-element.28.refs_1_, bf16[4,192,128]{2,1,0:T(8,128)(2,1)S(1)} %collective-permute-done.7.refs_2_, ...), custom_call_target="tpu_custom_call" | custom-call | tf_op jit(solution)/shard_map/pallas_call | solution.py:232
  (11 shorter events, 0.1 us)
Async XLA Ops:
  0.6 22.2 %copy-start = (s32[1536]{0:T(1024)S(1)}, s32[1536]{0:T(1024)}, u32[]{:S(2)}) copy-start(s32[1536]{0:T(1024)} %param.9) | copy-start | bytes 18436
  2.3 15.1 %collective-permute-start = (bf16[4,192,128]{2,1,0:T(8,128)(2,1)S(1)}, bf16[4,192,128]{2,1,0:T(8,128)(2,1)S(1)}, u32[]{:S(2)}, u32[]{:S(2)}) collective-permute-start(bf16[4,192,128]{2,1,0:T(8,128)(2,1)S(1)} %get-tuple-element.21), channel_id=1, source_target_pairs={{0,10},{2,8},{4,14},{6,12},{8,2},{10,0},{12,6},{14,4},{1,11},{3,9}... | collective-permute-start | bytes 589832 | tf_op jit(solution)/shard_map/ppermute | solution.py:256
  7.4 13.9 %collective-permute-start.1 = (bf16[4,192,128]{2,1,0:T(8,128)(2,1)S(1)}, bf16[4,192,128]{2,1,0:T(8,128)(2,1)S(1)}, u32[]{:S(2)}, u32[]{:S(2)}) collective-permute-start(bf16[4,192,128]{2,1,0:T(8,128)(2,1)S(1)} %get-tuple-element.22), channel_id=1, source_target_pairs={{0,6},{2,4},{4,2},{6,0},{8,14},{10,12},{12,10},{14,8},{1,7},{3,5},... | collective-permute-start | bytes 589832 | tf_op jit(solution)/shard_map/ppermute | solution.py:256
  8.9 17.4 %collective-permute-start.2 = (bf16[4,192,128]{2,1,0:T(8,128)(2,1)S(1)}, bf16[4,192,128]{2,1,0:T(8,128)(2,1)S(1)}, u32[]{:S(2)}, u32[]{:S(2)}) collective-permute-start(bf16[4,192,128]{2,1,0:T(8,128)(2,1)S(1)} %get-tuple-element.23), channel_id=1, source_target_pairs={{0,8},{2,10},{4,12},{6,14},{8,0},{10,2},{12,4},{14,6},{1,9},{3,11}... | collective-permute-start | bytes 589832 | tf_op jit(solution)/shard_map/ppermute | solution.py:256
  9.2 17.1 %collective-permute-start.3 = (bf16[4,192,128]{2,1,0:T(8,128)(2,1)S(1)}, bf16[4,192,128]{2,1,0:T(8,128)(2,1)S(1)}, u32[]{:S(2)}, u32[]{:S(2)}) collective-permute-start(bf16[4,192,128]{2,1,0:T(8,128)(2,1)S(1)} %get-tuple-element.24), channel_id=1, source_target_pairs={{0,4},{2,6},{4,0},{6,2},{8,12},{10,14},{12,8},{14,10},{1,5},{3,7},... | collective-permute-start | bytes 589832 | tf_op jit(solution)/shard_map/ppermute | solution.py:256
  9.5 22.9 %collective-permute-start.4 = (bf16[4,192,128]{2,1,0:T(8,128)(2,1)S(1)}, bf16[4,192,128]{2,1,0:T(8,128)(2,1)S(1)}, u32[]{:S(2)}, u32[]{:S(2)}) collective-permute-start(bf16[4,192,128]{2,1,0:T(8,128)(2,1)S(1)} %get-tuple-element.25), channel_id=1, source_target_pairs={{0,14},{2,12},{4,10},{6,8},{8,6},{10,4},{12,2},{14,0},{1,15},{3,13... | collective-permute-start | bytes 589832 | tf_op jit(solution)/shard_map/ppermute | solution.py:256
  17.4 15.0 %collective-permute-start.5 = (bf16[4,192,128]{2,1,0:T(8,128)(2,1)S(1)}, bf16[4,192,128]{2,1,0:T(8,128)(2,1)S(1)}, u32[]{:S(2)}, u32[]{:S(2)}) collective-permute-start(bf16[4,192,128]{2,1,0:T(8,128)(2,1)S(1)} %get-tuple-element.26), channel_id=1, source_target_pairs={{0,2},{2,0},{4,6},{6,4},{8,10},{10,8},{12,14},{14,12},{1,3},{3,1},... | collective-permute-start | bytes 589832 | tf_op jit(solution)/shard_map/ppermute | solution.py:256
  21.3 14.3 %collective-permute-start.6 = (bf16[4,192,128]{2,1,0:T(8,128)(2,1)S(1)}, bf16[4,192,128]{2,1,0:T(8,128)(2,1)S(1)}, u32[]{:S(2)}, u32[]{:S(2)}) collective-permute-start(bf16[4,192,128]{2,1,0:T(8,128)(2,1)S(1)} %get-tuple-element.27), channel_id=1, source_target_pairs={{0,12},{2,14},{4,8},{6,10},{8,4},{10,6},{12,0},{14,2},{1,13},{3,15... | collective-permute-start | bytes 589832 | tf_op jit(solution)/shard_map/ppermute | solution.py:256
  41.1 13.3 %collective-permute-start.7 = (bf16[4,192,128]{2,1,0:T(8,128)(2,1)S(1)}, bf16[4,192,128]{2,1,0:T(8,128)(2,1)S(1)}, u32[]{:S(2)}, u32[]{:S(2)}) collective-permute-start(bf16[4,192,128]{2,1,0:T(8,128)(2,1)S(1)} %get-tuple-element.29), channel_id=1, source_target_pairs={{0,12},{2,14},{4,8},{6,10},{8,4},{10,6},{12,0},{14,2},{1,13},{3,15... | collective-permute-start | bytes 589832 | tf_op jit(solution)/shard_map/ppermute | solution.py:256
  42.6 25.7 %collective-permute-start.8 = (bf16[4,192,128]{2,1,0:T(8,128)(2,1)S(1)}, bf16[4,192,128]{2,1,0:T(8,128)(2,1)S(1)}, u32[]{:S(2)}, u32[]{:S(2)}) collective-permute-start(bf16[4,192,128]{2,1,0:T(8,128)(2,1)S(1)} %get-tuple-element.30), channel_id=1, source_target_pairs={{0,10},{2,8},{4,14},{6,12},{8,2},{10,0},{12,6},{14,4},{1,11},{3,9}... | collective-permute-start | bytes 589832 | tf_op jit(solution)/shard_map/ppermute | solution.py:256
  50.0 22.5 %collective-permute-start.9 = (bf16[4,192,128]{2,1,0:T(8,128)(2,1)S(1)}, bf16[4,192,128]{2,1,0:T(8,128)(2,1)S(1)}, u32[]{:S(2)}, u32[]{:S(2)}) collective-permute-start(bf16[4,192,128]{2,1,0:T(8,128)(2,1)S(1)} %get-tuple-element.31), channel_id=1, source_target_pairs={{0,8},{2,10},{4,12},{6,14},{8,0},{10,2},{12,4},{14,6},{1,9},{3,11}... | collective-permute-start | bytes 589832 | tf_op jit(solution)/shard_map/ppermute | solution.py:256
  50.1 22.4 %collective-permute-start.10 = (bf16[4,192,128]{2,1,0:T(8,128)(2,1)S(1)}, bf16[4,192,128]{2,1,0:T(8,128)(2,1)S(1)}, u32[]{:S(2)}, u32[]{:S(2)}) collective-permute-start(bf16[4,192,128]{2,1,0:T(8,128)(2,1)S(1)} %get-tuple-element.32), channel_id=1, source_target_pairs={{0,6},{2,4},{4,2},{6,0},{8,14},{10,12},{12,10},{14,8},{1,7},{3,5},... | collective-permute-start | bytes 589832 | tf_op jit(solution)/shard_map/ppermute | solution.py:256
  54.4 18.2 %collective-permute-start.11 = (bf16[4,192,128]{2,1,0:T(8,128)(2,1)S(1)}, bf16[4,192,128]{2,1,0:T(8,128)(2,1)S(1)}, u32[]{:S(2)}, u32[]{:S(2)}) collective-permute-start(bf16[4,192,128]{2,1,0:T(8,128)(2,1)S(1)} %get-tuple-element.33), channel_id=1, source_target_pairs={{0,4},{2,6},{4,0},{6,2},{8,12},{10,14},{12,8},{14,10},{1,5},{3,7},... | collective-permute-start | bytes 589832 | tf_op jit(solution)/shard_map/ppermute | solution.py:256
  54.4 18.2 %collective-permute-start.12 = (bf16[4,192,128]{2,1,0:T(8,128)(2,1)S(1)}, bf16[4,192,128]{2,1,0:T(8,128)(2,1)S(1)}, u32[]{:S(2)}, u32[]{:S(2)}) collective-permute-start(bf16[4,192,128]{2,1,0:T(8,128)(2,1)S(1)} %get-tuple-element.34), channel_id=1, source_target_pairs={{0,2},{2,0},{4,6},{6,4},{8,10},{10,8},{12,14},{14,12},{1,3},{3,1},... | collective-permute-start | bytes 589832 | tf_op jit(solution)/shard_map/ppermute | solution.py:256
  68.3 8.4 %collective-permute-start.13 = (bf16[4,192,128]{2,1,0:T(8,128)(2,1)S(1)}, bf16[4,192,128]{2,1,0:T(8,128)(2,1)S(1)}, u32[]{:S(2)}, u32[]{:S(2)}) collective-permute-start(bf16[4,192,128]{2,1,0:T(8,128)(2,1)S(1)} %get-tuple-element.35), channel_id=1, source_target_pairs={{0,14},{2,12},{4,10},{6,8},{8,6},{10,4},{12,2},{14,0},{1,15},{3,13... | collective-permute-start | bytes 589832 | tf_op jit(solution)/shard_map/ppermute | solution.py:256

commit v6 on v5

--- a/solution.py
+++ b/solution.py
@@ -41,6 +41,7 @@
     head_size = rows.shape[2]
     tile = TILE
     scaling = head_size ** (-0.5)
+    longest = tokens * 5 // 8
     exponent = scaling * math.log2(math.e)
 
     for n, d in enumerate(order):
@@ -67,7 +68,15 @@
         query_tb = q_blk.T
 
         def cols(i):
-            return slice(tile, wide) if i == size - 1 else slice(0, wide)
+            if i == size - 1:
+                return slice(tile, wide)
+            gap = q_at + tile - (k_at + (i + 1) * tile - 1)
+            return slice(0, tile) if gap > longest - 1 else slice(0, wide)
+
+        def join(i, old, new, f):
+            c = cols(i)
+            parts = [old[:, : c.start], f(old[:, c], new), old[:, c.stop :]]
+            return jnp.concatenate([p for p in parts if p.shape[1]], 1)
 
         best = jnp.full((1, wide), HIDDEN, jnp.float32)
         for i in range(size):
@@ -82,19 +91,17 @@
             s = jnp.where(seen, s, HIDDEN)
             scores[i * tile : (i + 1) * tile, c] = s
             top = jnp.max(s, axis=0, keepdims=True)
-            if i == size - 1:
-                best = jnp.concatenate([best[:, :tile], jnp.maximum(best[:, tile:], top)], 1)
-            else:
-                best = jnp.maximum(best, top)
+            best = join(i, best, top, jnp.maximum)
         total = jnp.zeros((1, wide), jnp.float32)
         for i in range(size):
             c = cols(i)
             e = jnp.exp2(scores[i * tile : (i + 1) * tile, c] - best[:, c])
             part = jnp.sum(e, axis=0, keepdims=True)
-            if i == size - 1:
-                total = jnp.concatenate([total[:, :tile], total[:, tile:] + part], 1)
-            else:
-                total = total + part
+            total = join(i, total, part, jnp.add)
+            if c.stop < wide:
+                blank = jnp.zeros((tile, wide - c.stop), jnp.bfloat16)
+                weights[i * tile : (i + 1) * tile, c.stop :] = blank
+                dweights[i * tile : (i + 1) * tile, c.stop :] = blank
             weights[i * tile : (i + 1) * tile, c] = e.astype(jnp.bfloat16)
         inverse = 1.0 / total
         body = size - 1

time: 79.6 us -> 79.4 us (level)
  no operation moved by 1% of the time
where the time goes in v6:
time: 79.4 us; the launch traced here: 78.1 us
  waiting for transfers between devices  34.9 us (44%)
  starting transfers between devices  33.1 us (42%)
  Pallas kernels  8.36 us (11%)
  other arithmetic  0.99 us (1%)
    ppermute x14, waiting for transfers between devices, exchange(): got[d] = lax.ppermute(blocks[d], 'ctx', [(s, s ^ d) for s in range(count)])  34.9 us
    ppermute x14, starting transfers between devices, exchange(): got[d] = lax.ppermute(blocks[d], 'ctx', [(s, s ^ d) for s in range(count)])  33.1 us
    pallas_call x1, Pallas kernels, attend(): pl.pallas_call(functools.partial(attention_kernel, order, tile_most), out...  5.24 us
    pallas_call x1, Pallas kernels, pack(): pl.pallas_call(functools.partial(pack_kernel, order, count // head_count)...  1.68 us
  transfers between devices with their start and end apart: 14, of which 8 were waited for; matrix products, arithmetic and copies ran while one was open for 1% of the time, Pallas kernels for 0%

profile of v6, /device:TPU:0, one launch (start us, length us, event | category | flops | bytes accessed | tf_op | source)
XLA Modules:
  0.0 78.1 jit_solution(15768068233963310353)
XLA Ops:
  0.6 1.7 %shard_map.84 = (bf16[4,192,128]{2,1,0:T(8,128)(2,1)S(1)}, bf16[4,192,128]{2,1,0:T(8,128)(2,1)S(1)}, bf16[4,192,128]{2,1,0:T(8,128)(2,1)S(1)}, bf16[4,192,128]{2...) custom-call(s32[1]{0:T(128)} %bitcast.refs_0_, ...), custom_call_target="tpu_custom_call" | custom-call | tf_op jit(solution)/shard_map/pallas_call | solution.py:201
  2.3 5.1 %collective-permute-start = (bf16[4,192,128]{2,1,0:T(8,128)(2,1)S(1)}, bf16[4,192,128]{2,1,0:T(8,128)(2,1)S(1)}, u32[]{:S(2)}, u32[]{:S(2)}) collective-permute-start(bf16[4,192,128]{2,1,0:T(8,128)(2,1)S(1)} %get-tuple-element.21), channel_id=1, source_target_pairs={{0,10},{2,8},{4,14},{6,12},{8,2},{10,0},{12,6},{14,4},{1,11},{3,9}... | collective-permute-start | bytes 589832 | tf_op jit(solution)/shard_map/ppermute | solution.py:263
  7.4 1.5 %collective-permute-start.1 = (bf16[4,192,128]{2,1,0:T(8,128)(2,1)S(1)}, bf16[4,192,128]{2,1,0:T(8,128)(2,1)S(1)}, u32[]{:S(2)}, u32[]{:S(2)}) collective-permute-start(bf16[4,192,128]{2,1,0:T(8,128)(2,1)S(1)} %get-tuple-element.22), channel_id=1, source_target_pairs={{0,6},{2,4},{4,2},{6,0},{8,14},{10,12},{12,10},{14,8},{1,7},{3,5},... | collective-permute-start | bytes 589832 | tf_op jit(solution)/shard_map/ppermute | solution.py:263
  8.9 0.3 collective-permute-start.2
  9.2 0.3 collective-permute-start.3
  9.5 4.8 %collective-permute-start.4 = (bf16[4,192,128]{2,1,0:T(8,128)(2,1)S(1)}, bf16[4,192,128]{2,1,0:T(8,128)(2,1)S(1)}, u32[]{:S(2)}, u32[]{:S(2)}) collective-permute-start(bf16[4,192,128]{2,1,0:T(8,128)(2,1)S(1)} %get-tuple-element.25), channel_id=1, source_target_pairs={{0,14},{2,12},{4,10},{6,8},{8,6},{10,4},{12,2},{14,0},{1,15},{3,13... | collective-permute-start | bytes 589832 | tf_op jit(solution)/shard_map/ppermute | solution.py:263
  14.3 3.2 %collective-permute-done.refs_3_ = bf16[4,192,128]{2,1,0:T(8,128)(2,1)S(1)} collective-permute-done((bf16[4,192,128]{2,1,0:T(8,128)(2,1)S(1)}, bf16[4,192,128]{2,1,0:T(8,128)(2,1)S(1)}, u32[]{:S(2)}, u32[]{:S(2)}) %collective-permute-start) | collective-permute-done | bytes 196640 | tf_op jit(solution)/shard_map/ppermute | solution.py:263
  17.4 1.9 %collective-permute-start.5 = (bf16[4,192,128]{2,1,0:T(8,128)(2,1)S(1)}, bf16[4,192,128]{2,1,0:T(8,128)(2,1)S(1)}, u32[]{:S(2)}, u32[]{:S(2)}) collective-permute-start(bf16[4,192,128]{2,1,0:T(8,128)(2,1)S(1)} %get-tuple-element.26), channel_id=1, source_target_pairs={{0,2},{2,0},{4,6},{6,4},{8,10},{10,8},{12,14},{14,12},{1,3},{3,1},... | collective-permute-start | bytes 589832 | tf_op jit(solution)/shard_map/ppermute | solution.py:263
  19.4 2.0 %collective-permute-done.1.refs_4_ = bf16[4,192,128]{2,1,0:T(8,128)(2,1)S(1)} collective-permute-done((bf16[4,192,128]{2,1,0:T(8,128)(2,1)S(1)}, bf16[4,192,128]{2,1,0:T(8,128)(2,1)S(1)}, u32[]{:S(2)}, u32[]{:S(2)}) %collective-permute-start.1) | collective-permute-done | bytes 196640 | tf_op jit(solution)/shard_map/ppermute | solution.py:263
  21.3 1.5 %collective-permute-start.6 = (bf16[4,192,128]{2,1,0:T(8,128)(2,1)S(1)}, bf16[4,192,128]{2,1,0:T(8,128)(2,1)S(1)}, u32[]{:S(2)}, u32[]{:S(2)}) collective-permute-start(bf16[4,192,128]{2,1,0:T(8,128)(2,1)S(1)} %get-tuple-element.27), channel_id=1, source_target_pairs={{0,12},{2,14},{4,8},{6,10},{8,4},{10,6},{12,0},{14,2},{1,13},{3,15... | collective-permute-start | bytes 589832 | tf_op jit(solution)/shard_map/ppermute | solution.py:263
  22.8 1.0 %convert_reduce_fusion = s32[1536]{0:T(1024)S(1)} fusion(s32[1536]{0:T(1024)S(1)} %copy-done), kind=kLoop, calls=%fused_computation | loop fusion | flops 7076352 | bytes 12288 | tf_op jit(solution)/shard_map/reduce_sum | solution.py:156
  23.8 2.5 %collective-permute-done.2.refs_5_ = bf16[4,192,128]{2,1,0:T(8,128)(2,1)S(1)} collective-permute-done((bf16[4,192,128]{2,1,0:T(8,128)(2,1)S(1)}, bf16[4,192,128]{2,1,0:T(8,128)(2,1)S(1)}, u32[]{:S(2)}, u32[]{:S(2)}) %collective-permute-start.2) | collective-permute-done | bytes 196640 | tf_op jit(solution)/shard_map/ppermute | solution.py:263
  26.3 6.1 %collective-permute-done.4.refs_7_ = bf16[4,192,128]{2,1,0:T(8,128)(2,1)S(1)} collective-permute-done((bf16[4,192,128]{2,1,0:T(8,128)(2,1)S(1)}, bf16[4,192,128]{2,1,0:T(8,128)(2,1)S(1)}, u32[]{:S(2)}, u32[]{:S(2)}) %collective-permute-start.4) | collective-permute-done | bytes 196640 | tf_op jit(solution)/shard_map/ppermute | solution.py:263
  32.4 3.2 %collective-permute-done.6.refs_9_ = bf16[4,192,128]{2,1,0:T(8,128)(2,1)S(1)} collective-permute-done((bf16[4,192,128]{2,1,0:T(8,128)(2,1)S(1)}, bf16[4,192,128]{2,1,0:T(8,128)(2,1)S(1)}, u32[]{:S(2)}, u32[]{:S(2)}) %collective-permute-start.6) | collective-permute-done | bytes 196640 | tf_op jit(solution)/shard_map/ppermute | solution.py:263
  35.6 5.2 %shard_map.85 = (bf16[4,192,128]{2,1,0:T(8,128)(2,1)S(1)}, bf16[4,192,128]{2,1,0:T(8,128)(2,1)S(1)}, bf16[4,192,128]{2,1,0:T(8,128)(2,1)S(1)}, bf16[4,192,128]{2...) custom-call(s32[1]{0:T(128)} %bitcast.refs_0_, ...), custom_call_target="tpu_custom_call" | custom-call | tf_op jit(solution)/shard_map/pallas_call | solution.py:159
  40.9 1.5 %collective-permute-start.7 = (bf16[4,192,128]{2,1,0:T(8,128)(2,1)S(1)}, bf16[4,192,128]{2,1,0:T(8,128)(2,1)S(1)}, u32[]{:S(2)}, u32[]{:S(2)}) collective-permute-start(bf16[4,192,128]{2,1,0:T(8,128)(2,1)S(1)} %get-tuple-element.29), channel_id=1, source_target_pairs={{0,12},{2,14},{4,8},{6,10},{8,4},{10,6},{12,0},{14,2},{1,13},{3,15... | collective-permute-start | bytes 589832 | tf_op jit(solution)/shard_map/ppermute | solution.py:263
  42.4 7.4 %collective-permute-start.8 = (bf16[4,192,128]{2,1,0:T(8,128)(2,1)S(1)}, bf16[4,192,128]{2,1,0:T(8,128)(2,1)S(1)}, u32[]{:S(2)}, u32[]{:S(2)}) collective-permute-start(bf16[4,192,128]{2,1,0:T(8,128)(2,1)S(1)} %get-tuple-element.30), channel_id=1, source_target_pairs={{0,10},{2,8},{4,14},{6,12},{8,2},{10,0},{12,6},{14,4},{1,11},{3,9}... | collective-permute-start | bytes 589832 | tf_op jit(solution)/shard_map/ppermute | solution.py:263
  50.0 4.2 %collective-permute-start.10 = (bf16[4,192,128]{2,1,0:T(8,128)(2,1)S(1)}, bf16[4,192,128]{2,1,0:T(8,128)(2,1)S(1)}, u32[]{:S(2)}, u32[]{:S(2)}) collective-permute-start(bf16[4,192,128]{2,1,0:T(8,128)(2,1)S(1)} %get-tuple-element.32), channel_id=1, source_target_pairs={{0,6},{2,4},{4,2},{6,0},{8,14},{10,12},{12,10},{14,8},{1,7},{3,5},... | collective-permute-start | bytes 589832 | tf_op jit(solution)/shard_map/ppermute | solution.py:263
  54.2 0.6 collective-permute-start.12
  54.8 13.4 %collective-permute-done.8.refs_3_ = bf16[4,192,128]{2,1,0:T(8,128)(2,1)S(1)} collective-permute-done((bf16[4,192,128]{2,1,0:T(8,128)(2,1)S(1)}, bf16[4,192,128]{2,1,0:T(8,128)(2,1)S(1)}, u32[]{:S(2)}, u32[]{:S(2)}) %collective-permute-start.8) | collective-permute-done | bytes 196640 | tf_op jit(solution)/shard_map/ppermute | solution.py:263
  68.1 3.9 %collective-permute-start.13 = (bf16[4,192,128]{2,1,0:T(8,128)(2,1)S(1)}, bf16[4,192,128]{2,1,0:T(8,128)(2,1)S(1)}, u32[]{:S(2)}, u32[]{:S(2)}) collective-permute-start(bf16[4,192,128]{2,1,0:T(8,128)(2,1)S(1)} %get-tuple-element.35), channel_id=1, source_target_pairs={{0,14},{2,12},{4,10},{6,8},{8,6},{10,4},{12,2},{14,0},{1,15},{3,13... | collective-permute-start | bytes 589832 | tf_op jit(solution)/shard_map/ppermute | solution.py:263
  72.0 0.4 collective-permute-done.9.refs_4_
  72.4 4.2 %collective-permute-done.13.refs_8_ = bf16[4,192,128]{2,1,0:T(8,128)(2,1)S(1)} collective-permute-done((bf16[4,192,128]{2,1,0:T(8,128)(2,1)S(1)}, bf16[4,192,128]{2,1,0:T(8,128)(2,1)S(1)}, u32[]{:S(2)}, u32[]{:S(2)}) %collective-permute-start.13) | collective-permute-done | bytes 196640 | tf_op jit(solution)/shard_map/ppermute | solution.py:263
  76.6 1.4 %shard_map.86 = (bf16[192,8,128]{2,1,0:T(8,128)(2,1)}, bf16[192,8,128]{2,1,0:T(8,128)(2,1)}, bf16[192,8,128]{2,1,0:T(8,128)(2,1)}, bf16[192,8,128]{2,1,0:T(8,128)(2,1)}) custom-call(s32[1]{0:T(128)} %bitcast.refs_0_, bf16[4,192,128]{2,1,0:T(8,128)(2,1)S(1)} %get-tuple-element.28.refs_1_, bf16[4,192,128]{2,1,0:T(8,128)(2,1)S(1)} %collective-permute-done.7.refs_2_, ...), custom_call_target="tpu_custom_call" | custom-call | tf_op jit(solution)/shard_map/pallas_call | solution.py:239
  (11 shorter events, 0.1 us)
Async XLA Ops:
  0.6 22.2 %copy-start = (s32[1536]{0:T(1024)S(1)}, s32[1536]{0:T(1024)}, u32[]{:S(2)}) copy-start(s32[1536]{0:T(1024)} %param.9) | copy-start | bytes 18436
  2.3 15.1 %collective-permute-start = (bf16[4,192,128]{2,1,0:T(8,128)(2,1)S(1)}, bf16[4,192,128]{2,1,0:T(8,128)(2,1)S(1)}, u32[]{:S(2)}, u32[]{:S(2)}) collective-permute-start(bf16[4,192,128]{2,1,0:T(8,128)(2,1)S(1)} %get-tuple-element.21), channel_id=1, source_target_pairs={{0,10},{2,8},{4,14},{6,12},{8,2},{10,0},{12,6},{14,4},{1,11},{3,9}... | collective-permute-start | bytes 589832 | tf_op jit(solution)/shard_map/ppermute | solution.py:263
  7.4 13.9 %collective-permute-start.1 = (bf16[4,192,128]{2,1,0:T(8,128)(2,1)S(1)}, bf16[4,192,128]{2,1,0:T(8,128)(2,1)S(1)}, u32[]{:S(2)}, u32[]{:S(2)}) collective-permute-start(bf16[4,192,128]{2,1,0:T(8,128)(2,1)S(1)} %get-tuple-element.22), channel_id=1, source_target_pairs={{0,6},{2,4},{4,2},{6,0},{8,14},{10,12},{12,10},{14,8},{1,7},{3,5},... | collective-permute-start | bytes 589832 | tf_op jit(solution)/shard_map/ppermute | solution.py:263
  8.9 17.4 %collective-permute-start.2 = (bf16[4,192,128]{2,1,0:T(8,128)(2,1)S(1)}, bf16[4,192,128]{2,1,0:T(8,128)(2,1)S(1)}, u32[]{:S(2)}, u32[]{:S(2)}) collective-permute-start(bf16[4,192,128]{2,1,0:T(8,128)(2,1)S(1)} %get-tuple-element.23), channel_id=1, source_target_pairs={{0,8},{2,10},{4,12},{6,14},{8,0},{10,2},{12,4},{14,6},{1,9},{3,11}... | collective-permute-start | bytes 589832 | tf_op jit(solution)/shard_map/ppermute | solution.py:263
  9.2 17.1 %collective-permute-start.3 = (bf16[4,192,128]{2,1,0:T(8,128)(2,1)S(1)}, bf16[4,192,128]{2,1,0:T(8,128)(2,1)S(1)}, u32[]{:S(2)}, u32[]{:S(2)}) collective-permute-start(bf16[4,192,128]{2,1,0:T(8,128)(2,1)S(1)} %get-tuple-element.24), channel_id=1, source_target_pairs={{0,4},{2,6},{4,0},{6,2},{8,12},{10,14},{12,8},{14,10},{1,5},{3,7},... | collective-permute-start | bytes 589832 | tf_op jit(solution)/shard_map/ppermute | solution.py:263
  9.5 22.9 %collective-permute-start.4 = (bf16[4,192,128]{2,1,0:T(8,128)(2,1)S(1)}, bf16[4,192,128]{2,1,0:T(8,128)(2,1)S(1)}, u32[]{:S(2)}, u32[]{:S(2)}) collective-permute-start(bf16[4,192,128]{2,1,0:T(8,128)(2,1)S(1)} %get-tuple-element.25), channel_id=1, source_target_pairs={{0,14},{2,12},{4,10},{6,8},{8,6},{10,4},{12,2},{14,0},{1,15},{3,13... | collective-permute-start | bytes 589832 | tf_op jit(solution)/shard_map/ppermute | solution.py:263
  17.4 15.0 %collective-permute-start.5 = (bf16[4,192,128]{2,1,0:T(8,128)(2,1)S(1)}, bf16[4,192,128]{2,1,0:T(8,128)(2,1)S(1)}, u32[]{:S(2)}, u32[]{:S(2)}) collective-permute-start(bf16[4,192,128]{2,1,0:T(8,128)(2,1)S(1)} %get-tuple-element.26), channel_id=1, source_target_pairs={{0,2},{2,0},{4,6},{6,4},{8,10},{10,8},{12,14},{14,12},{1,3},{3,1},... | collective-permute-start | bytes 589832 | tf_op jit(solution)/shard_map/ppermute | solution.py:263
  21.3 14.3 %collective-permute-start.6 = (bf16[4,192,128]{2,1,0:T(8,128)(2,1)S(1)}, bf16[4,192,128]{2,1,0:T(8,128)(2,1)S(1)}, u32[]{:S(2)}, u32[]{:S(2)}) collective-permute-start(bf16[4,192,128]{2,1,0:T(8,128)(2,1)S(1)} %get-tuple-element.27), channel_id=1, source_target_pairs={{0,12},{2,14},{4,8},{6,10},{8,4},{10,6},{12,0},{14,2},{1,13},{3,15... | collective-permute-start | bytes 589832 | tf_op jit(solution)/shard_map/ppermute | solution.py:263
  40.9 13.3 %collective-permute-start.7 = (bf16[4,192,128]{2,1,0:T(8,128)(2,1)S(1)}, bf16[4,192,128]{2,1,0:T(8,128)(2,1)S(1)}, u32[]{:S(2)}, u32[]{:S(2)}) collective-permute-start(bf16[4,192,128]{2,1,0:T(8,128)(2,1)S(1)} %get-tuple-element.29), channel_id=1, source_target_pairs={{0,12},{2,14},{4,8},{6,10},{8,4},{10,6},{12,0},{14,2},{1,13},{3,15... | collective-permute-start | bytes 589832 | tf_op jit(solution)/shard_map/ppermute | solution.py:263
  42.4 25.7 %collective-permute-start.8 = (bf16[4,192,128]{2,1,0:T(8,128)(2,1)S(1)}, bf16[4,192,128]{2,1,0:T(8,128)(2,1)S(1)}, u32[]{:S(2)}, u32[]{:S(2)}) collective-permute-start(bf16[4,192,128]{2,1,0:T(8,128)(2,1)S(1)} %get-tuple-element.30), channel_id=1, source_target_pairs={{0,10},{2,8},{4,14},{6,12},{8,2},{10,0},{12,6},{14,4},{1,11},{3,9}... | collective-permute-start | bytes 589832 | tf_op jit(solution)/shard_map/ppermute | solution.py:263
  49.9 22.5 %collective-permute-start.9 = (bf16[4,192,128]{2,1,0:T(8,128)(2,1)S(1)}, bf16[4,192,128]{2,1,0:T(8,128)(2,1)S(1)}, u32[]{:S(2)}, u32[]{:S(2)}) collective-permute-start(bf16[4,192,128]{2,1,0:T(8,128)(2,1)S(1)} %get-tuple-element.31), channel_id=1, source_target_pairs={{0,8},{2,10},{4,12},{6,14},{8,0},{10,2},{12,4},{14,6},{1,9},{3,11}... | collective-permute-start | bytes 589832 | tf_op jit(solution)/shard_map/ppermute | solution.py:263
  50.0 22.4 %collective-permute-start.10 = (bf16[4,192,128]{2,1,0:T(8,128)(2,1)S(1)}, bf16[4,192,128]{2,1,0:T(8,128)(2,1)S(1)}, u32[]{:S(2)}, u32[]{:S(2)}) collective-permute-start(bf16[4,192,128]{2,1,0:T(8,128)(2,1)S(1)} %get-tuple-element.32), channel_id=1, source_target_pairs={{0,6},{2,4},{4,2},{6,0},{8,14},{10,12},{12,10},{14,8},{1,7},{3,5},... | collective-permute-start | bytes 589832 | tf_op jit(solution)/shard_map/ppermute | solution.py:263
  54.2 18.2 %collective-permute-start.11 = (bf16[4,192,128]{2,1,0:T(8,128)(2,1)S(1)}, bf16[4,192,128]{2,1,0:T(8,128)(2,1)S(1)}, u32[]{:S(2)}, u32[]{:S(2)}) collective-permute-start(bf16[4,192,128]{2,1,0:T(8,128)(2,1)S(1)} %get-tuple-element.33), channel_id=1, source_target_pairs={{0,4},{2,6},{4,0},{6,2},{8,12},{10,14},{12,8},{14,10},{1,5},{3,7},... | collective-permute-start | bytes 589832 | tf_op jit(solution)/shard_map/ppermute | solution.py:263
  54.2 18.2 %collective-permute-start.12 = (bf16[4,192,128]{2,1,0:T(8,128)(2,1)S(1)}, bf16[4,192,128]{2,1,0:T(8,128)(2,1)S(1)}, u32[]{:S(2)}, u32[]{:S(2)}) collective-permute-start(bf16[4,192,128]{2,1,0:T(8,128)(2,1)S(1)} %get-tuple-element.34), channel_id=1, source_target_pairs={{0,2},{2,0},{4,6},{6,4},{8,10},{10,8},{12,14},{14,12},{1,3},{3,1},... | collective-permute-start | bytes 589832 | tf_op jit(solution)/shard_map/ppermute | solution.py:263
  68.1 8.5 %collective-permute-start.13 = (bf16[4,192,128]{2,1,0:T(8,128)(2,1)S(1)}, bf16[4,192,128]{2,1,0:T(8,128)(2,1)S(1)}, u32[]{:S(2)}, u32[]{:S(2)}) collective-permute-start(bf16[4,192,128]{2,1,0:T(8,128)(2,1)S(1)} %get-tuple-element.35), channel_id=1, source_target_pairs={{0,14},{2,12},{4,10},{6,8},{8,6},{10,4},{12,2},{14,0},{1,15},{3,13... | collective-permute-start | bytes 589832 | tf_op jit(solution)/shard_map/ppermute | solution.py:263
